TPU v7x, 32 devices: a whole 2x2x4 slice. The times are simulated.
32 devices in a mesh: ctx: 16 (over z, y, x), ws: 2 (over core).
Axes of the slice: x: 2, y: 2, z: 4, core: 2. Of those that a mesh axis runs over, the one named last changes fastest.
Arguments:
- tokens: bfloat16 [2, 4096, 512], P('ws', 'ctx'), may hold values from -6 to 6
- segment_ids: int32 [2, 4096], P('ws', 'ctx'), may hold values from 0 to 7, never falling along the last dimension, each value on 1 to 2048 neighbouring positions
- out_grad: bfloat16 [2, 4096, 512], P('ws', 'ctx'), may hold values from -6 to 6
- ln1_gain: float32 [512], P('ws'), may hold values from 0.5 to 1.5
- ln1_bias: float32 [512], P('ws'), may hold values from -3 to 3
- glu_weight: float32 [512, 1024], P('ws'), may hold values from -0.25 to 0.25
- glu_bias: float32 [1024], P('ws'), may hold values from -3 to 3
- ln2_gain: float32 [512], P('ws'), may hold values from 0.5 to 1.5
- ln2_bias: float32 [512], P('ws'), may hold values from -3 to 3
- left_weight: float32 [512, 2048], P('ws'), may hold values from -0.25 to 0.25
- left_bias: float32 [2048], P('ws'), may hold values from -3 to 3
- conv_weight: float32 [3, 512, 256], P(None, 'ws'), may hold values from -0.15625 to 0.15625
- conv_bias: float32 [256], P('ws'), may hold values from -3 to 3
- ln3_gain: float32 [2048], P('ws'), may hold values from 0.5 to 1.5
- ln3_bias: float32 [2048], P('ws'), may hold values from -3 to 3
- depth_weight: float32 [9, 2048], P(None, 'ws'), may hold values from -2 to 2
- point_weight: float32 [2048, 256], P('ws'), may hold values from -0.125 to 0.125
- point_bias: float32 [256], P('ws'), may hold values from -3 to 3
- ln4_gain: float32 [512], P('ws'), may hold values from 0.5 to 1.5
- ln4_bias: float32 [512], P('ws'), may hold values from -3 to 3
- qkv_weight: float32 [512, 1536], P('ws'), may hold values from -0.25 to 0.25
- attn_out_weight: float32 [512, 512], P('ws'), may hold values from -0.75 to 0.75
- attn_out_bias: float32 [512], P('ws'), may hold values from -3 to 3
- ln5_gain: float32 [512], P('ws'), may hold values from 0.5 to 1.5
- ln5_bias: float32 [512], P('ws'), may hold values from -3 to 3
- expand_weight: float32 [512, 2048], P('ws'), may hold values from -0.25 to 0.25
- expand_bias: float32 [2048], P('ws'), may hold values from -3 to 3
- shrink_weight: float32 [2048, 512], P('ws'), may hold values from -0.125 to 0.125
- shrink_bias: float32 [512], P('ws'), may hold values from -3 to 3
Outputs:
- output: bfloat16 [2, 4096, 512], P('ws', 'ctx')
- input_grad: float32 [2, 4096, 512], P('ws', 'ctx')
- d_ln1_gain: float32 [512], P('ws')
- d_ln1_bias: float32 [512], P('ws')
- d_glu_weight: float32 [512, 1024], P('ws')
- d_glu_bias: float32 [1024], P('ws')
- d_ln2_gain: float32 [512], P('ws')
- d_ln2_bias: float32 [512], P('ws')
- d_left_weight: float32 [512, 2048], P('ws')
- d_left_bias: float32 [2048], P('ws')
- d_conv_weight: float32 [3, 512, 256], P(None, 'ws')
- d_conv_bias: float32 [256], P('ws')
- d_ln3_gain: float32 [2048], P('ws')
- d_ln3_bias: float32 [2048], P('ws')
- d_depth_weight: float32 [9, 2048], P(None, 'ws')
- d_point_weight: float32 [2048, 256], P('ws')
- d_point_bias: float32 [256], P('ws')
- d_ln4_gain: float32 [512], P('ws')
- d_ln4_bias: float32 [512], P('ws')
- d_qkv_weight: float32 [512, 1536], P('ws')
- d_attn_out_weight: float32 [512, 512], P('ws')
- d_attn_out_bias: float32 [512], P('ws')
- d_ln5_gain: float32 [512], P('ws')
- d_ln5_bias: float32 [512], P('ws')
- d_expand_weight: float32 [512, 2048], P('ws')
- d_expand_bias: float32 [2048], P('ws')
- d_shrink_weight: float32 [2048, 512], P('ws')
- d_shrink_bias: float32 [512], P('ws')
Inputs may be any that keep to these rules, and one draw needn't show every extreme that they name: `segment_ids`: segment numbers never fall along a sequence; each document is a run of 1 to 2048 positions, and some document has exactly that many.
All inputs are finite; a program needn't handle non-finite values.
Results may differ from a plain program's by a relative error of at most 0.015.
Values may be sent and summed in bfloat16 or wider, within the bound.
A program may use at most 192 MiB of HBM per device.

v0:
```python
import math

import jax
import jax.numpy as jnp
from jax import lax
from jax.sharding import PartitionSpec as P

HEAD_DIM = 64


NORM_EPS = 1e-06
MASK_FILL = -1e30


def extended(block, sides, width):
    for axis, dim in sides:
        count = lax.axis_size(axis)
        forward = [(i, i + 1) for i in range(count - 1)]
        backward = [(target, source) for source, target in forward]
        low = lax.ppermute(
            lax.slice_in_dim(block, block.shape[dim] - width, None, axis=dim), axis, forward
        )
        high = lax.ppermute(lax.slice_in_dim(block, 0, width, axis=dim), axis, backward)
        block = jnp.concatenate([low, block, high], axis=dim)
    return block


def passed_along(block, axis, distance):
    devices = range(lax.axis_size(axis))
    route = [((i - distance) % len(devices), i) for i in devices]
    return lax.ppermute(block, axis, route)


def to_low(array_in):
    return array_in.astype(jnp.bfloat16)


def smooth_slope(array_in):
    sigma = jax.nn.sigmoid(array_in)
    return sigma * (1.0 + array_in * (1.0 - sigma))


def matmul(left_op, right_op):
    return jnp.dot(left_op, right_op, preferred_element_type=jnp.float32)


def outer_sum(left_op, right_op):
    return lax.dot_general(
        left_op, right_op, (((0,), (0,)), ((), ())), preferred_element_type=jnp.float32
    )


def back_mul(grad_in, weight):
    return lax.dot_general(
        grad_in, weight, (((1,), (1,)), ((), ())), preferred_element_type=jnp.float32
    )


def col_sum(grad_in):
    return jnp.sum(grad_in.astype(jnp.float32), axis=0)


def norm_fwd(array_in, gain_vec, shift_vec):
    average = jnp.mean(array_in, axis=-1, keepdims=True)
    centred = array_in - average
    inv_std = lax.rsqrt(jnp.mean(centred * centred, axis=-1, keepdims=True) + NORM_EPS)
    normed = centred * inv_std
    return (normed * gain_vec + shift_vec, normed, inv_std)


def norm_back(grad_in, normed, inv_std, gain_vec):
    scaled = grad_in * gain_vec
    inner_term = jnp.mean(scaled, axis=-1, keepdims=True)
    cross_term = jnp.mean(scaled * normed, axis=-1, keepdims=True)
    return (
        inv_std * (scaled - inner_term - normed * cross_term),
        jnp.sum(grad_in * normed, axis=0),
        jnp.sum(grad_in, axis=0),
    )


def masked_rows(rim_rows, seg_rim, seg_own, first_row, row_count):
    keep_mask = (lax.slice_in_dim(seg_rim, first_row, first_row + row_count) == seg_own)[:, None]
    return jnp.where(
        keep_mask,
        lax.slice_in_dim(rim_rows, first_row, first_row + row_count),
        jnp.zeros((), rim_rows.dtype),
    )


def head_view(flat_rows):
    return flat_rows.reshape(flat_rows.shape[0], -1, HEAD_DIM)


def score_block(queries, key_heads, seg_rows, seg_cols):
    scores = jnp.einsum(
        "qhd,khd->hqk", queries, key_heads, preferred_element_type=jnp.float32
    ) * HEAD_DIM ** (-0.5)
    same_doc = (seg_rows[:, None] == seg_cols[None, :])[None]
    return (scores, same_doc)


def grad_block(queries, key_heads, value_heads, out_heads, log_sum, row_inner, seg_rows, seg_cols):
    scores, same_doc = score_block(queries, key_heads, seg_rows, seg_cols)
    attn_prob = jnp.where(same_doc, jnp.exp(scores - log_sum[:, :, None]), 0.0)
    prob_grad = jnp.einsum(
        "qhd,khd->hqk", out_heads, value_heads, preferred_element_type=jnp.float32
    )
    score_grad = to_low(attn_prob * (prob_grad - row_inner[:, :, None]))
    query_term = jnp.einsum(
        "hqk,khd->qhd", score_grad, key_heads, preferred_element_type=jnp.float32
    ) * HEAD_DIM ** (-0.5)
    key_term = jnp.einsum(
        "hqk,qhd->khd", score_grad, queries, preferred_element_type=jnp.float32
    ) * HEAD_DIM ** (-0.5)
    value_term = jnp.einsum(
        "hqk,qhd->khd", to_low(attn_prob), out_heads, preferred_element_type=jnp.float32
    )
    return (query_term, key_term, value_term)


def body(
    tokens,
    segment_ids,
    out_grad,
    ln1_gain,
    ln1_bias,
    glu_weight,
    glu_bias,
    ln2_gain,
    ln2_bias,
    left_weight,
    left_bias,
    conv_weight,
    conv_bias,
    ln3_gain,
    ln3_bias,
    depth_weight,
    point_weight,
    point_bias,
    ln4_gain,
    ln4_bias,
    qkv_weight,
    attn_out_weight,
    attn_out_bias,
    ln5_gain,
    ln5_bias,
    expand_weight,
    expand_bias,
    shrink_weight,
    shrink_bias,
):
    (
        n1_gain,
        n1_shift,
        glu_w,
        glu_b,
        n2_gain,
        n2_shift,
        left_w,
        left_b,
        conv_w,
        conv_b,
        n3_gain,
        n3_shift,
        depth_w,
        point_w,
        point_b,
        n4_gain,
        n4_shift,
        qkv_w,
        attn_w,
        attn_b,
        n5_gain,
        n5_shift,
        expand_w,
        expand_b,
        shrink_w,
        shrink_b,
    ) = (
        lax.all_gather(to_low(ln1_gain), "ws", axis=0, tiled=True),
        lax.all_gather(to_low(ln1_bias), "ws", axis=0, tiled=True),
        lax.all_gather(to_low(glu_weight), "ws", axis=0, tiled=True),
        lax.all_gather(to_low(glu_bias), "ws", axis=0, tiled=True),
        lax.all_gather(to_low(ln2_gain), "ws", axis=0, tiled=True),
        lax.all_gather(to_low(ln2_bias), "ws", axis=0, tiled=True),
        lax.all_gather(to_low(left_weight), "ws", axis=0, tiled=True),
        lax.all_gather(to_low(left_bias), "ws", axis=0, tiled=True),
        lax.all_gather(to_low(conv_weight), "ws", axis=1, tiled=True),
        lax.all_gather(to_low(conv_bias), "ws", axis=0, tiled=True),
        lax.all_gather(to_low(ln3_gain), "ws", axis=0, tiled=True),
        lax.all_gather(to_low(ln3_bias), "ws", axis=0, tiled=True),
        lax.all_gather(to_low(depth_weight), "ws", axis=1, tiled=True),
        lax.all_gather(to_low(point_weight), "ws", axis=0, tiled=True),
        lax.all_gather(to_low(point_bias), "ws", axis=0, tiled=True),
        lax.all_gather(to_low(ln4_gain), "ws", axis=0, tiled=True),
        lax.all_gather(to_low(ln4_bias), "ws", axis=0, tiled=True),
        lax.all_gather(to_low(qkv_weight), "ws", axis=0, tiled=True),
        lax.all_gather(to_low(attn_out_weight), "ws", axis=0, tiled=True),
        lax.all_gather(to_low(attn_out_bias), "ws", axis=0, tiled=True),
        lax.all_gather(to_low(ln5_gain), "ws", axis=0, tiled=True),
        lax.all_gather(to_low(ln5_bias), "ws", axis=0, tiled=True),
        lax.all_gather(to_low(expand_weight), "ws", axis=0, tiled=True),
        lax.all_gather(to_low(expand_bias), "ws", axis=0, tiled=True),
        lax.all_gather(to_low(shrink_weight), "ws", axis=0, tiled=True),
        lax.all_gather(to_low(shrink_bias), "ws", axis=0, tiled=True),
    )
    float_t = jnp.float32
    gain_one = n1_gain.astype(float_t)
    gain_two = n2_gain.astype(float_t)
    gain_three = n3_gain.astype(float_t)
    gain_four = n4_gain.astype(float_t)
    gain_five = n5_gain.astype(float_t)
    row_count = tokens.shape[1]
    state_in = tokens[0].astype(float_t)
    model_width = state_in.shape[1]
    seg_own = segment_ids[0]
    seg_all = lax.all_gather(seg_own, "ctx", axis=0, tiled=True)
    ctx_count = lax.axis_size("ctx")
    start_row = lax.axis_index("ctx") * row_count
    seg_rim = lax.dynamic_slice_in_dim(
        jnp.pad(seg_all, 4, constant_values=-1), start_row, row_count + 8
    )
    seg_near = lax.slice_in_dim(seg_rim, 3, row_count + 5)
    ln_out, normed_one, inv_one = norm_fwd(state_in, gain_one, n1_shift.astype(float_t))
    h_one = to_low(ln_out)
    glu_pre = matmul(h_one, glu_w) + glu_b.astype(float_t)
    glu_val = glu_pre[:, :model_width]
    glu_gate = jax.nn.sigmoid(glu_pre[:, model_width:])
    state_one = state_in + glu_val * glu_gate
    ln_out, normed_two, inv_two = norm_fwd(state_one, gain_two, n2_shift.astype(float_t))
    h_two = to_low(ln_out)
    left_pre = matmul(h_two, left_w) + left_b.astype(float_t)
    h_two_rim = extended(h_two, (("ctx", 0),), 1)
    conv_pre = conv_b.astype(float_t)
    for tap_no in range(3):
        conv_pre = conv_pre + matmul(
            masked_rows(h_two_rim, seg_near, seg_own, tap_no, row_count), conv_w[tap_no]
        )
    narrow = conv_pre.shape[1]
    wide_width = left_pre.shape[1]
    mixed_sum = jax.nn.silu(left_pre) + jnp.pad(
        jax.nn.silu(conv_pre), ((0, 0), (0, wide_width - narrow))
    )
    ln_out, normed_three, inv_three = norm_fwd(mixed_sum, gain_three, n3_shift.astype(float_t))
    g_three = to_low(ln_out)
    g_rim = extended(g_three, (("ctx", 0),), 4)
    depth_f = depth_w.astype(float_t)
    depth_acc = jnp.zeros((row_count, wide_width), float_t)
    for tap_no in range(9):
        depth_acc = (
            depth_acc
            + masked_rows(g_rim, seg_rim, seg_own, tap_no, row_count).astype(float_t)
            * depth_f[tap_no]
        )
    depth_out = to_low(depth_acc)
    sep_out = matmul(depth_out, point_w) + point_b.astype(float_t)
    state_two = state_one + jnp.pad(sep_out, ((0, 0), (0, model_width - narrow)))
    ln_out, normed_four, inv_four = norm_fwd(state_two, gain_four, n4_shift.astype(float_t))
    h_four = to_low(ln_out)
    qkv_all = matmul(h_four, qkv_w)
    queries_flat = to_low(qkv_all[:, :model_width])
    queries = head_view(queries_flat)
    keys_flat = to_low(qkv_all[:, model_width : 2 * model_width])
    values_flat = to_low(qkv_all[:, 2 * model_width :])
    head_count = model_width // HEAD_DIM
    keys_whole, values_whole = (
        lax.all_gather(keys_flat, "ctx", axis=0, tiled=True),
        lax.all_gather(values_flat, "ctx", axis=0, tiled=True),
    )
    group_size = math.gcd(ctx_count, 4)
    block_rows = row_count * group_size
    block_total = ctx_count // group_size

    def over_blocks(step_fn, init_carry):

        def block_turn(block_no, carry_in):
            first_row = block_no * block_rows
            pieces = (
                lax.dynamic_slice_in_dim(keys_whole, first_row, block_rows),
                lax.dynamic_slice_in_dim(values_whole, first_row, block_rows),
            )
            return step_fn(carry_in, pieces, first_row)

        return lax.fori_loop(0, block_total, block_turn, init_carry)

    def stats_step(carry_in, pieces, first_row):
        key_piece = pieces[0]
        seg_cols = lax.dynamic_slice_in_dim(seg_all, first_row, key_piece.shape[0])
        run_max, run_sum = carry_in
        scores, same_doc = score_block(queries, head_view(key_piece), seg_own, seg_cols)
        masked = jnp.where(same_doc, scores, MASK_FILL)
        new_max = jnp.maximum(run_max, jnp.max(masked, axis=2))
        exp_terms = jnp.where(same_doc, jnp.exp(masked - new_max[:, :, None]), 0.0)
        return (new_max, run_sum * jnp.exp(run_max - new_max) + jnp.sum(exp_terms, axis=2))

    init_max = jnp.full((head_count, row_count), MASK_FILL, float_t)
    init_sum = jnp.zeros((head_count, row_count), float_t)
    run_max, run_sum = over_blocks(stats_step, (init_max, init_sum))
    log_sum = run_max + jnp.log(run_sum)

    def value_step(carry_in, pieces, first_row):
        key_piece, value_piece = pieces
        seg_cols = lax.dynamic_slice_in_dim(seg_all, first_row, key_piece.shape[0])
        scores, same_doc = score_block(queries, head_view(key_piece), seg_own, seg_cols)
        attn_prob = to_low(jnp.where(same_doc, jnp.exp(scores - log_sum[:, :, None]), 0.0))
        return carry_in + jnp.einsum(
            "hqk,khd->qhd", attn_prob, head_view(value_piece), preferred_element_type=float_t
        )

    attn_acc = over_blocks(value_step, jnp.zeros((row_count, head_count, HEAD_DIM), float_t))
    attn_low = to_low(attn_acc.reshape(row_count, model_width))
    state_three = state_two + matmul(attn_low, attn_w) + attn_b.astype(float_t)
    ln_out, normed_five, inv_five = norm_fwd(state_three, gain_five, n5_shift.astype(float_t))
    h_five = to_low(ln_out)
    expand_pre = matmul(h_five, expand_w) + expand_b.astype(float_t)
    hidden = to_low(jax.nn.silu(expand_pre))
    state_four = state_three + matmul(hidden, shrink_w) + shrink_b.astype(float_t)
    output = to_low(state_four)[None]
    grad_four = out_grad[0].astype(float_t)
    z_grad = to_low(grad_four)
    g_shrink_w = outer_sum(hidden, z_grad)
    g_shrink_b = col_sum(z_grad)
    pre_grad = to_low(back_mul(z_grad, shrink_w) * smooth_slope(expand_pre))
    g_expand_w = outer_sum(h_five, pre_grad)
    g_expand_b = col_sum(pre_grad)
    in_grad, g_n5_gain, g_n5_shift = norm_back(
        back_mul(pre_grad, expand_w), normed_five, inv_five, gain_five
    )
    grad_three = grad_four + in_grad
    y_grad = to_low(grad_three)
    g_attn_w = outer_sum(attn_low, y_grad)
    g_attn_b = col_sum(y_grad)
    o_grad = to_low(back_mul(y_grad, attn_w))
    o_heads = head_view(o_grad)
    row_inner = jnp.einsum("qhd,qhd->hq", o_heads.astype(float_t), attn_acc)
    zero_flat = jnp.zeros((row_count, model_width), float_t)
    zero_heads = jnp.zeros((row_count, head_count, HEAD_DIM), float_t)

    def cycle_turn(turn_no, carry_in):
        query_grad, key_acc, value_acc = carry_in
        anchor = (lax.axis_index("ctx") - turn_no) % ctx_count
        first_row = anchor * row_count
        seg_cols = lax.dynamic_slice_in_dim(seg_all, first_row, row_count)
        key_piece = lax.dynamic_slice_in_dim(keys_whole, first_row, row_count)
        value_piece = lax.dynamic_slice_in_dim(values_whole, first_row, row_count)
        q_acc = query_grad
        k_acc = key_acc
        v_acc = value_acc
        query_term, key_term, value_term = grad_block(
            queries,
            head_view(key_piece),
            head_view(value_piece),
            o_heads,
            log_sum,
            row_inner,
            seg_own,
            seg_cols,
        )
        query_grad = q_acc + query_term
        key_acc = k_acc + key_term.reshape(row_count, model_width)
        value_acc = v_acc + value_term.reshape(row_count, model_width)
        key_acc, value_acc = (
            passed_along(key_acc.astype(jnp.bfloat16), "ctx", 1).astype(key_acc.dtype),
            passed_along(value_acc.astype(jnp.bfloat16), "ctx", 1).astype(value_acc.dtype),
        )
        return (query_grad, key_acc, value_acc)

    query_grad, key_grad, value_grad = lax.fori_loop(
        0, ctx_count, cycle_turn, (zero_heads, zero_flat, zero_flat)
    )
    qkv_grad = jnp.concatenate(
        [to_low(query_grad.reshape(row_count, model_width)), to_low(key_grad), to_low(value_grad)],
        axis=1,
    )
    g_qkv_w = outer_sum(h_four, qkv_grad)
    in_grad, g_n4_gain, g_n4_shift = norm_back(
        back_mul(qkv_grad, qkv_w), normed_four, inv_four, gain_four
    )
    grad_two = grad_three + in_grad
    sep_grad = to_low(grad_two[:, :narrow])
    g_point_w = outer_sum(depth_out, sep_grad)
    g_point_b = col_sum(sep_grad)
    depth_grad = to_low(back_mul(sep_grad, point_w))
    depth_rim = extended(depth_grad, (("ctx", 0),), 4)
    depth_grad_f = depth_grad.astype(float_t)
    g_depth = []
    g3_grad = jnp.zeros((row_count, wide_width), float_t)
    for tap_no in range(9):
        g_depth.append(
            jnp.sum(
                masked_rows(g_rim, seg_rim, seg_own, tap_no, row_count).astype(float_t)
                * depth_grad_f,
                axis=0,
            )
        )
        g3_grad = (
            g3_grad
            + masked_rows(depth_rim, seg_rim, seg_own, 8 - tap_no, row_count).astype(float_t)
            * depth_f[tap_no]
        )
    g_depth_w = jnp.stack(g_depth)
    mixed_grad, g_n3_gain, g_n3_shift = norm_back(g3_grad, normed_three, inv_three, gain_three)
    left_grad = to_low(mixed_grad * smooth_slope(left_pre))
    conv_grad = to_low(mixed_grad[:, :narrow] * smooth_slope(conv_pre))
    g_left_w = outer_sum(h_two, left_grad)
    g_left_b = col_sum(left_grad)
    h_two_grad = back_mul(left_grad, left_w)
    conv_grad_rim = extended(conv_grad, (("ctx", 0),), 1)
    g_conv = []
    for tap_no in range(3):
        g_conv.append(
            outer_sum(masked_rows(h_two_rim, seg_near, seg_own, tap_no, row_count), conv_grad)
        )
        h_two_grad = h_two_grad + back_mul(
            masked_rows(conv_grad_rim, seg_near, seg_own, 2 - tap_no, row_count), conv_w[tap_no]
        )
    g_conv_w = jnp.stack(g_conv)
    g_conv_b = col_sum(conv_grad)
    in_grad, g_n2_gain, g_n2_shift = norm_back(h_two_grad, normed_two, inv_two, gain_two)
    grad_one = grad_two + in_grad
    glu_grad = to_low(
        jnp.concatenate(
            [grad_one * glu_gate, grad_one * glu_val * glu_gate * (1.0 - glu_gate)], axis=1
        )
    )
    g_glu_w = outer_sum(h_one, glu_grad)
    g_glu_b = col_sum(glu_grad)
    in_grad, g_n1_gain, g_n1_shift = norm_back(
        back_mul(glu_grad, glu_w), normed_one, inv_one, gain_one
    )
    grad_zero = grad_one + in_grad
    local_grads = (
        g_n1_gain,
        g_n1_shift,
        g_glu_w,
        g_glu_b,
        g_n2_gain,
        g_n2_shift,
        g_left_w,
        g_left_b,
        g_conv_w,
        g_conv_b,
        g_n3_gain,
        g_n3_shift,
        g_depth_w,
        g_point_w,
        g_point_b,
        g_n4_gain,
        g_n4_shift,
        g_qkv_w,
        g_attn_w,
        g_attn_b,
        g_n5_gain,
        g_n5_shift,
        g_expand_w,
        g_expand_b,
        g_shrink_w,
        g_shrink_b,
    )
    pair_share = (
        lax.psum_scatter(
            local_grads[0].astype(jnp.bfloat16), "ws", scatter_dimension=0, tiled=True
        ).astype(jnp.float32),
        lax.psum_scatter(
            local_grads[1].astype(jnp.bfloat16), "ws", scatter_dimension=0, tiled=True
        ).astype(jnp.float32),
        lax.psum_scatter(
            local_grads[2].astype(jnp.bfloat16), "ws", scatter_dimension=0, tiled=True
        ).astype(jnp.float32),
        lax.psum_scatter(
            local_grads[3].astype(jnp.bfloat16), "ws", scatter_dimension=0, tiled=True
        ).astype(jnp.float32),
        lax.psum_scatter(
            local_grads[4].astype(jnp.bfloat16), "ws", scatter_dimension=0, tiled=True
        ).astype(jnp.float32),
        lax.psum_scatter(
            local_grads[5].astype(jnp.bfloat16), "ws", scatter_dimension=0, tiled=True
        ).astype(jnp.float32),
        lax.psum_scatter(
            local_grads[6].astype(jnp.bfloat16), "ws", scatter_dimension=0, tiled=True
        ).astype(jnp.float32),
        lax.psum_scatter(
            local_grads[7].astype(jnp.bfloat16), "ws", scatter_dimension=0, tiled=True
        ).astype(jnp.float32),
        lax.psum_scatter(
            local_grads[8].astype(jnp.bfloat16), "ws", scatter_dimension=1, tiled=True
        ).astype(jnp.float32),
        lax.psum_scatter(
            local_grads[9].astype(jnp.bfloat16), "ws", scatter_dimension=0, tiled=True
        ).astype(jnp.float32),
        lax.psum_scatter(
            local_grads[10].astype(jnp.bfloat16), "ws", scatter_dimension=0, tiled=True
        ).astype(jnp.float32),
        lax.psum_scatter(
            local_grads[11].astype(jnp.bfloat16), "ws", scatter_dimension=0, tiled=True
        ).astype(jnp.float32),
        lax.psum_scatter(
            local_grads[12].astype(jnp.bfloat16), "ws", scatter_dimension=1, tiled=True
        ).astype(jnp.float32),
        lax.psum_scatter(
            local_grads[13].astype(jnp.bfloat16), "ws", scatter_dimension=0, tiled=True
        ).astype(jnp.float32),
        lax.psum_scatter(
            local_grads[14].astype(jnp.bfloat16), "ws", scatter_dimension=0, tiled=True
        ).astype(jnp.float32),
        lax.psum_scatter(
            local_grads[15].astype(jnp.bfloat16), "ws", scatter_dimension=0, tiled=True
        ).astype(jnp.float32),
        lax.psum_scatter(
            local_grads[16].astype(jnp.bfloat16), "ws", scatter_dimension=0, tiled=True
        ).astype(jnp.float32),
        lax.psum_scatter(
            local_grads[17].astype(jnp.bfloat16), "ws", scatter_dimension=0, tiled=True
        ).astype(jnp.float32),
        lax.psum_scatter(
            local_grads[18].astype(jnp.bfloat16), "ws", scatter_dimension=0, tiled=True
        ).astype(jnp.float32),
        lax.psum_scatter(
            local_grads[19].astype(jnp.bfloat16), "ws", scatter_dimension=0, tiled=True
        ).astype(jnp.float32),
        lax.psum_scatter(
            local_grads[20].astype(jnp.bfloat16), "ws", scatter_dimension=0, tiled=True
        ).astype(jnp.float32),
        lax.psum_scatter(
            local_grads[21].astype(jnp.bfloat16), "ws", scatter_dimension=0, tiled=True
        ).astype(jnp.float32),
        lax.psum_scatter(
            local_grads[22].astype(jnp.bfloat16), "ws", scatter_dimension=0, tiled=True
        ).astype(jnp.float32),
        lax.psum_scatter(
            local_grads[23].astype(jnp.bfloat16), "ws", scatter_dimension=0, tiled=True
        ).astype(jnp.float32),
        lax.psum_scatter(
            local_grads[24].astype(jnp.bfloat16), "ws", scatter_dimension=0, tiled=True
        ).astype(jnp.float32),
        lax.psum_scatter(
            local_grads[25].astype(jnp.bfloat16), "ws", scatter_dimension=0, tiled=True
        ).astype(jnp.float32),
    )
    own_grads = tuple(
        lax.psum(
            (
                pair_share[0],
                pair_share[1],
                pair_share[2],
                pair_share[3],
                pair_share[4],
                pair_share[5],
                pair_share[6],
                pair_share[7],
                pair_share[8],
                pair_share[9],
                pair_share[10],
                pair_share[11],
                pair_share[12],
                pair_share[13],
                pair_share[14],
                pair_share[15],
                pair_share[16],
                pair_share[17],
                pair_share[18],
                pair_share[19],
                pair_share[20],
                pair_share[21],
                pair_share[22],
                pair_share[23],
                pair_share[24],
                pair_share[25],
            ),
            "ctx",
        )
    )
    return (output, grad_zero[None]) + own_grads


def solution(mesh):
    return jax.shard_map(
        body,
        mesh=mesh,
        in_specs=(
            P("ws", "ctx", None),
            P("ws", "ctx"),
            P("ws", "ctx", None),
            P("ws"),
            P("ws"),
            P("ws", None),
            P("ws"),
            P("ws"),
            P("ws"),
            P("ws", None),
            P("ws"),
            P(None, "ws", None),
            P("ws"),
            P("ws"),
            P("ws"),
            P(None, "ws"),
            P("ws", None),
            P("ws"),
            P("ws"),
            P("ws"),
            P("ws", None),
            P("ws", None),
            P("ws"),
            P("ws"),
            P("ws"),
            P("ws", None),
            P("ws"),
            P("ws", None),
            P("ws"),
        ),
        out_specs=(
            P("ws", "ctx", None),
            P("ws", "ctx", None),
            P("ws"),
            P("ws"),
            P("ws", None),
            P("ws"),
            P("ws"),
            P("ws"),
            P("ws", None),
            P("ws"),
            P(None, "ws", None),
            P("ws"),
            P("ws"),
            P("ws"),
            P(None, "ws"),
            P("ws", None),
            P("ws"),
            P("ws"),
            P("ws"),
            P("ws", None),
            P("ws", None),
            P("ws"),
            P("ws"),
            P("ws"),
            P("ws", None),
            P("ws"),
            P("ws", None),
            P("ws"),
        ),
        check_vma=False,
    )
```

profile of v0, /device:TPU:0, one launch (start us, length us, event | category | flops | bytes accessed | tf_op | source)
XLA Modules:
  0.0 1285.5 jit_solution(17358077149953843502)
XLA Ops:
  27.5 42.2 %all-gather = s32[1,4096]{1,0:T(1,128)S(1)} all-gather(s32[1,256]{1,0:T(1,128)S(1)} %copy-done.47), channel_id=2, replica_groups=mesh['ctx'=16,'ws'=2] {'ctx'}, dimensions={1}, use_global_device_ids=true | all-gather | bytes 17408 | tf_op jit(solution)/shard_map/all_gather | solution.py:218
  101.7 6.5 fusion.32
  130.6 58.6 %all-gather.33.cloned.1.call-done = bf16[4096,512]{1,0:T(8,128)(2,1)} async-done(((bf16[256,512]{1,0:T(8,128)(2,1)}), bf16[4096,512]{1,0:T(8,128)(2,1)}) %all-gather.33.cloned.1.call-update) | async-done | bytes 4194320 | tf_op jit(solution)/shard_map/all_gather | solution.py:268
  189.2 6.4 copy.88
  195.6 47.7 %while.50 = (s32[]{:T(128)}, f32[8,256]{1,0:T(8,128)S(1)}, f32[8,256]{1,0:T(8,128)S(1)}, s32[1,256]{1,0:T(1,128)S(1)}, s32[4096]{0:T(1024)S(1)}, /*index=5*/bf16...) while((s32[]{:T(128)}, f32[8,256]{1,0:T(8,128)S(1)}, ...), condition=%wide.region_11.12_spmd.clone, body=%wide.region_8.11_spmd.clone.sunk | while | flops 285485056 | bytes 21091508 | solution.py:285
  197.1 5.8 fusion.233
  221.1 5.8 fusion.233
  243.9 23.2 %all-gather.31.cloned.1.call-done = bf16[4096,512]{1,0:T(8,128)(2,1)} async-done(((bf16[256,512]{1,0:T(8,128)(2,1)}), bf16[4096,512]{1,0:T(8,128)(2,1)}) %all-gather.31.cloned.1.call-update) | async-done | bytes 4194320 | tf_op jit(solution)/shard_map/all_gather | solution.py:269
  267.1 6.4 copy.87
  273.5 31.0 %while.51 = (s32[]{:T(128)}, f32[256,8,64]{0,2,1:T(8,128)}, bf16[4096,512]{0,1:T(8,128)(2,1)}, s32[1,256]{1,0:T(1,128)S(1)}, s32[4096]{0:T(1024)S(1)}, /*index=5...) while((s32[]{:T(128)}, f32[256,8,64]{0,2,1:T(8,128)}, ...), condition=%wide.region_13.14_spmd.clone, body=%wide.region_12.13_spmd.clone.sunk | while | flops 545783808 | bytes 8148157 | solution.py:285
  319.6 354.4 %while.52 = (s32[]{:T(128)}, f32[256,8,64]{0,2,1:T(8,128)}, f32[256,512]{0,1:T(8,128)}, f32[256,512]{0,1:T(8,128)}, bf16[4096,512]{0,1:T(8,128)(2,1)}, /*index=5...) while((s32[]{:T(128)}, f32[256,8,64]{0,2,1:T(8,128)}, ...), condition=%wide.region_19.20_spmd.clone, body=%wide.region_18.19_spmd.clone.sunk | while | flops 340852736 | bytes 26104376 | solution.py:369
  332.9 6.8 collective-permute-done
  355.1 8.7 collective-permute-done
  378.3 8.2 collective-permute-done
  401.0 7.3 collective-permute-done
  422.8 6.8 collective-permute-done
  444.2 6.8 collective-permute-done
  465.5 6.8 collective-permute-done
  486.8 6.8 collective-permute-done
  508.2 6.8 collective-permute-done
  529.5 6.8 collective-permute-done
  550.8 6.8 collective-permute-done
  572.2 6.8 collective-permute-done
  593.5 6.8 collective-permute-done
  615.4 6.8 collective-permute-done
  638.4 6.8 collective-permute-done
  662.5 6.8 collective-permute-done
  697.1 15.8 %multiply_reduce_fusion = (bf16[2048]{0:T(1024)(128)(2,1)}, f32[256]{0:T(256)S(1)}, f32[256]{0:T(256)S(1)}, bf16[2048]{0:T(1024)(128)(2,1)}, f32[256,2048]{1,0:T(8,128)S(1)}) fusion(f32[256,2048]{1,0:T(8,128)S(1)} %get-tuple-element.897, f32[256]{0:T(256)} %copy-done.68, f32[256]{0:T(256)S(1)} %broadcast_multiply_fusion.2, ...), kind=kLoop, calls=%fused_computation.83 | loop fusion | flops 39841280 | bytes 5372160 | tf_op jit(solution)/shard_map/reduce_sum | solution.py:77
  766.3 13.6 %reduce-scatter.24.cloned.1.call-done = bf16[256,2048]{1,0:T(8,128)(2,1)} async-done(((bf16[512,2048]{1,0:T(8,128)(2,1)}), bf16[256,2048]{1,0:T(8,128)(2,1)}) %reduce-scatter.24.cloned.1.call-update) | async-done | bytes 1048592 | tf_op jit(solution)/shard_map/reduce_scatter | solution.py:528
  779.9 12.9 %reduce-scatter.26.cloned.1.call-done = bf16[1024,512]{1,0:T(8,128)(2,1)} async-done(((bf16[2048,512]{1,0:T(8,128)(2,1)}), bf16[1024,512]{1,0:T(8,128)(2,1)}) %reduce-scatter.26.cloned.1.call-update) | async-done | bytes 1048592 | tf_op jit(solution)/shard_map/reduce_scatter | solution.py:534
  792.8 13.6 %reduce-scatter.12.cloned.1.call-done = bf16[256,2048]{1,0:T(8,128)(2,1)} async-done(((bf16[512,2048]{1,0:T(8,128)(2,1)}), bf16[256,2048]{1,0:T(8,128)(2,1)}) %reduce-scatter.12.cloned.1.call-update) | async-done | bytes 1048592 | tf_op jit(solution)/shard_map/reduce_scatter | solution.py:480
  806.4 472.4 %all-reduce.23 = (f32[256]{0:T(256)}, f32[256]{0:T(256)}, f32[256,1024]{1,0:T(8,128)}, f32[512]{0:T(512)}, f32[256]{0:T(256)}, /*index=5*/f32[256]{0:T(256)}, f3...) all-reduce(f32[256]{0:T(256)S(1)} %dynamic-slice_convert_fusion.16,, ...), channel_id=1, replica_groups=mesh['ctx'=16,'ws'=2] {'ctx'}, use_global_device_ids=true, to_apply=%region_30.31 | all-reduce | flops 2834688 | bytes 17022976 | tf_op jit(solution)/shard_map/psum | solution.py:542
  (932 shorter events, 468.5 us)
Async XLA Ops:
  7.2 69.9 %all-gather.23.cloned.1.call-start = ((), (), s32[]{:S(2)}) async-start(), calls=%async_computation.9 | async-start | bytes 1572864 | tf_op jit(solution)/shard_map/all_gather | solution.py:183
  9.5 77.9 %all-gather.25.cloned.1.call-start = ((), (), s32[]{:S(2)}) async-start(), calls=%async_computation.10 | async-start | bytes 3145728 | tf_op jit(solution)/shard_map/all_gather | solution.py:187
  10.7 97.4 %all-gather.27.cloned.1.call-start = ((), (), s32[]{:S(2)}) async-start(), calls=%async_computation.11 | async-start | bytes 1572864 | tf_op jit(solution)/shard_map/all_gather | solution.py:194
  11.9 98.7 %all-gather.29.cloned.1.call-start = ((), (), s32[]{:S(2)}) async-start(), calls=%async_computation.12 | async-start | bytes 2359296 | tf_op jit(solution)/shard_map/all_gather | solution.py:198
  13.4 175.8 %all-gather.33.cloned.1.call-start = ((), (), s32[]{:S(2)}) async-start(), calls=%async_computation.14 | async-start | bytes 4456448 | tf_op jit(solution)/shard_map/all_gather | solution.py:268
  113.5 153.6 %all-gather.31.cloned.1.call-start = ((), (), s32[]{:S(2)}) async-start(), calls=%async_computation.13 | async-start | bytes 4456448 | tf_op jit(solution)/shard_map/all_gather | solution.py:269
  114.1 194.0 %all-gather.35.cloned.1.call-start = ((), (), s32[]{:S(2)}) async-start(), calls=%async_computation.15 | async-start | bytes 3145728 | tf_op jit(solution)/shard_map/all_gather | solution.py:203
  116.9 195.0 %all-gather.37.cloned.1.call-start = ((), (), s32[]{:S(2)}) async-start(), calls=%async_computation.16 | async-start | bytes 3145728 | tf_op jit(solution)/shard_map/all_gather | solution.py:205
  119.8 644.7 %reduce-scatter.16.cloned.1.call-start = ((), (), s32[]{:S(2)}) async-start(), calls=%async_computation.20 | async-start | bytes 98304 | tf_op jit(solution)/shard_map/reduce_scatter | solution.py:498
  326.6 13.2 %collective-permute-start = (bf16[256,512]{0,1:T(8,128)(2,1)}, bf16[256,512]{0,1:T(8,128)(2,1)}, u32[]{:S(2)}, u32[]{:S(2)}) collective-permute-start(bf16[256,512]{0,1:T(8,128)(2,1)} %fusion.252), channel_id=1, source_target_pairs={{30,0},{0,2},{2,4},{4,6},{6,8},{8,10},{10,12},{12,14},{14,16},{16,... | collective-permute-start | bytes 786440 | tf_op jit(solution)/shard_map/while/body/eval_jaxpr/ppermute | solution.py:31
  329.4 13.6 %collective-permute-start.1 = (bf16[256,512]{0,1:T(8,128)(2,1)}, bf16[256,512]{0,1:T(8,128)(2,1)}, u32[]{:S(2)}, u32[]{:S(2)}) collective-permute-start(bf16[256,512]{0,1:T(8,128)(2,1)} %fusion.254), channel_id=1, source_target_pairs={{30,0},{0,2},{2,4},{4,6},{6,8},{8,10},{10,12},{12,14},{14,16},{16,... | collective-permute-start | bytes 786440 | tf_op jit(solution)/shard_map/while/body/eval_jaxpr/ppermute | solution.py:31
  351.2 12.6 collective-permute-start
  352.4 14.2 %collective-permute-start.1 = (bf16[256,512]{0,1:T(8,128)(2,1)}, bf16[256,512]{0,1:T(8,128)(2,1)}, u32[]{:S(2)}, u32[]{:S(2)}) collective-permute-start(bf16[256,512]{0,1:T(8,128)(2,1)} %fusion.254), channel_id=1, source_target_pairs={{30,0},{0,2},{2,4},{4,6},{6,8},{8,10},{10,12},{12,14},{14,16},{16,... | collective-permute-start | bytes 786440 | tf_op jit(solution)/shard_map/while/body/eval_jaxpr/ppermute | solution.py:31
  376.1 13.3 %collective-permute-start.1 = (bf16[256,512]{0,1:T(8,128)(2,1)}, bf16[256,512]{0,1:T(8,128)(2,1)}, u32[]{:S(2)}, u32[]{:S(2)}) collective-permute-start(bf16[256,512]{0,1:T(8,128)(2,1)} %fusion.254), channel_id=1, source_target_pairs={{30,0},{0,2},{2,4},{4,6},{6,8},{8,10},{10,12},{12,14},{14,16},{16,... | collective-permute-start | bytes 786440 | tf_op jit(solution)/shard_map/while/body/eval_jaxpr/ppermute | solution.py:31
  398.8 12.3 collective-permute-start.1
  441.9 11.9 collective-permute-start.1
  463.3 11.9 collective-permute-start.1
  505.9 11.9 collective-permute-start.1
  569.9 11.9 collective-permute-start.1
  591.2 12.5 collective-permute-start.1
  613.2 13.5 %collective-permute-start.1 = (bf16[256,512]{0,1:T(8,128)(2,1)}, bf16[256,512]{0,1:T(8,128)(2,1)}, u32[]{:S(2)}, u32[]{:S(2)}) collective-permute-start(bf16[256,512]{0,1:T(8,128)(2,1)} %fusion.254), channel_id=1, source_target_pairs={{30,0},{0,2},{2,4},{4,6},{6,8},{8,10},{10,12},{12,14},{14,16},{16,... | collective-permute-start | bytes 786440 | tf_op jit(solution)/shard_map/while/body/eval_jaxpr/ppermute | solution.py:31
  636.2 14.6 %collective-permute-start.1 = (bf16[256,512]{0,1:T(8,128)(2,1)}, bf16[256,512]{0,1:T(8,128)(2,1)}, u32[]{:S(2)}, u32[]{:S(2)}) collective-permute-start(bf16[256,512]{0,1:T(8,128)(2,1)} %fusion.254), channel_id=1, source_target_pairs={{30,0},{0,2},{2,4},{4,6},{6,8},{8,10},{10,12},{12,14},{14,16},{16,... | collective-permute-start | bytes 786440 | tf_op jit(solution)/shard_map/while/body/eval_jaxpr/ppermute | solution.py:31
  683.4 13.8 %collective-permute-start.7 = (bf16[4,2048]{1,0:T(4,128)(2,1)}, bf16[4,2048]{1,0:T(4,128)(2,1)}, u32[]{:S(2)}, u32[]{:S(2)}) collective-permute-start(bf16[4,2048]{1,0:T(4,128)(2,1)} %get-tuple-element.905), channel_id=1, source_target_pairs={{0,2},{2,4},{4,6},{6,8},{8,10},{10,12},{12,14},{14,16},{16,18},{18... | collective-permute-start | bytes 49160 | tf_op jit(solution)/shard_map/ppermute | solution.py:20
  685.2 11.9 collective-permute-start.6
  695.8 68.6 %reduce-scatter.22.cloned.1.call-start = ((), (), s32[]{:S(2)}) async-start(), calls=%async_computation.23 | async-start | bytes 786432 | tf_op jit(solution)/shard_map/reduce_scatter | solution.py:516
  697.1 67.4 %reduce-scatter.14.cloned.1.call-start = ((), (), s32[]{:S(2)}) async-start(), calls=%async_computation.19 | async-start | bytes 1179648 | tf_op jit(solution)/shard_map/reduce_scatter | solution.py:486
  718.8 45.6 %reduce-scatter.18.cloned.1.call-start = ((), (), s32[]{:S(2)}) async-start(), calls=%async_computation.21 | async-start | bytes 1572864 | tf_op jit(solution)/shard_map/reduce_scatter | solution.py:501
  720.4 44.0 %reduce-scatter.10.cloned.1.call-start = ((), (), s32[]{:S(2)}) async-start(), calls=%async_computation.17 | async-start | bytes 1572864 | tf_op jit(solution)/shard_map/reduce_scatter | solution.py:468
  734.4 31.9 %reduce-scatter.20.cloned.1.call-start = ((), (), s32[]{:S(2)}) async-start(), calls=%async_computation.22 | async-start | bytes 2359296 | tf_op jit(solution)/shard_map/reduce_scatter | solution.py:513
  737.6 42.3 %reduce-scatter.24.cloned.1.call-start = ((), (), s32[]{:S(2)}) async-start(), calls=%async_computation.24 | async-start | bytes 3145728 | tf_op jit(solution)/shard_map/reduce_scatter | solution.py:528
  741.4 51.4 %reduce-scatter.26.cloned.1.call-start = ((), (), s32[]{:S(2)}) async-start(), calls=%async_computation.25 | async-start | bytes 3145728 | tf_op jit(solution)/shard_map/reduce_scatter | solution.py:534
  745.2 61.2 %reduce-scatter.12.cloned.1.call-start = ((), (), s32[]{:S(2)}) async-start(), calls=%async_computation.18 | async-start | bytes 3145728 | tf_op jit(solution)/shard_map/reduce_scatter | solution.py:480
  (211 other events, 1671.1 us)
Sparse Core Ops, SparseCore 0:
  10.2 11.7 all-gather.22
  24.1 11.6 all-gather.24
  38.0 10.1 all-gather.26
  50.2 10.9 all-gather.28
  113.7 75.4 all-gather.32
  192.4 74.6 all-gather.30
  269.2 9.1 all-gather.34
  280.5 11.7 all-gather.36
  695.9 9.0 reduce-scatter.15
  707.2 9.1 reduce-scatter.21
  719.2 9.6 reduce-scatter.13
  731.0 9.6 reduce-scatter.17
  743.6 9.7 reduce-scatter.9
  756.1 10.1 reduce-scatter.19
  769.1 10.7 reduce-scatter.23
  782.0 10.7 reduce-scatter.25
  795.6 10.7 reduce-scatter.11
where the time goes:
time: 1300 us; the launch traced here: 1290 us
  blocking collectives  555 us (43%)
  waiting for transfers between devices  263 us (20%)
  matrix products  192 us (15%)
  other arithmetic  156 us (12%)
  local copies, waits for them, and re-layouts  76.9 us (6%)
  starting transfers between devices  20.8 us (2%)
  between operations  19 us (1%)
    psum x1, blocking collectives, body(): lax.psum((pair_share[0], pair_share[1], pair_share[2], pair_share[3], pai...  472 us
    ppermute x32, waiting for transfers between devices, passed_along(): return lax.ppermute(block, axis, route)  135 us
    all_gather x1, waiting for transfers between devices, body(): lax.all_gather(keys_flat, 'ctx', axis=0, tiled=True)  58.6 us
    dot_general x20, matrix products, score_block(): jnp.einsum('qhd,khd->hqk', queries, key_heads, preferred_element_type=jnp...  48.5 us
    all_gather x1, blocking collectives, body(): seg_all = lax.all_gather(seg_own, 'ctx', axis=0, tiled=True)  42.2 us
    dot_general x16, matrix products, grad_block(): jnp.einsum('hqk,khd->qhd', score_grad, key_heads, preferred_element_type=...  35.6 us
    convert_element_type x16, other arithmetic, cycle_turn(): passed_along(key_acc.astype(jnp.bfloat16), 'ctx', 1).astype(key_acc.dtype)  28.4 us
    convert_element_type x16, other arithmetic, cycle_turn(): passed_along(value_acc.astype(jnp.bfloat16), 'ctx', 1)  28.3 us
  transfers between devices with their start and end apart: 57, of which 39 were waited for; matrix products, arithmetic and copies ran while one was open for 21% of the time, Pallas kernels for 0%

commit v1 on v0

--- a/solution.py
+++ b/solution.py
@@ -1,8 +1,11 @@
+import functools
 import math
 
 import jax
 import jax.numpy as jnp
 from jax import lax
+from jax.experimental import pallas as pl
+from jax.experimental.pallas import tpu as pltpu
 from jax.sharding import PartitionSpec as P
 
 HEAD_DIM = 64
@@ -23,12 +26,6 @@
         high = lax.ppermute(lax.slice_in_dim(block, 0, width, axis=dim), axis, backward)
         block = jnp.concatenate([low, block, high], axis=dim)
     return block
-
-
-def passed_along(block, axis, distance):
-    devices = range(lax.axis_size(axis))
-    route = [((i - distance) % len(devices), i) for i in devices]
-    return lax.ppermute(block, axis, route)
 
 
 def to_low(array_in):
@@ -92,31 +89,576 @@
     return flat_rows.reshape(flat_rows.shape[0], -1, HEAD_DIM)
 
 
-def score_block(queries, key_heads, seg_rows, seg_cols):
-    scores = jnp.einsum(
-        "qhd,khd->hqk", queries, key_heads, preferred_element_type=jnp.float32
-    ) * HEAD_DIM ** (-0.5)
-    same_doc = (seg_rows[:, None] == seg_cols[None, :])[None]
-    return (scores, same_doc)
-
-
-def grad_block(queries, key_heads, value_heads, out_heads, log_sum, row_inner, seg_rows, seg_cols):
-    scores, same_doc = score_block(queries, key_heads, seg_rows, seg_cols)
-    attn_prob = jnp.where(same_doc, jnp.exp(scores - log_sum[:, :, None]), 0.0)
-    prob_grad = jnp.einsum(
-        "qhd,khd->hqk", out_heads, value_heads, preferred_element_type=jnp.float32
-    )
-    score_grad = to_low(attn_prob * (prob_grad - row_inner[:, :, None]))
-    query_term = jnp.einsum(
-        "hqk,khd->qhd", score_grad, key_heads, preferred_element_type=jnp.float32
-    ) * HEAD_DIM ** (-0.5)
-    key_term = jnp.einsum(
-        "hqk,qhd->khd", score_grad, queries, preferred_element_type=jnp.float32
-    ) * HEAD_DIM ** (-0.5)
-    value_term = jnp.einsum(
-        "hqk,qhd->khd", to_low(attn_prob), out_heads, preferred_element_type=jnp.float32
-    )
-    return (query_term, key_term, value_term)
+MESH_ID = pl.DeviceIdType.MESH
+LANES = 128
+ROW_BLOCK = 16
+KEY_TILE = 512
+VMEM_MOST = 56 * 1024 * 1024
+
+
+def vmem_spec():
+    return pl.BlockSpec(memory_space=pltpu.VMEM)
+
+
+def any_spec():
+    return pl.BlockSpec(memory_space=pl.ANY)
+
+
+def comm_params(number):
+    return pltpu.CompilerParams(
+        collective_id=number, has_side_effects=True, vmem_limit_bytes=VMEM_MOST
+    )
+
+
+def greet(peers):
+    barrier = pltpu.get_barrier_semaphore()
+    for peer in peers:
+        pl.semaphore_signal(barrier, inc=1, device_id=peer, device_id_type=MESH_ID)
+    pl.semaphore_wait(barrier, len(peers))
+
+
+def push(src, dst, sems, at, peer):
+    copy = pltpu.make_async_remote_copy(
+        src_ref=src,
+        dst_ref=dst,
+        send_sem=sems[0].at[at],
+        recv_sem=sems[1].at[at],
+        device_id=peer,
+        device_id_type=MESH_ID,
+    )
+    copy.start()
+    return copy
+
+
+def sem_pair(count):
+    return [pltpu.SemaphoreType.DMA((count,)), pltpu.SemaphoreType.DMA((count,))]
+
+
+def bound(value, step):
+    return pl.multiple_of(value, step)
+
+
+def seg_body(count, row_ref, out_ref, local_sem, send_sem, recv_sem):
+    own, core = lax.axis_index("ctx"), lax.axis_index("ws")
+    peers = [(lax.rem(own + gap, count), core) for gap in range(1, count)]
+    greet(peers)
+    keep = pltpu.make_async_copy(row_ref, out_ref.at[own], local_sem)
+    keep.start()
+    copies = [
+        push(row_ref, out_ref.at[own], (send_sem, recv_sem), gap, peer)
+        for gap, peer in enumerate(peers)
+    ]
+    keep.wait()
+    for copy in copies:
+        copy.wait()
+
+
+def gather_segments(row, count):
+    return pl.pallas_call(
+        functools.partial(seg_body, count),
+        out_shape=jax.ShapeDtypeStruct((count,) + row.shape, row.dtype),
+        in_specs=[vmem_spec()],
+        out_specs=vmem_spec(),
+        scratch_shapes=[pltpu.SemaphoreType.DMA] + sem_pair(count - 1),
+        compiler_params=comm_params(1),
+        name="gather_segments",
+    )(row)
+
+
+def spread_body(count, heads, q_ref, kv_ref, qo_ref, kvo_ref, local_sem, qs, qr, ks, kr):
+    own, core = lax.axis_index("ctx"), lax.axis_index("ws")
+    parts = count // heads
+    rows = kv_ref.shape[0]
+    head, part = own // parts, lax.rem(own, parts)
+    peers = [lax.rem(own + gap, count) for gap in range(1, count)]
+    greet([(peer, core) for peer in peers])
+
+    def q_piece(which):
+        return q_ref.at[pl.ds(bound(which * HEAD_DIM, HEAD_DIM), HEAD_DIM), :]
+
+    def kv_piece(which):
+        return kv_ref.at[:, pl.ds(bound(which * LANES, LANES), LANES)]
+
+    q_slot = qo_ref.at[:, pl.ds(bound(head * rows, rows), rows)]
+    kv_slot = kvo_ref.at[pl.ds(bound(own * rows, rows), rows), :]
+    copies = []
+    for gap in range(1, heads):
+        other = lax.rem(head + gap, heads)
+        copies.append(
+            push(q_piece(other), q_slot, (qs, qr), gap - 1, (other * parts + part, core))
+        )
+    for gap, peer in enumerate(peers):
+        copies.append(push(kv_piece(peer // parts), kv_slot, (ks, kr), gap, (peer, core)))
+    keep_q = pltpu.make_async_copy(q_piece(head), q_slot, local_sem.at[0])
+    keep_kv = pltpu.make_async_copy(kv_piece(head), kv_slot, local_sem.at[1])
+    keep_q.start()
+    keep_kv.start()
+    keep_q.wait()
+    keep_kv.wait()
+    for copy in copies:
+        copy.wait()
+
+
+def spread_heads(q_t, kv, count, heads):
+    rows = kv.shape[0]
+    return pl.pallas_call(
+        functools.partial(spread_body, count, heads),
+        out_shape=(
+            jax.ShapeDtypeStruct((HEAD_DIM, heads * rows), q_t.dtype),
+            jax.ShapeDtypeStruct((count * rows, LANES), kv.dtype),
+        ),
+        in_specs=[vmem_spec(), vmem_spec()],
+        out_specs=(vmem_spec(), vmem_spec()),
+        scratch_shapes=[pltpu.SemaphoreType.DMA((2,))]
+        + sem_pair(heads - 1)
+        + sem_pair(count - 1),
+        compiler_params=comm_params(2),
+        name="spread_heads",
+    )(q_t, kv)
+
+
+def swap_body(count, heads, outward, in_ref, out_ref, local_sem, send_sem, recv_sem):
+    own, core = lax.axis_index("ctx"), lax.axis_index("ws")
+    parts = count // heads
+    head, part = own // parts, lax.rem(own, parts)
+    rows = in_ref.shape[1] if outward else out_ref.shape[1]
+    others = [lax.rem(head + gap, heads) for gap in range(heads)]
+    greet([(other * parts + part, core) for other in others[1:]])
+
+    def tall(ref, which):
+        return ref.at[pl.ds(bound(which * HEAD_DIM, HEAD_DIM), HEAD_DIM), :]
+
+    def wide(ref, which):
+        return ref.at[:, pl.ds(bound(which * rows, rows), rows)]
+
+    take, put = (tall, wide) if outward else (wide, tall)
+    copies = [
+        push(
+            take(in_ref, other),
+            put(out_ref, head),
+            (send_sem, recv_sem),
+            gap,
+            (other * parts + part, core),
+        )
+        for gap, other in enumerate(others[1:])
+    ]
+    keep = pltpu.make_async_copy(take(in_ref, head), put(out_ref, head), local_sem)
+    keep.start()
+    keep.wait()
+    for copy in copies:
+        copy.wait()
+
+
+def swap_heads(block, count, heads, outward, number):
+    if outward:
+        shape = (HEAD_DIM, heads * block.shape[1])
+    else:
+        shape = (heads * HEAD_DIM, block.shape[1] // heads)
+    return pl.pallas_call(
+        functools.partial(swap_body, count, heads, outward),
+        out_shape=jax.ShapeDtypeStruct(shape, block.dtype),
+        in_specs=[vmem_spec()],
+        out_specs=vmem_spec(),
+        scratch_shapes=[pltpu.SemaphoreType.DMA] + sem_pair(heads - 1),
+        compiler_params=comm_params(number),
+        name="swap_heads",
+    )(block)
+
+
+def collect_body(count, heads, dq_ref, dkv_ref, dqo_ref, dkvo_ref, local_sem, qs, qr, ks, kr):
+    own, core = lax.axis_index("ctx"), lax.axis_index("ws")
+    parts = count // heads
+    rows = dqo_ref.shape[1]
+    head, part = own // parts, lax.rem(own, parts)
+    peers = [lax.rem(own + gap, count) for gap in range(1, count)]
+    greet([(peer, core) for peer in peers])
+
+    def dq_piece(which):
+        return dq_ref.at[:, pl.ds(bound(which * rows, rows), rows)]
+
+    def dkv_piece(which):
+        return dkv_ref.at[pl.ds(bound(which * rows, rows), rows), :]
+
+    dq_slot = dqo_ref.at[pl.ds(bound(head * HEAD_DIM, HEAD_DIM), HEAD_DIM), :]
+    dkv_slot = dkvo_ref.at[part, :, pl.ds(bound(head * LANES, LANES), LANES)]
+    copies = []
+    for gap in range(1, heads):
+        other = lax.rem(head + gap, heads)
+        copies.append(
+            push(dq_piece(other), dq_slot, (qs, qr), gap - 1, (other * parts + part, core))
+        )
+    for gap, peer in enumerate(peers):
+        copies.append(push(dkv_piece(peer), dkv_slot, (ks, kr), gap, (peer, core)))
+    keep_q = pltpu.make_async_copy(dq_piece(head), dq_slot, local_sem.at[0])
+    keep_kv = pltpu.make_async_copy(dkv_piece(own), dkv_slot, local_sem.at[1])
+    keep_q.start()
+    keep_kv.start()
+    keep_q.wait()
+    keep_kv.wait()
+    for copy in copies:
+        copy.wait()
+
+
+def collect_heads(dq_t, dkv, count, heads):
+    rows = dkv.shape[0] // count
+    return pl.pallas_call(
+        functools.partial(collect_body, count, heads),
+        out_shape=(
+            jax.ShapeDtypeStruct((heads * HEAD_DIM, rows), dq_t.dtype),
+            jax.ShapeDtypeStruct((count // heads, rows, heads * LANES), dkv.dtype),
+        ),
+        in_specs=[vmem_spec(), vmem_spec()],
+        out_specs=(vmem_spec(), vmem_spec()),
+        scratch_shapes=[pltpu.SemaphoreType.DMA((2,))]
+        + sem_pair(heads - 1)
+        + sem_pair(count - 1),
+        compiler_params=comm_params(3),
+        name="collect_heads",
+    )(dq_t, dkv)
+
+
+def same_doc(segk_ref, seg_q, first):
+    seg_k = segk_ref[pl.ds(first, KEY_TILE), :]
+    return jnp.concatenate([seg_k] * (seg_q.shape[1] // LANES), axis=1) == seg_q
+
+
+def turn_keys(kv_ref, turned):
+    @pl.loop(0, kv_ref.shape[0] // KEY_TILE)
+    def _(tile):
+        first = bound(tile * KEY_TILE, KEY_TILE)
+        turned[:, pl.ds(first, KEY_TILE)] = (
+            kv_ref[pl.ds(first, KEY_TILE), :].astype(jnp.float32).T.astype(jnp.bfloat16)
+        )
+
+
+def attend_body(rows, range_ref, q_ref, kv_ref, segq_ref, segk_ref, o_ref, low_ref, lse_ref, turned):
+    turn_keys(kv_ref, turned)
+
+    @pl.loop(0, q_ref.shape[1] // rows)
+    def _(tile):
+        at = bound(tile * rows, rows)
+        q = q_ref[:, pl.ds(at, rows)] * jnp.bfloat16(HEAD_DIM**-0.5)
+        q_pad = jnp.concatenate([q, jnp.zeros_like(q)], axis=0)
+        seg_q = segq_ref[:, pl.ds(at, rows)]
+
+        def block(key_tile, carry):
+            top, total, acc = carry
+            first = bound(key_tile * KEY_TILE, KEY_TILE)
+            scores = matmul(kv_ref[pl.ds(first, KEY_TILE), :], q_pad)
+            scores = jnp.where(same_doc(segk_ref, seg_q, first), scores, MASK_FILL)
+            new_top = jnp.maximum(top, jnp.max(scores, axis=0, keepdims=True))
+            probs = jnp.exp(scores - new_top)
+            shrink = jnp.exp(top - new_top)
+            total = total * shrink + jnp.sum(probs, axis=0, keepdims=True)
+            values = turned[HEAD_DIM:, pl.ds(first, KEY_TILE)]
+            acc = acc * shrink + matmul(values, probs.astype(jnp.bfloat16))
+            return (new_top, total, acc)
+
+        top, total, acc = lax.fori_loop(
+            range_ref[0, tile],
+            range_ref[1, tile],
+            block,
+            (
+                jnp.full((1, rows), MASK_FILL, jnp.float32),
+                jnp.zeros((1, rows), jnp.float32),
+                jnp.zeros((HEAD_DIM, rows), jnp.float32),
+            ),
+        )
+        out = acc / total
+        o_ref[:, pl.ds(at, rows)] = out
+        low_ref[:, pl.ds(at, rows)] = out.astype(jnp.bfloat16)
+        lse_ref[:, pl.ds(at, rows)] = top + jnp.log(total)
+
+
+def attend(ranges, q_t, kv, seg_q, seg_k, rows):
+    return pl.pallas_call(
+        functools.partial(attend_body, rows),
+        out_shape=(
+            jax.ShapeDtypeStruct(q_t.shape, jnp.float32),
+            jax.ShapeDtypeStruct(q_t.shape, jnp.bfloat16),
+            jax.ShapeDtypeStruct((1, q_t.shape[1]), jnp.float32),
+        ),
+        in_specs=[pl.BlockSpec(memory_space=pltpu.SMEM)] + [vmem_spec()] * 4,
+        out_specs=(vmem_spec(),) * 3,
+        scratch_shapes=[pltpu.VMEM(kv.shape[::-1], jnp.bfloat16)],
+        compiler_params=pltpu.CompilerParams(vmem_limit_bytes=VMEM_MOST),
+        name="attend",
+    )(ranges, q_t, kv, seg_q, seg_k)
+
+
+def attend_back_body(
+    rows,
+    range_ref,
+    q_ref,
+    do_ref,
+    o_ref,
+    lse_ref,
+    kv_ref,
+    segq_ref,
+    segk_ref,
+    dq_ref,
+    dkv_ref,
+    turned,
+    dkv_acc,
+):
+    turn_keys(kv_ref, turned)
+    dkv_acc[...] = jnp.zeros_like(dkv_acc)
+    scale = HEAD_DIM**-0.5
+
+    @pl.loop(0, q_ref.shape[1] // rows)
+    def _(tile):
+        at = bound(tile * rows, rows)
+        q = q_ref[:, pl.ds(at, rows)] * jnp.bfloat16(scale)
+        do = do_ref[:, pl.ds(at, rows)]
+        none = jnp.zeros_like(q)
+        both = jnp.concatenate(
+            [jnp.concatenate([q, none], axis=1), jnp.concatenate([none, do], axis=1)], axis=0
+        )
+        delta = jnp.sum(o_ref[:, pl.ds(at, rows)] * do.astype(jnp.float32), axis=0, keepdims=True)
+        lse = lse_ref[:, pl.ds(at, rows)]
+        seg_q = segq_ref[:, pl.ds(at, rows)]
+
+        def block(key_tile, dq):
+            first = bound(key_tile * KEY_TILE, KEY_TILE)
+            pair = matmul(kv_ref[pl.ds(first, KEY_TILE), :], both)
+            scores, prob_grad = pair[:, :rows], pair[:, rows:]
+            scores = jnp.where(same_doc(segk_ref, seg_q, first), scores, MASK_FILL)
+            probs = jnp.exp(scores - lse)
+            score_grad = (probs * (prob_grad - delta)).astype(jnp.bfloat16)
+            joined = jnp.concatenate([score_grad, probs.astype(jnp.bfloat16)], axis=1)
+            dkv_acc[pl.ds(first, KEY_TILE), :] += back_mul(joined, both)
+            return dq + matmul(turned[:HEAD_DIM, pl.ds(first, KEY_TILE)], score_grad)
+
+        dq = lax.fori_loop(
+            range_ref[0, tile],
+            range_ref[1, tile],
+            block,
+            jnp.zeros((HEAD_DIM, rows), jnp.float32),
+        )
+        dq_ref[:, pl.ds(at, rows)] = (dq * scale).astype(jnp.bfloat16)
+
+    dkv_ref[...] = dkv_acc[...].astype(jnp.bfloat16)
+
+
+def attend_back(ranges, q_t, do_t, o_t, lse, kv, seg_q, seg_k, rows):
+    return pl.pallas_call(
+        functools.partial(attend_back_body, rows),
+        out_shape=(
+            jax.ShapeDtypeStruct(q_t.shape, jnp.bfloat16),
+            jax.ShapeDtypeStruct(kv.shape, jnp.bfloat16),
+        ),
+        in_specs=[pl.BlockSpec(memory_space=pltpu.SMEM)] + [vmem_spec()] * 7,
+        out_specs=(vmem_spec(),) * 2,
+        scratch_shapes=[
+            pltpu.VMEM(kv.shape[::-1], jnp.bfloat16),
+            pltpu.VMEM(kv.shape, jnp.float32),
+        ],
+        compiler_params=pltpu.CompilerParams(vmem_limit_bytes=VMEM_MOST),
+        name="attend_back",
+    )(ranges, q_t, do_t, o_t, lse, kv, seg_q, seg_k)
+
+
+def column_groups(width, bits):
+    tiles = width // LANES
+    unit = 2 ** max(0, bits - 4)
+    shares = [0.182, 0.182, 0.136] * 2
+    sizes = [max(1, round(tiles * share / unit)) * unit for share in shares]
+    sizes[-1] += tiles - sum(sizes)
+    orders = [
+        list(range(bits)),
+        [1, 0] + list(range(2, bits)),
+        list(range(2, bits)) + [0, 1],
+    ] * 2
+    groups, first = [], 0
+    for size, order in zip(sizes, orders):
+        groups.append((first * LANES, size * LANES, order))
+        first += size
+    return groups
+
+
+def add_rows(dst, own, other, place, spot, first):
+    row, tall, col, wide = place
+
+    @pl.loop(0, tall // ROW_BLOCK)
+    def _(step):
+        gap = step * ROW_BLOCK
+        here = (
+            pl.ds(bound(row + gap, ROW_BLOCK), ROW_BLOCK),
+            pl.ds(col if isinstance(col, int) else bound(col, LANES), wide),
+        )
+        there = (pl.ds(bound(spot + gap, ROW_BLOCK), ROW_BLOCK), pl.ds(first, wide))
+        mine, got = own[here].astype(jnp.float32), other[there].astype(jnp.float32)
+        dst[here] = (mine + got).astype(jnp.bfloat16)
+
+
+def reduce_body(count, groups, g_ref, out_ref, buf, got_pair, got, ls, ws, wr, rs, rr, gs, gr):
+    own, core = lax.axis_index("ctx"), lax.axis_index("ws")
+    bits = count.bit_length() - 1
+    rows = buf.shape[0]
+    sibling = (own, 1 - core)
+    bit_of = [lax.rem(own // 2**bit, 2) for bit in range(bits)]
+    partner = [
+        (own + 2**bit - 2 * 2**bit * bit_of[bit], core) for bit in range(bits)
+    ]
+    greet([sibling] + partner)
+
+    sends, state, waiting = [], [], []
+    for at, (first, width, order) in enumerate(groups):
+        cols = pl.ds(first, width)
+        waiting.append(
+            push(
+                g_ref.at[1 - core, :, cols], got_pair.at[:, cols], (ws, wr), at, sibling
+            )
+        )
+        keep = pltpu.make_async_copy(g_ref.at[core, :, cols], buf.at[:, cols], ls.at[at])
+        keep.start()
+        state.append(keep)
+
+    def start_step(at, step, place):
+        first, width, order = groups[at]
+        row, tall, col, wide, spot = place
+        bit = order[step]
+        if tall > ROW_BLOCK:
+            half = tall // 2
+            kept = (row + half * bit_of[bit], half, col, wide)
+            sent = (row + half * (1 - bit_of[bit]), half, col, wide)
+        else:
+            half = wide // 2
+            kept = (row, tall, col + half * bit_of[bit], half)
+            sent = (row, tall, col + half * (1 - bit_of[bit]), half)
+        copy = push(
+            view(buf, sent),
+            got.at[pl.ds(spot, sent[1]), pl.ds(first, sent[3])],
+            (rs, rr),
+            at * bits + step,
+            partner[bit],
+        )
+        return copy, kept, spot
+
+    def view(ref, place):
+        row, tall, col, wide = place
+        if not isinstance(row, int):
+            row = bound(row, ROW_BLOCK)
+        if not isinstance(col, int):
+            col = bound(col, LANES)
+        return ref.at[pl.ds(row, tall), pl.ds(col, wide)]
+
+    places = [None] * len(groups)
+    for at, (first, width, order) in enumerate(groups):
+        state[at].wait()
+        waiting[at].wait()
+        add_rows(buf, buf, got_pair, (0, rows, first, width), 0, first)
+        copy, kept, spot = start_step(at, 0, (0, rows, first, width, 0))
+        places[at] = (copy, kept, spot)
+    trail = [[] for _ in groups]
+    for step in range(bits):
+        for at, (first, width, order) in enumerate(groups):
+            copy, kept, spot = places[at]
+            copy.wait()
+            trail[at].append(kept)
+            row, tall, col, wide = kept
+            last = step == bits - 1
+            target = out_ref if last else buf
+            add_rows(target, buf, got, kept, spot, first)
+            if not last:
+                places[at] = start_step(
+                    at, step + 1, (row, tall, col, wide, spot + tall)
+                )
+    for step in reversed(range(bits)):
+        for at, (first, width, order) in enumerate(groups):
+            place = view(out_ref, trail[at][step])
+            if step < bits - 1:
+                places[at].wait()
+            places[at] = push(
+                place, place, (gs, gr), at * bits + step, partner[order[step]]
+            )
+    for at in range(len(groups)):
+        places[at].wait()
+
+
+def reduce_grads(packed, count):
+    rows, width = packed.shape[1:]
+    bits = count.bit_length() - 1
+    groups = column_groups(width, bits)
+    spots = len(groups)
+    return pl.pallas_call(
+        functools.partial(reduce_body, count, groups),
+        out_shape=jax.ShapeDtypeStruct((rows, width), packed.dtype),
+        in_specs=[any_spec()],
+        out_specs=vmem_spec(),
+        scratch_shapes=[
+            pltpu.VMEM((rows, width), packed.dtype),
+            pltpu.VMEM((rows, width), packed.dtype),
+            pltpu.VMEM((rows + ROW_BLOCK * max(0, bits - 4), width), packed.dtype),
+            pltpu.SemaphoreType.DMA((spots,)),
+        ]
+        + sem_pair(spots)
+        + sem_pair(spots * bits)
+        + sem_pair(spots * bits),
+        compiler_params=comm_params(5),
+        name="reduce_grads",
+    )(packed)
+
+
+def half_shape(grad):
+    axis = 1 if grad.shape[0] in (3, 9) and grad.ndim > 1 else 0
+    return axis, grad.shape[:axis] + (grad.shape[axis] // 2,) + grad.shape[axis + 1 :]
+
+
+def is_small(grad):
+    return grad.ndim == 1 or (grad.ndim == 2 and grad.shape[0] == 9)
+
+
+SMALL_ROWS = 32
+SMALL_WIDTH = 1024
+BLOCK = 256
+
+
+def pack_grads(grads):
+    halves = []
+    for half in range(2):
+        columns, vectors = [], []
+        for grad in grads:
+            axis, shape = half_shape(grad)
+            piece = lax.slice_in_dim(
+                to_low(grad), half * shape[axis], (half + 1) * shape[axis], axis=axis
+            )
+            if is_small(grad):
+                piece = piece.reshape(-1, shape[-1])
+                vectors.append(jnp.pad(piece, ((0, 0), (0, SMALL_WIDTH - shape[-1]))))
+            else:
+                piece = piece.reshape(-1, BLOCK, shape[-1])
+                columns.extend(piece[at] for at in range(piece.shape[0]))
+        small = jnp.concatenate(vectors, axis=0)
+        small = jnp.pad(small, ((0, SMALL_ROWS - small.shape[0]), (0, 0)))
+        small = jnp.concatenate(jnp.split(small, SMALL_WIDTH // BLOCK, axis=1), axis=0)
+        columns.append(jnp.pad(small, ((0, BLOCK - small.shape[0]), (0, 0))))
+        halves.append(jnp.concatenate(columns, axis=1))
+    return jnp.stack(halves)
+
+
+def unpack_grads(packed, grads):
+    results, first, row = [], 0, 0
+    small = packed[: SMALL_ROWS * SMALL_WIDTH // BLOCK, packed.shape[1] - BLOCK :]
+    small = jnp.concatenate(jnp.split(small, SMALL_WIDTH // BLOCK, axis=0), axis=1)
+    for grad in grads:
+        axis, shape = half_shape(grad)
+        if is_small(grad):
+            count = 1 if grad.ndim == 1 else grad.shape[0]
+            piece = small[row : row + count, : shape[-1]].reshape(shape)
+            row += count
+        else:
+            blocks = math.prod(shape) // (BLOCK * shape[-1])
+            piece = jnp.concatenate(
+                [
+                    packed[:, first + at * shape[-1] : first + (at + 1) * shape[-1]]
+                    for at in range(blocks)
+                ],
+                axis=0,
+            ).reshape(shape)
+            first += blocks * shape[-1]
+        results.append(piece.astype(jnp.float32))
+    return tuple(results)
 
 
 def body(
@@ -215,8 +757,8 @@
     state_in = tokens[0].astype(float_t)
     model_width = state_in.shape[1]
     seg_own = segment_ids[0]
-    seg_all = lax.all_gather(seg_own, "ctx", axis=0, tiled=True)
     ctx_count = lax.axis_size("ctx")
+    seg_all = gather_segments(segment_ids, ctx_count).reshape(-1)
     start_row = lax.axis_index("ctx") * row_count
     seg_rim = lax.dynamic_slice_in_dim(
         jnp.pad(seg_all, 4, constant_values=-1), start_row, row_count + 8
@@ -259,57 +801,28 @@
     ln_out, normed_four, inv_four = norm_fwd(state_two, gain_four, n4_shift.astype(float_t))
     h_four = to_low(ln_out)
     qkv_all = matmul(h_four, qkv_w)
-    queries_flat = to_low(qkv_all[:, :model_width])
-    queries = head_view(queries_flat)
-    keys_flat = to_low(qkv_all[:, model_width : 2 * model_width])
-    values_flat = to_low(qkv_all[:, 2 * model_width :])
     head_count = model_width // HEAD_DIM
-    keys_whole, values_whole = (
-        lax.all_gather(keys_flat, "ctx", axis=0, tiled=True),
-        lax.all_gather(values_flat, "ctx", axis=0, tiled=True),
-    )
-    group_size = math.gcd(ctx_count, 4)
-    block_rows = row_count * group_size
-    block_total = ctx_count // group_size
-
-    def over_blocks(step_fn, init_carry):
-
-        def block_turn(block_no, carry_in):
-            first_row = block_no * block_rows
-            pieces = (
-                lax.dynamic_slice_in_dim(keys_whole, first_row, block_rows),
-                lax.dynamic_slice_in_dim(values_whole, first_row, block_rows),
-            )
-            return step_fn(carry_in, pieces, first_row)
-
-        return lax.fori_loop(0, block_total, block_turn, init_carry)
-
-    def stats_step(carry_in, pieces, first_row):
-        key_piece = pieces[0]
-        seg_cols = lax.dynamic_slice_in_dim(seg_all, first_row, key_piece.shape[0])
-        run_max, run_sum = carry_in
-        scores, same_doc = score_block(queries, head_view(key_piece), seg_own, seg_cols)
-        masked = jnp.where(same_doc, scores, MASK_FILL)
-        new_max = jnp.maximum(run_max, jnp.max(masked, axis=2))
-        exp_terms = jnp.where(same_doc, jnp.exp(masked - new_max[:, :, None]), 0.0)
-        return (new_max, run_sum * jnp.exp(run_max - new_max) + jnp.sum(exp_terms, axis=2))
-
-    init_max = jnp.full((head_count, row_count), MASK_FILL, float_t)
-    init_sum = jnp.zeros((head_count, row_count), float_t)
-    run_max, run_sum = over_blocks(stats_step, (init_max, init_sum))
-    log_sum = run_max + jnp.log(run_sum)
-
-    def value_step(carry_in, pieces, first_row):
-        key_piece, value_piece = pieces
-        seg_cols = lax.dynamic_slice_in_dim(seg_all, first_row, key_piece.shape[0])
-        scores, same_doc = score_block(queries, head_view(key_piece), seg_own, seg_cols)
-        attn_prob = to_low(jnp.where(same_doc, jnp.exp(scores - log_sum[:, :, None]), 0.0))
-        return carry_in + jnp.einsum(
-            "hqk,khd->qhd", attn_prob, head_view(value_piece), preferred_element_type=float_t
-        )
-
-    attn_acc = over_blocks(value_step, jnp.zeros((row_count, head_count, HEAD_DIM), float_t))
-    attn_low = to_low(attn_acc.reshape(row_count, model_width))
+    parts = ctx_count // head_count
+    queries_turned = to_low(qkv_all[:, :model_width]).T
+    key_value = (
+        to_low(qkv_all[:, model_width:])
+        .reshape(row_count, 2, head_count, HEAD_DIM)
+        .transpose(0, 2, 1, 3)
+        .reshape(row_count, 2 * model_width)
+    )
+    part = lax.rem(lax.axis_index("ctx"), parts)
+    seg_q = lax.dynamic_slice_in_dim(
+        seg_all.reshape(head_count, parts, row_count), part, 1, axis=1
+    ).reshape(head_count, row_count)
+    key_first = jnp.sum(seg_all[None, :] < seg_q[:, :1], axis=1, dtype=jnp.int32)
+    key_end = jnp.sum(seg_all[None, :] <= seg_q[:, -1:], axis=1, dtype=jnp.int32)
+    ranges = jnp.stack([key_first // KEY_TILE, (key_end + KEY_TILE - 1) // KEY_TILE])
+    seg_q = seg_q.reshape(1, head_count * row_count)
+    seg_k = jnp.broadcast_to(seg_all[:, None], (seg_all.shape[0], LANES))
+    q_head, kv_head = spread_heads(queries_turned, key_value, ctx_count, head_count)
+    o_head, o_low, log_sum = attend(ranges, q_head, kv_head, seg_q, seg_k, row_count)
+    attn_turned = swap_heads(o_low, ctx_count, head_count, False, 4)
+    attn_low = attn_turned.T
     state_three = state_two + matmul(attn_low, attn_w) + attn_b.astype(float_t)
     ln_out, normed_five, inv_five = norm_fwd(state_three, gain_five, n5_shift.astype(float_t))
     h_five = to_low(ln_out)
@@ -331,48 +844,19 @@
     y_grad = to_low(grad_three)
     g_attn_w = outer_sum(attn_low, y_grad)
     g_attn_b = col_sum(y_grad)
-    o_grad = to_low(back_mul(y_grad, attn_w))
-    o_heads = head_view(o_grad)
-    row_inner = jnp.einsum("qhd,qhd->hq", o_heads.astype(float_t), attn_acc)
-    zero_flat = jnp.zeros((row_count, model_width), float_t)
-    zero_heads = jnp.zeros((row_count, head_count, HEAD_DIM), float_t)
-
-    def cycle_turn(turn_no, carry_in):
-        query_grad, key_acc, value_acc = carry_in
-        anchor = (lax.axis_index("ctx") - turn_no) % ctx_count
-        first_row = anchor * row_count
-        seg_cols = lax.dynamic_slice_in_dim(seg_all, first_row, row_count)
-        key_piece = lax.dynamic_slice_in_dim(keys_whole, first_row, row_count)
-        value_piece = lax.dynamic_slice_in_dim(values_whole, first_row, row_count)
-        q_acc = query_grad
-        k_acc = key_acc
-        v_acc = value_acc
-        query_term, key_term, value_term = grad_block(
-            queries,
-            head_view(key_piece),
-            head_view(value_piece),
-            o_heads,
-            log_sum,
-            row_inner,
-            seg_own,
-            seg_cols,
-        )
-        query_grad = q_acc + query_term
-        key_acc = k_acc + key_term.reshape(row_count, model_width)
-        value_acc = v_acc + value_term.reshape(row_count, model_width)
-        key_acc, value_acc = (
-            passed_along(key_acc.astype(jnp.bfloat16), "ctx", 1).astype(key_acc.dtype),
-            passed_along(value_acc.astype(jnp.bfloat16), "ctx", 1).astype(value_acc.dtype),
-        )
-        return (query_grad, key_acc, value_acc)
-
-    query_grad, key_grad, value_grad = lax.fori_loop(
-        0, ctx_count, cycle_turn, (zero_heads, zero_flat, zero_flat)
-    )
-    qkv_grad = jnp.concatenate(
-        [to_low(query_grad.reshape(row_count, model_width)), to_low(key_grad), to_low(value_grad)],
-        axis=1,
-    )
+    o_grad = to_low(back_mul(y_grad, attn_w)).T
+    do_head = swap_heads(o_grad, ctx_count, head_count, True, 6)
+    dq_head, dkv_head = attend_back(
+        ranges, q_head, do_head, o_head, log_sum, kv_head, seg_q, seg_k, row_count
+    )
+    dq_turned, dkv_parts = collect_heads(dq_head, dkv_head, ctx_count, head_count)
+    dkv = (
+        to_low(jnp.sum(dkv_parts.astype(float_t), axis=0))
+        .reshape(row_count, head_count, 2, HEAD_DIM)
+        .transpose(0, 2, 1, 3)
+        .reshape(row_count, 2 * model_width)
+    )
+    qkv_grad = jnp.concatenate([dq_turned.T, dkv], axis=1)
     g_qkv_w = outer_sum(h_four, qkv_grad)
     in_grad, g_n4_gain, g_n4_shift = norm_back(
         back_mul(qkv_grad, qkv_w), normed_four, inv_four, gain_four
@@ -458,120 +942,10 @@
         g_shrink_w,
         g_shrink_b,
     )
-    pair_share = (
-        lax.psum_scatter(
-            local_grads[0].astype(jnp.bfloat16), "ws", scatter_dimension=0, tiled=True
-        ).astype(jnp.float32),
-        lax.psum_scatter(
-            local_grads[1].astype(jnp.bfloat16), "ws", scatter_dimension=0, tiled=True
-        ).astype(jnp.float32),
-        lax.psum_scatter(
-            local_grads[2].astype(jnp.bfloat16), "ws", scatter_dimension=0, tiled=True
-        ).astype(jnp.float32),
-        lax.psum_scatter(
-            local_grads[3].astype(jnp.bfloat16), "ws", scatter_dimension=0, tiled=True
-        ).astype(jnp.float32),
-        lax.psum_scatter(
-            local_grads[4].astype(jnp.bfloat16), "ws", scatter_dimension=0, tiled=True
-        ).astype(jnp.float32),
-        lax.psum_scatter(
-            local_grads[5].astype(jnp.bfloat16), "ws", scatter_dimension=0, tiled=True
-        ).astype(jnp.float32),
-        lax.psum_scatter(
-            local_grads[6].astype(jnp.bfloat16), "ws", scatter_dimension=0, tiled=True
-        ).astype(jnp.float32),
-        lax.psum_scatter(
-            local_grads[7].astype(jnp.bfloat16), "ws", scatter_dimension=0, tiled=True
-        ).astype(jnp.float32),
-        lax.psum_scatter(
-            local_grads[8].astype(jnp.bfloat16), "ws", scatter_dimension=1, tiled=True
-        ).astype(jnp.float32),
-        lax.psum_scatter(
-            local_grads[9].astype(jnp.bfloat16), "ws", scatter_dimension=0, tiled=True
-        ).astype(jnp.float32),
-        lax.psum_scatter(
-            local_grads[10].astype(jnp.bfloat16), "ws", scatter_dimension=0, tiled=True
-        ).astype(jnp.float32),
-        lax.psum_scatter(
-            local_grads[11].astype(jnp.bfloat16), "ws", scatter_dimension=0, tiled=True
-        ).astype(jnp.float32),
-        lax.psum_scatter(
-            local_grads[12].astype(jnp.bfloat16), "ws", scatter_dimension=1, tiled=True
-        ).astype(jnp.float32),
-        lax.psum_scatter(
-            local_grads[13].astype(jnp.bfloat16), "ws", scatter_dimension=0, tiled=True
-        ).astype(jnp.float32),
-        lax.psum_scatter(
-            local_grads[14].astype(jnp.bfloat16), "ws", scatter_dimension=0, tiled=True
-        ).astype(jnp.float32),
-        lax.psum_scatter(
-            local_grads[15].astype(jnp.bfloat16), "ws", scatter_dimension=0, tiled=True
-        ).astype(jnp.float32),
-        lax.psum_scatter(
-            local_grads[16].astype(jnp.bfloat16), "ws", scatter_dimension=0, tiled=True
-        ).astype(jnp.float32),
-        lax.psum_scatter(
-            local_grads[17].astype(jnp.bfloat16), "ws", scatter_dimension=0, tiled=True
-        ).astype(jnp.float32),
-        lax.psum_scatter(
-            local_grads[18].astype(jnp.bfloat16), "ws", scatter_dimension=0, tiled=True
-        ).astype(jnp.float32),
-        lax.psum_scatter(
-            local_grads[19].astype(jnp.bfloat16), "ws", scatter_dimension=0, tiled=True
-        ).astype(jnp.float32),
-        lax.psum_scatter(
-            local_grads[20].astype(jnp.bfloat16), "ws", scatter_dimension=0, tiled=True
-        ).astype(jnp.float32),
-        lax.psum_scatter(
-            local_grads[21].astype(jnp.bfloat16), "ws", scatter_dimension=0, tiled=True
-        ).astype(jnp.float32),
-        lax.psum_scatter(
-            local_grads[22].astype(jnp.bfloat16), "ws", scatter_dimension=0, tiled=True
-        ).astype(jnp.float32),
-        lax.psum_scatter(
-            local_grads[23].astype(jnp.bfloat16), "ws", scatter_dimension=0, tiled=True
-        ).astype(jnp.float32),
-        lax.psum_scatter(
-            local_grads[24].astype(jnp.bfloat16), "ws", scatter_dimension=0, tiled=True
-        ).astype(jnp.float32),
-        lax.psum_scatter(
-            local_grads[25].astype(jnp.bfloat16), "ws", scatter_dimension=0, tiled=True
-        ).astype(jnp.float32),
-    )
-    own_grads = tuple(
-        lax.psum(
-            (
-                pair_share[0],
-                pair_share[1],
-                pair_share[2],
-                pair_share[3],
-                pair_share[4],
-                pair_share[5],
-                pair_share[6],
-                pair_share[7],
-                pair_share[8],
-                pair_share[9],
-                pair_share[10],
-                pair_share[11],
-                pair_share[12],
-                pair_share[13],
-                pair_share[14],
-                pair_share[15],
-                pair_share[16],
-                pair_share[17],
-                pair_share[18],
-                pair_share[19],
-                pair_share[20],
-                pair_share[21],
-                pair_share[22],
-                pair_share[23],
-                pair_share[24],
-                pair_share[25],
-            ),
-            "ctx",
-        )
-    )
-    return (output, grad_zero[None]) + own_grads
+    packed = pack_grads(local_grads)
+    return (output, grad_zero[None]) + unpack_grads(
+        reduce_grads(packed, ctx_count), local_grads
+    )
 
 
 def solution(mesh):

time: 1300 us -> 508 us (0.39)
  blocking collectives: 555 us -> 37.2 us
  Pallas kernels: 0 us -> 266 us
  waiting for transfers between devices: 263 us -> 1.62 us
  matrix products: 192 us -> 47.3 us
  other arithmetic: 156 us -> 61.3 us
  local copies, waits for them, and re-layouts: 76.9 us -> 42.7 us
    psum x1 -> x0, blocking collectives: 472 us -> none  [body(): lax.psum((pair_share[0], pair_share[1], pair_share[2], pair_share[3], pai...]
    pallas_call x0 -> x8, Pallas kernels: none -> 266 us  [the longest x1 131 us: reduce_grads(): pl.pallas_call(functools.partial(reduce_body, count, groups), out_shape=j...]
    dot_general x88 -> x0, matrix products: 140 us -> none  [the longest x20 48.5 us: score_block(): jnp.einsum('qhd,khd->hqk', queries, key_heads, preferred_element_type=jnp...]
    ppermute x32 -> x0, waiting for transfers between devices: 135 us -> none  [passed_along(): return lax.ppermute(block, axis, route)]
    all_gather x2 -> x0, waiting for transfers between devices: 81.8 us -> none  [the longest x1 58.6 us: body(): lax.all_gather(keys_flat, 'ctx', axis=0, tiled=True)]
    convert_element_type x81 -> x11, other arithmetic: 82.6 us -> 15.5 us  [unpack_grads(): results.append(piece.astype(jnp.float32))]
    dynamic_slice x64 -> x2, local copies, waits for them, and re-layouts: 48.9 us -> 0.14 us  [body(): lax.dynamic_slice_in_dim(seg_all.reshape(head_count, parts, row_count), p...]
    all_gather x1 -> x0, blocking collectives: 42.2 us -> none  [body(): seg_all = lax.all_gather(seg_own, 'ctx', axis=0, tiled=True)]
  transfers between devices with their start and end apart: 57 -> 14, of which waited for: 39 -> 2; matrix products, arithmetic and copies ran while one was open for 21% -> 13% of each run, Pallas kernels for 0% -> 16%
where the time goes in v1:
time: 508 us; the launch traced here: 499 us
  Pallas kernels  266 us (52%)
  other arithmetic  61.3 us (12%)
  matrix products  47.3 us (9%)
  local copies, waits for them, and re-layouts  42.7 us (8%)
  blocking collectives  37.2 us (7%)
  starting transfers between devices  24.9 us (5%)
  between operations  18.1 us (4%)
    pallas_call x1, Pallas kernels, reduce_grads(): pl.pallas_call(functools.partial(reduce_body, count, groups), out_shape=j...  131 us
    pallas_call x1, Pallas kernels, spread_heads(): pl.pallas_call(functools.partial(spread_body, count, heads), out_shape=(j...  32.1 us
    pallas_call x2, Pallas kernels, swap_heads(): pl.pallas_call(functools.partial(swap_body, count, heads, outward), out_s...  26.7 us
    pallas_call x1, Pallas kernels, collect_heads(): pl.pallas_call(functools.partial(collect_body, count, heads), out_shape=(...  23.3 us
    pallas_call x1, Pallas kernels, attend_back(): pl.pallas_call(functools.partial(attend_back_body, rows), out_shape=(jax....  20.9 us
    pallas_call x1, Pallas kernels, attend(): pl.pallas_call(functools.partial(attend_body, rows), out_shape=(jax.Shape...  20.7 us
    ppermute x4, starting transfers between devices, extended(): lax.ppermute(lax.slice_in_dim(block, block.shape[dim] - width, None, axis...  19.5 us
    dot_general x10, matrix products, matmul(): return jnp.dot(left_op, right_op, preferred_element_type=jnp.float32)  19.1 us
  transfers between devices with their start and end apart: 14, of which 2 were waited for; matrix products, arithmetic and copies ran while one was open for 13% of the time, Pallas kernels for 16%

profile of v1, /device:TPU:0, one launch (start us, length us, event | category | flops | bytes accessed | tf_op | source)
XLA Modules:
  0.0 498.6 jit_solution(11140048603447573111)
XLA Ops:
  7.3 2.2 convert_element_type.537
  11.9 2.5 convert_element_type.578
  15.8 2.8 convert_element_type.591
  35.7 10.6 %gather_segments.1 = s32[16,1,256]{2,1,0:T(1,128)} custom-call(s32[1,256]{1,0:T(1,128)} %row_ref.1), custom_call_target="tpu_custom_call" | custom-call | tf_op jit(solution)/shard_map/gather_segments/pallas_call | solution.py:157
  49.4 2.3 all_gather.96
  51.8 2.4 all_gather.87
  58.5 4.5 collective-permute-start
  65.7 3.8 fusion.154
  71.8 4.9 collective-permute-start.2
  94.4 6.5 %fusion.9 = bf16[256,2048]{1,0:T(8,128)(2,1)} fusion(f32[2048]{0:T(1024)S(1)} %bitcast.253, f32[2048]{0:T(1024)S(1)} %bitcast.251, f32[2048]{0:T(1024)S(1)} %bitcast.249, f32[2048]{0:T(1024)S(1)} %bitcast.247, f32[2048]{0:T(1024)S(1)} %bitcast.245, f32[2048]{0:T(1024)S(1)} %bitcast.243, f32[2048]{0:T(1024)S(1)} %bitcast.241, f32[2048]{0:T(1024)S(1)} %bitcast.239, ...), kind=kLoop, calls=%fused_computation.38 | loop fusion | flops 35651584 | bytes 2205952 | tf_op jit(solution)/shard_map/convert_element_type | solution.py:32
  103.2 2.2 convolution_convert_fusion.6
  110.9 32.1 %spread_heads.1 = (bf16[64,2048]{1,0:T(8,128)(2,1)}, bf16[4096,128]{1,0:T(8,128)(2,1)}) custom-call(bf16[512,256]{1,0:T(8,128)(2,1)} %slice_bitcast_fusion.q_ref, bf16[256,1024]{1,0:T(8,128)(2,1)} %copy.104.kv_ref), custom_call_target="tpu_custom_call" | custom-call | tf_op jit(solution)/shard_map/spread_heads/pallas_call | solution.py:204
  143.0 2.9 broadcast_in_dim.295.segk_ref
  145.9 20.7 %attend.1 = (f32[64,2048]{1,0:T(8,128)}, bf16[64,2048]{1,0:T(8,128)(2,1)}, f32[1,2048]{1,0:T(1,128)}) custom-call(s32[2,8]{1,0:T(2,128)} %pad_add_fusion.2.range_ref, bf16[64,2048]{1,0:T(8,128)(2,1)} %get-tuple-element.37.q_ref, bf16[4096,128]{1,0:T(8,128)(2,1)} %get-tuple-element.38.kv_ref, s32[1,2048]{1,0:T(1,128)} %bitcast.235, ...), custom_call_target="tpu_custom_call" | custom-call | tf_op jit(solution)/shard_map/attend/pallas_call | solution.py:374
  166.7 16.6 %swap_heads.2 = bf16[512,256]{1,0:T(8,128)(2,1)} custom-call(bf16[64,2048]{1,0:T(8,128)(2,1)} %get-tuple-element.39.in_ref), custom_call_target="tpu_custom_call" | custom-call | tf_op jit(solution)/shard_map/swap_heads/pallas_call | solution.py:257
  185.7 2.6 convolution_add_fusion
  191.7 3.5 fusion.182
  201.7 10.1 %swap_heads.3.do_ref = bf16[64,2048]{1,0:T(8,128)(2,1)} custom-call(bf16[512,256]{1,0:T(8,128)(2,1)} %fusion.22.in_ref), custom_call_target="tpu_custom_call" | custom-call | tf_op jit(solution)/shard_map/swap_heads/pallas_call | solution.py:257
  211.8 20.9 %attend_back.1 = (bf16[64,2048]{1,0:T(8,128)(2,1)}, bf16[4096,128]{1,0:T(8,128)(2,1)}) custom-call(s32[2,8]{1,0:T(2,128)} %pad_add_fusion.2.range_ref, bf16[64,2048]{1,0:T(8,128)(2,1)} %get-tuple-element.37.q_ref, bf16[64,2048]{1,0:T(8,128)(2,1)} %swap_heads.3.do_ref, f32[64,2048]{1,0:T(8,128)} %get-tuple-element.40.o_ref, ...), custom_call_target="tpu_custom_call" | custom-call | tf_op jit(solution)/shard_map/attend_back/pallas_call | solution.py:444
  232.7 23.3 %collect_heads.1 = (bf16[512,256]{1,0:T(8,128)(2,1)}, bf16[2,256,1024]{2,1,0:T(8,128)(2,1)}) custom-call(bf16[64,2048]{1,0:T(8,128)(2,1)} %get-tuple-element.42.dq_ref, bf16[4096,128]{1,0:T(8,128)(2,1)} %get-tuple-element.43.dkv_ref), custom_call_target="tpu_custom_call" | custom-call | tf_op jit(solution)/shard_map/collect_heads/pallas_call | solution.py:304
  256.0 2.4 reduce_sum.482
  261.5 2.3 multiply_reduce_fusion.5
  275.4 4.0 fusion.18
  282.2 4.5 collective-permute-start.5
  287.1 3.8 fusion.27
  299.8 6.4 %multiply_reduce_fusion = (bf16[2048]{0:T(1024)(128)(2,1)S(1)}, f32[256]{0:T(256)S(1)}, f32[256]{0:T(256)S(1)}, bf16[2048]{0:T(1024)(128)(2,1)S(1)}, f32[256,2048]{1,0:T(8,128)S(1)}) fusion(f32[256,2048]{1,0:T(8,128)S(1)} %get-tuple-element.90, f32[256]{0:T(256)S(1)} %copy-done.93, f32[256]{0:T(256)S(1)} %copy-done.67, f32[2048]{0:T(1024)S(1)} %convert_element_type.552, ...), kind=kLoop, calls=%fused_computation.48 | loop fusion | flops 39841280 | bytes 5372160 | tf_op jit(solution)/shard_map/reduce_sum | solution.py:74
  310.2 5.5 %collective-permute-start.7 = (bf16[1,256]{1,0:T(2,128)(2,1)S(1)}, bf16[1,256]{1,0:T(2,128)(2,1)S(1)}, u32[]{:S(2)}, u32[]{:S(2)}) collective-permute-start(bf16[1,256]{1,0:T(2,128)(2,1)S(1)} %get-tuple-element.161), channel_id=1, source_target_pairs={{0,2},{2,4},{4,6},{6,8},{8,10},{10,12},{12,14},{14,16},{16,18},{18... | collective-permute-start | bytes 1544 | tf_op jit(solution)/shard_map/ppermute | solution.py:23
  334.9 5.2 %pad_maximum_fusion.g_ref = bf16[2,256,11264]{2,1,0:T(8,128)(2,1)} fusion(bf16[1,256,11264]{2,1,0:T(8,128)(2,1)S(1)} %bitcast.222, bf16[1,256,11264]{2,1,0:T(8,128)(2,1)S(1)} %bitcast.221), kind=kLoop, calls=%fused_computation | loop fusion | flops 5767168 | bytes 23068672 | tf_op jit(solution)/shard_map/stack | solution.py:637
  340.2 131.3 %reduce_grads.1 = bf16[256,11264]{1,0:T(8,128)(2,1)} custom-call(bf16[2,256,11264]{2,1,0:T(8,128)(2,1)} %pad_maximum_fusion.g_ref), custom_call_target="tpu_custom_call" | custom-call | tf_op jit(solution)/shard_map/reduce_grads/pallas_call | solution.py:584
  477.6 2.4 slice_convert_fusion.3
  480.0 2.5 slice_convert_fusion.2
  483.4 2.6 slice_convert_fusion
  (651 shorter events, 130.2 us)
Async XLA Ops:
  7.2 47.5 %all-gather.20.cloned.1.call-start = ((), (), s32[]{:S(2)}) async-start(), calls=%async_computation | async-start | bytes 1572864 | tf_op jit(solution)/shard_map/all_gather | solution.py:725
  9.5 56.2 %all-gather.22.cloned.1.call-start = ((), (), s32[]{:S(2)}) async-start(), calls=%async_computation.1 | async-start | bytes 3145728 | tf_op jit(solution)/shard_map/all_gather | solution.py:729
  10.7 90.1 %all-gather.24.cloned.1.call-start = ((), (), s32[]{:S(2)}) async-start(), calls=%async_computation.2 | async-start | bytes 1572864 | tf_op jit(solution)/shard_map/all_gather | solution.py:736
  11.8 91.4 %all-gather.26.cloned.1.call-start = ((), (), s32[]{:S(2)}) async-start(), calls=%async_computation.3 | async-start | bytes 2359296 | tf_op jit(solution)/shard_map/all_gather | solution.py:740
  14.4 171.2 %all-gather.28.cloned.1.call-start = ((), (), s32[]{:S(2)}) async-start(), calls=%async_computation.4 | async-start | bytes 3145728 | tf_op jit(solution)/shard_map/all_gather | solution.py:745
  15.8 176.0 %all-gather.30.cloned.1.call-start = ((), (), s32[]{:S(2)}) async-start(), calls=%async_computation.5 | async-start | bytes 3145728 | tf_op jit(solution)/shard_map/all_gather | solution.py:747
  49.1 45.1 %copy-start.49 = (f32[1,2048]{1,0:T(1,128)}, f32[1,2048]{1,0:T(1,128)S(1)}, u32[]{:S(2)}) copy-start(f32[1,2048]{1,0:T(1,128)S(1)} %get-tuple-element.180) | copy-start | bytes 24580
  49.1 45.1 %copy-start.51 = (f32[1,2048]{1,0:T(1,128)}, f32[1,2048]{1,0:T(1,128)S(1)}, u32[]{:S(2)}) copy-start(f32[1,2048]{1,0:T(1,128)S(1)} %get-tuple-element.181) | copy-start | bytes 24580
  49.1 45.1 %copy-start.53 = (f32[1,2048]{1,0:T(1,128)}, f32[1,2048]{1,0:T(1,128)S(1)}, u32[]{:S(2)}) copy-start(f32[1,2048]{1,0:T(1,128)S(1)} %get-tuple-element.182) | copy-start | bytes 24580
  49.1 45.1 %copy-start.55 = (f32[1,2048]{1,0:T(1,128)}, f32[1,2048]{1,0:T(1,128)S(1)}, u32[]{:S(2)}) copy-start(f32[1,2048]{1,0:T(1,128)S(1)} %get-tuple-element.183) | copy-start | bytes 24580
  49.1 45.1 %copy-start.57 = (f32[1,2048]{1,0:T(1,128)}, f32[1,2048]{1,0:T(1,128)S(1)}, u32[]{:S(2)}) copy-start(f32[1,2048]{1,0:T(1,128)S(1)} %get-tuple-element.184) | copy-start | bytes 24580
  49.1 45.1 %copy-start.59 = (f32[1,2048]{1,0:T(1,128)}, f32[1,2048]{1,0:T(1,128)S(1)}, u32[]{:S(2)}) copy-start(f32[1,2048]{1,0:T(1,128)S(1)} %get-tuple-element.185) | copy-start | bytes 24580
  49.1 45.1 %copy-start.61 = (f32[1,2048]{1,0:T(1,128)}, f32[1,2048]{1,0:T(1,128)S(1)}, u32[]{:S(2)}) copy-start(f32[1,2048]{1,0:T(1,128)S(1)} %get-tuple-element.186) | copy-start | bytes 24580
  49.2 45.1 %copy-start.63 = (f32[1,2048]{1,0:T(1,128)}, f32[1,2048]{1,0:T(1,128)S(1)}, u32[]{:S(2)}) copy-start(f32[1,2048]{1,0:T(1,128)S(1)} %get-tuple-element.187) | copy-start | bytes 24580
  54.3 40.0 %copy-start.94 = (pred[256]{0:T(512)(128)(4,1)}, pred[256]{0:T(512)(128)(4,1)S(1)}, u32[]{:S(2)}) copy-start(pred[256]{0:T(512)(128)(4,1)S(1)} %get-tuple-element.202) | copy-start | bytes 772
  54.3 40.0 %copy-start.97 = (pred[256]{0:T(512)(128)(4,1)}, pred[256]{0:T(512)(128)(4,1)S(1)}, u32[]{:S(2)}) copy-start(pred[256]{0:T(512)(128)(4,1)S(1)} %get-tuple-element.201) | copy-start | bytes 772
  54.3 40.0 %copy-start.111 = (pred[256]{0:T(512)(128)(4,1)}, pred[256]{0:T(512)(128)(4,1)S(1)}, u32[]{:S(2)}) copy-start(pred[256]{0:T(512)(128)(4,1)S(1)} %get-tuple-element.196) | copy-start | bytes 772
  54.3 40.0 %copy-start.114 = (pred[256]{0:T(512)(128)(4,1)}, pred[256]{0:T(512)(128)(4,1)S(1)}, u32[]{:S(2)}) copy-start(pred[256]{0:T(512)(128)(4,1)S(1)} %get-tuple-element.197) | copy-start | bytes 772
  54.3 40.0 %copy-start.117 = (pred[256]{0:T(512)(128)(4,1)}, pred[256]{0:T(512)(128)(4,1)S(1)}, u32[]{:S(2)}) copy-start(pred[256]{0:T(512)(128)(4,1)S(1)} %get-tuple-element.198) | copy-start | bytes 772
  54.3 40.0 %copy-start.120 = (pred[256]{0:T(512)(128)(4,1)}, pred[256]{0:T(512)(128)(4,1)S(1)}, u32[]{:S(2)}) copy-start(pred[256]{0:T(512)(128)(4,1)S(1)} %get-tuple-element.203) | copy-start | bytes 772
  54.4 40.0 %copy-start.123 = (pred[256]{0:T(512)(128)(4,1)}, pred[256]{0:T(512)(128)(4,1)S(1)}, u32[]{:S(2)}) copy-start(pred[256]{0:T(512)(128)(4,1)S(1)} %get-tuple-element.199) | copy-start | bytes 772
  54.4 40.0 %copy-start.126 = (pred[256]{0:T(512)(128)(4,1)}, pred[256]{0:T(512)(128)(4,1)S(1)}, u32[]{:S(2)}) copy-start(pred[256]{0:T(512)(128)(4,1)S(1)} %get-tuple-element.200) | copy-start | bytes 772
  54.4 40.0 %copy-start.129 = (pred[256]{0:T(512)(128)(4,1)}, pred[256]{0:T(512)(128)(4,1)S(1)}, u32[]{:S(2)}) copy-start(pred[256]{0:T(512)(128)(4,1)S(1)} %get-tuple-element.204) | copy-start | bytes 772
  57.2 7.4 %collective-permute-start.1 = (bf16[1,512]{1,0:T(2,128)(2,1)S(1)}, bf16[1,512]{1,0:T(2,128)(2,1)S(1)}, u32[]{:S(2)}, u32[]{:S(2)}) collective-permute-start(bf16[1,512]{1,0:T(2,128)(2,1)S(1)} %get-tuple-element.159), channel_id=1, source_target_pairs={{2,0},{4,2},{6,4},{8,6},{10,8},{12,10},{14,12},{16,14},{18,16},{20... | collective-permute-start | bytes 3080 | tf_op jit(solution)/shard_map/ppermute | solution.py:26
  58.5 5.8 %collective-permute-start = (bf16[1,512]{1,0:T(2,128)(2,1)S(1)}, bf16[1,512]{1,0:T(2,128)(2,1)S(1)}, u32[]{:S(2)}, u32[]{:S(2)}) collective-permute-start(bf16[1,512]{1,0:T(2,128)(2,1)S(1)} %get-tuple-element.160), channel_id=1, source_target_pairs={{0,2},{2,4},{4,6},{6,8},{8,10},{10,12},{12,14},{14,16},{16,18},{18... | collective-permute-start | bytes 3080 | tf_op jit(solution)/shard_map/ppermute | solution.py:23
  70.5 23.7 %collective-permute-start.3 = (bf16[4,2048]{1,0:T(4,128)(2,1)S(1)}, bf16[4,2048]{1,0:T(4,128)(2,1)S(1)}, u32[]{:S(2)}, u32[]{:S(2)}) collective-permute-start(bf16[4,2048]{1,0:T(4,128)(2,1)S(1)} %get-tuple-element.149), channel_id=1, source_target_pairs={{2,0},{4,2},{6,4},{8,6},{10,8},{12,10},{14,12},{16,14},{18,16},{20... | collective-permute-start | bytes 49160 | tf_op jit(solution)/shard_map/ppermute | solution.py:26
  71.8 22.4 %collective-permute-start.2 = (bf16[4,2048]{1,0:T(4,128)(2,1)S(1)}, bf16[4,2048]{1,0:T(4,128)(2,1)S(1)}, u32[]{:S(2)}, u32[]{:S(2)}) collective-permute-start(bf16[4,2048]{1,0:T(4,128)(2,1)S(1)} %get-tuple-element.150), channel_id=1, source_target_pairs={{0,2},{2,4},{4,6},{6,8},{8,10},{10,12},{12,14},{14,16},{16,18},{18... | collective-permute-start | bytes 49160 | tf_op jit(solution)/shard_map/ppermute | solution.py:23
  145.9 37.3 %copy-start.110 = (f32[2,1,256]{2,1,0:T(1,128)S(1)}, f32[2,1,256]{2,1,0:T(1,128)}, u32[]{:S(2)}) copy-start(f32[2,1,256]{2,1,0:T(1,128)} %convert_element_type.701) | copy-start | bytes 6148
  280.9 18.6 %collective-permute-start.4 = (bf16[4,2048]{1,0:T(4,128)(2,1)}, bf16[4,2048]{1,0:T(4,128)(2,1)S(1)}, u32[]{:S(2)}, u32[]{:S(2)}) collective-permute-start(bf16[4,2048]{1,0:T(4,128)(2,1)} %get-tuple-element.147), channel_id=1, source_target_pairs={{2,0},{4,2},{6,4},{8,6},{10,8},{12,10},{14,12},{16,14},{18,16},{20... | collective-permute-start | bytes 49160 | tf_op jit(solution)/shard_map/ppermute | solution.py:26
  282.2 17.3 %collective-permute-start.5 = (bf16[4,2048]{1,0:T(4,128)(2,1)}, bf16[4,2048]{1,0:T(4,128)(2,1)S(1)}, u32[]{:S(2)}, u32[]{:S(2)}) collective-permute-start(bf16[4,2048]{1,0:T(4,128)(2,1)} %get-tuple-element.148), channel_id=1, source_target_pairs={{0,2},{2,4},{4,6},{6,8},{8,10},{10,12},{12,14},{14,16},{16,18},{18... | collective-permute-start | bytes 49160 | tf_op jit(solution)/shard_map/ppermute | solution.py:23
  310.2 11.6 %collective-permute-start.7 = (bf16[1,256]{1,0:T(2,128)(2,1)S(1)}, bf16[1,256]{1,0:T(2,128)(2,1)S(1)}, u32[]{:S(2)}, u32[]{:S(2)}) collective-permute-start(bf16[1,256]{1,0:T(2,128)(2,1)S(1)} %get-tuple-element.161), channel_id=1, source_target_pairs={{0,2},{2,4},{4,6},{6,8},{8,10},{10,12},{12,14},{14,16},{16,18},{18... | collective-permute-start | bytes 1544 | tf_op jit(solution)/shard_map/ppermute | solution.py:23
  315.8 5.5 %collective-permute-start.6 = (bf16[1,256]{1,0:T(2,128)(2,1)S(1)}, bf16[1,256]{1,0:T(2,128)(2,1)S(1)}, u32[]{:S(2)}, u32[]{:S(2)}) collective-permute-start(bf16[1,256]{1,0:T(2,128)(2,1)S(1)} %get-tuple-element.162), channel_id=1, source_target_pairs={{2,0},{4,2},{6,4},{8,6},{10,8},{12,10},{14,12},{16,14},{18,16},{20... | collective-permute-start | bytes 1544 | tf_op jit(solution)/shard_map/ppermute | solution.py:26
  (156 other events, 1143.0 us)
Sparse Core Ops, SparseCore 0:
  10.2 11.7 all-gather.19
  24.1 11.7 all-gather.21
  38.0 10.1 all-gather.23
  50.2 10.9 all-gather.25
  63.1 11.7 all-gather.27
  76.9 11.7 all-gather.29

commit v2 on v0

v2 whole, which is shorter than its diff:
```python
import functools
import math

import jax
import jax.numpy as jnp
from jax import lax
from jax.experimental import pallas as pl
from jax.experimental.pallas import tpu as pltpu
from jax.sharding import PartitionSpec as P

MESH_ID = pl.DeviceIdType.MESH
F32 = jnp.float32
BF16 = jnp.bfloat16
HEAD_DIM = 64
NORM_EPS = 1e-06
MASK_FILL = -1e30
LANES = 128
ROW_BLOCK = 16
EDGE = 16
KEY_TILE = 512
BLOCK = 256
VMEM_MOST = 60 * 1024 * 1024

D = 512
FF = 2048
HALF = 256
TAPS = 9
REACH = 4

QKV, POINT, LEFT, CONV, GLU, SMALL, LATE = 0, 1536, 2560, 4608, 5376, 6400, 6656
ATTN, EXPAND, SHRINK, EARLY = 0, 512, 2560, 4608
WIDTH = LATE + EARLY

SMALL_ROWS = 32
SMALL_WIDTH = 1024
(LN1G, LN1B, GLUB, LN2G, LN2B, LEFTB, CONVB, LN3G, LN3B, DEPTH) = range(10)
(POINTB, LN4G, LN4B, ATTNB, LN5G, LN5B, EXPANDB, SHRINKB) = range(DEPTH + TAPS, DEPTH + TAPS + 8)


def vmem_spec():
    return pl.BlockSpec(memory_space=pltpu.VMEM)


def any_spec():
    return pl.BlockSpec(memory_space=pl.ANY)


def smem_spec():
    return pl.BlockSpec(memory_space=pltpu.SMEM)


def shaped(shape, kind=F32):
    return jax.ShapeDtypeStruct(shape, kind)


def comm_params(number):
    return pltpu.CompilerParams(
        collective_id=number, has_side_effects=True, vmem_limit_bytes=VMEM_MOST
    )


def greet(peers):
    barrier = pltpu.get_barrier_semaphore()
    for peer in peers:
        pl.semaphore_signal(barrier, inc=1, device_id=peer, device_id_type=MESH_ID)
    pl.semaphore_wait(barrier, len(peers))


def push(src, dst, sems, at, peer):
    copy = pltpu.make_async_remote_copy(
        src_ref=src,
        dst_ref=dst,
        send_sem=sems[0].at[at],
        recv_sem=sems[1].at[at],
        device_id=peer,
        device_id_type=MESH_ID,
    )
    copy.start()
    return copy


def move(src, dst, sem):
    copy = pltpu.make_async_copy(src, dst, sem)
    copy.start()
    return copy


def sem_pair(count):
    return [pltpu.SemaphoreType.DMA((count,)), pltpu.SemaphoreType.DMA((count,))]


def bound(value, step):
    return value if isinstance(value, int) else pl.multiple_of(value, step)


def span(value, step):
    return pl.ds(bound(value * step, step), step)


def matmul(left_op, right_op):
    return jnp.dot(left_op, right_op, preferred_element_type=F32)


def back_mul(grad_in, weight):
    return lax.dot_general(grad_in, weight, (((1,), (1,)), ((), ())), preferred_element_type=F32)


def turn(block):
    return block.astype(F32).T.astype(BF16)


def col_sum(block):
    return jnp.sum(block.astype(F32), axis=0, keepdims=True)


def lane_mean(block):
    return jnp.mean(block, axis=-1, keepdims=True)


def smooth_slope(block):
    sigma = jax.nn.sigmoid(block)
    return sigma * (1.0 + block * (1.0 - sigma))


def norm_fwd(block):
    centred = block - lane_mean(block)
    inv_std = lax.rsqrt(lane_mean(centred * centred) + NORM_EPS)
    return centred * inv_std, inv_std


def norm_back(grad_in, normed, inv_std, gain):
    scaled = grad_in * gain
    inner, cross = lane_mean(scaled), lane_mean(scaled * normed)
    return inv_std * (scaled - inner - normed * cross)


def vector(small_ref, row, size):
    half = size // 2
    return jnp.concatenate(
        [small_ref[core, row : row + 1, :half] for core in range(2)], axis=1
    )


def put_vector(small_ref, row, value):
    half = value.shape[1] // 2
    for core in range(2):
        small_ref[core, row : row + 1, :half] = value[:, core * half : (core + 1) * half]


def place():
    own, core = lax.axis_index("ctx"), lax.axis_index("ws")
    return own, core


def others_of(own, core, count):
    return [(lax.rem(own + gap, count), core) for gap in range(1, count)]


def widened(dst_ref, src_ref):
    @pl.loop(0, 2)
    def _(core):
        dst_ref[core] = src_ref[core].astype(BF16).astype(F32)


WEIGHT_COLUMNS = [
    (0, GLU, 1024, 1, False),
    (1, LEFT, 2048, 1, False),
    (2, CONV, 256, 3, False),
    (3, POINT, 256, 4, False),
    (4, QKV, 1536, 1, False),
    (5, ATTN, 512, 1, True),
    (6, EXPAND, 2048, 1, True),
    (7, SHRINK, 512, 4, True),
]


def tap_masks(mask_ref, seg_ref):
    seg = seg_ref[...]
    for tap in range(TAPS):
        moved = pltpu.roll(seg, (REACH - tap) % seg.shape[0], 0)
        mask_ref[tap] = jnp.where(moved == seg, 1.0, 0.0).astype(F32)


def first_body(
    count,
    heads,
    tok_ref,
    seg_row_ref,
    seg_col_ref,
    small_in,
    *refs,
):
    weights, refs = refs[:8], refs[8:]
    outs, refs = refs[:18], refs[18:]
    (
        late_out,
        early_out,
        small_out,
        seg_all,
        plan_out,
        q_out,
        kv_out,
        n1_out,
        glu_out,
        n2_out,
        left_out,
        conv_out,
        n3_out,
        depth_out,
        n4_out,
        x2_out,
        inv_out,
        masks_out,
    ) = outs
    (
        staged,
        late,
        early,
        edges,
        seg_edges,
        x_ext,
        seg_ext,
        masks,
        small,
        low_ext,
        n1,
        glu_pre,
        x1,
        n2,
        shifted,
        left_pre,
        conv_pre,
        n3,
        g3,
        depth,
        x2,
        n4,
        inv,
        q_turned,
        kv_own,
        load_sem,
        out_sem,
        ws_send,
        ws_recv,
        edge_send,
        edge_recv,
        row_send,
        row_recv,
        q_send,
        q_recv,
        kv_send,
        kv_recv,
    ) = refs
    own, core = place()
    parts = count // heads
    head, part = own // parts, lax.rem(own, parts)
    rows = tok_ref.shape[0]
    ext = rows + 2 * EDGE
    mid = slice(EDGE, EDGE + rows)
    sibling = (own, 1 - core)
    peers = others_of(own, core, count)

    loads, column = [], 0
    stage_at = []
    for number, first, width, blocks, _ in WEIGHT_COLUMNS:
        stage_at.append(column)
        for block in range(blocks):
            source = weights[number]
            if blocks == 3:
                source = source.at[block]
            elif blocks > 1:
                source = source.at[pl.ds(block * BLOCK, BLOCK), :]
            loads.append(
                move(
                    source,
                    staged.at[:, pl.ds(column, width)],
                    load_sem.at[len(loads)],
                )
            )
            column += width
    greet([sibling] + peers)

    copies = []
    right, left = (lax.rem(own + 1, count), core), (lax.rem(own + count - 1, count), core)
    edge_copies = [
        push(tok_ref.at[pl.ds(rows - EDGE, EDGE), :], edges.at[0], (edge_send, edge_recv), 0, right),
        push(tok_ref.at[pl.ds(0, EDGE), :], edges.at[1], (edge_send, edge_recv), 1, left),
        push(seg_col_ref.at[pl.ds(rows - EDGE, EDGE), :], seg_edges.at[0], (edge_send, edge_recv), 2, right),
        push(seg_col_ref.at[pl.ds(0, EDGE), :], seg_edges.at[1], (edge_send, edge_recv), 3, left),
    ]
    small_copy = push(small_in, small_out.at[core], (ws_send, ws_recv), len(WEIGHT_COLUMNS), sibling)
    small_out[core] = small_in[...]

    at, weight_copies = 0, []
    for (number, first, width, blocks, is_early), column in zip(WEIGHT_COLUMNS, stage_at):
        target = early if is_early else late
        for _ in range(blocks):
            loads[at].wait()
            at += 1
        size = width * blocks
        mine = pl.ds(bound(core * BLOCK, BLOCK), BLOCK)

        @pl.loop(0, BLOCK // ROW_BLOCK)
        def _(step):
            source = staged[span(step, ROW_BLOCK), pl.ds(column, size)]
            goes = pl.ds(bound(core * BLOCK + step * ROW_BLOCK, ROW_BLOCK), ROW_BLOCK)
            target[goes, pl.ds(first, size)] = source.astype(BF16)

        piece = target.at[mine, pl.ds(first, size)]
        weight_copies.append(push(piece, piece, (ws_send, ws_recv), number, sibling))

    for copy in edge_copies:
        copy.wait()
    small_copy.wait()
    row_copies = [
        push(seg_row_ref, seg_all.at[own], (row_send, row_recv), gap, peer)
        for gap, peer in enumerate(peers)
    ]
    seg_all[own] = seg_row_ref[...]
    widened(small, small_out)

    x_ext[:EDGE, :] = edges[0].astype(F32)
    x_ext[mid, :] = tok_ref[...].astype(F32)
    x_ext[EDGE + rows :, :] = edges[1].astype(F32)
    seg_ext[:EDGE, :] = jnp.where(own == 0, -1, seg_edges[0])
    seg_ext[mid, :] = seg_col_ref[...]
    seg_ext[EDGE + rows :, :] = jnp.where(own == count - 1, -1, seg_edges[1])
    tap_masks(masks, seg_ext)

    normed, inv_std = norm_fwd(x_ext[...])
    n1[...] = normed[mid, :]
    inv[0] = jnp.broadcast_to(inv_std, (ext, LANES))
    low_ext[...] = (normed * vector(small, LN1G, D) + vector(small, LN1B, D)).astype(BF16)

    weight_copies[0].wait()
    glu_bias = vector(small, GLUB, 2 * D)
    for step in range(2 * D // 512):
        cols = slice(512 * step, 512 * (step + 1))
        glu_pre[:, cols] = (
            matmul(low_ext[...], late[:, GLU + 512 * step : GLU + 512 * (step + 1)])
            + glu_bias[:, cols]
        )
    state = x_ext[...] + glu_pre[:, :D] * jax.nn.sigmoid(glu_pre[:, D:])
    x1[...] = state[mid, :]
    normed, inv_std = norm_fwd(state)
    n2[...] = normed[mid, :]
    inv[1] = jnp.broadcast_to(inv_std, (ext, LANES))
    low_f = (normed * vector(small, LN2G, D) + vector(small, LN2B, D)).astype(BF16).astype(F32)
    before = pltpu.roll(low_f, 1, 0) * jnp.concatenate([masks[REACH - 1]] * (D // LANES), axis=1)
    after = pltpu.roll(low_f, ext - 1, 0) * jnp.concatenate([masks[REACH + 1]] * (D // LANES), axis=1)
    shifted[0] = before.astype(BF16)
    shifted[1] = low_f.astype(BF16)
    shifted[2] = after.astype(BF16)

    weight_copies[1].wait()

    @pl.loop(0, FF // 512)
    def _(step):
        weight = late[:, pl.ds(bound(LEFT + step * 512, 512), 512)]
        left_pre[:, span(step, 512)] = matmul(shifted[1], weight)

    weight_copies[2].wait()
    conv_sum = vector(small, CONVB, HALF)
    for tap in range(3):
        conv_sum = conv_sum + matmul(
            shifted[tap], late[:, CONV + HALF * tap : CONV + HALF * (tap + 1)]
        )
    conv_pre[...] = conv_sum

    left_bias = vector(small, LEFTB, FF)
    gain, shift = vector(small, LN3G, FF), vector(small, LN3B, FF)

    @pl.loop(0, ext // ROW_BLOCK)
    def _(step):
        here = span(step, ROW_BLOCK)
        pre = left_pre[here, :] + left_bias
        left_pre[here, :] = pre
        mixed = jax.nn.silu(pre)
        mixed = jnp.concatenate(
            [mixed[:, :HALF] + jax.nn.silu(conv_pre[here, :]), mixed[:, HALF:]], axis=1
        )
        normed, inv_std = norm_fwd(mixed)
        n3[here, :] = normed
        inv[2, here, :] = jnp.broadcast_to(inv_std, (ROW_BLOCK, LANES))
        g3[here, :] = (normed * gain + shift).astype(BF16).astype(F32)

    saves = [
        move(n1, n1_out, out_sem.at[0]),
        move(glu_pre.at[pl.ds(EDGE, rows), :], glu_out, out_sem.at[1]),
        move(n2, n2_out, out_sem.at[2]),
        move(left_pre.at[pl.ds(EDGE, rows), :], left_out, out_sem.at[3]),
        move(conv_pre, conv_out, out_sem.at[4]),
        move(n3, n3_out, out_sem.at[5]),
    ]

    @pl.loop(0, FF // LANES)
    def _(step):
        cols = span(step, LANES)
        block = g3[:, cols]
        total = jnp.zeros((rows, LANES), F32)
        for tap in range(TAPS):
            row = DEPTH + tap
            moved = pltpu.roll(block, (REACH - tap) % ext, 0)[mid, :]
            half = FF // 2 // LANES
            taps = small[step // half, row : row + 1, span(lax.rem(step, half), LANES)]
            total = total + moved * masks[tap, mid, :] * taps
        depth[:, cols] = total.astype(BF16)

    saves.append(move(depth, depth_out, out_sem.at[6]))
    weight_copies[3].wait()
    sep = vector(small, POINTB, HALF)
    for side in range(2):
        for block in range(4):
            first = side * (FF // 2) + block * BLOCK
            sep = sep + matmul(
                depth[:, first : first + BLOCK],
                late[side * BLOCK : (side + 1) * BLOCK, POINT + HALF * block : POINT + HALF * (block + 1)],
            )
    state = jnp.concatenate([x1[:, :HALF] + sep, x1[:, HALF:]], axis=1)
    x2[...] = state
    normed, inv_std = norm_fwd(state)
    n4[...] = normed
    inv[3, :rows, :] = jnp.broadcast_to(inv_std, (rows, LANES))
    low = (normed * vector(small, LN4G, D) + vector(small, LN4B, D)).astype(BF16)
    weight_copies[4].wait()
    for step in range(D // 256):
        cols = slice(256 * step, 256 * (step + 1))
        query = matmul(low, late[:, QKV + 256 * step : QKV + 256 * (step + 1)])
        q_turned[cols, :] = turn(query)
    near = lax.broadcasted_iota(jnp.int32, (rows, LANES), 1) < HEAD_DIM
    for step in range(D // LANES):
        first = QKV + D + LANES * step
        keys = matmul(low, late[:, first : first + LANES])
        values = matmul(low, late[:, first + D : first + D + LANES])
        kv_own[:, 2 * step * LANES : (2 * step + 1) * LANES] = jnp.where(
            near, keys, pltpu.roll(values, HEAD_DIM, 1)
        ).astype(BF16)
        kv_own[:, (2 * step + 1) * LANES : (2 * step + 2) * LANES] = jnp.where(
            near, pltpu.roll(keys, HEAD_DIM, 1), values
        ).astype(BF16)

    q_slot = q_out.at[:, span(head, rows)]
    kv_slot = kv_out.at[span(own, rows), :]
    for gap, (peer, _) in enumerate(peers):
        copies.append(
            push(kv_own.at[:, span(peer // parts, LANES)], kv_slot, (kv_send, kv_recv), gap, (peer, core))
        )
    for gap in range(1, heads):
        other = lax.rem(head + gap, heads)
        copies.append(
            push(q_turned.at[span(other, HEAD_DIM), :], q_slot, (q_send, q_recv), gap - 1, (other * parts + part, core))
        )
    saves.append(move(q_turned.at[span(head, HEAD_DIM), :], q_slot, out_sem.at[7]))
    saves.append(move(kv_own.at[:, span(head, LANES)], kv_slot, out_sem.at[8]))
    saves.append(move(n4, n4_out, out_sem.at[9]))
    saves.append(move(x2, x2_out, out_sem.at[10]))
    saves.append(move(inv, inv_out, out_sem.at[11]))
    saves.append(move(masks, masks_out, out_sem.at[14]))
    for copy in weight_copies[5:]:
        copy.wait()
    saves.append(move(late, late_out, out_sem.at[12]))
    saves.append(move(early, early_out, out_sem.at[13]))

    for copy in row_copies:
        copy.wait()
    lane = lax.broadcasted_iota(jnp.int32, (1, LANES), 1)
    every = seg_all[:, 0, :]
    for tile in range(heads):
        source = tile * parts + part
        mine = seg_all[source]
        first = jnp.min(mine, axis=1, keepdims=True)
        last = jnp.max(mine, axis=1, keepdims=True)
        below = jnp.sum(jnp.sum((every < first).astype(F32), axis=0, keepdims=True), axis=1, keepdims=True).astype(jnp.int32)
        upto = jnp.sum(jnp.sum((every <= last).astype(F32), axis=0, keepdims=True), axis=1, keepdims=True).astype(jnp.int32)
        plan_out[tile : tile + 1, :] = jnp.where(
            lane == 0, below, jnp.where(lane == 1, upto, source)
        )
    for copy in copies + saves:
        copy.wait()


def first_kernel(tokens, seg_row, seg_col, small, weights, count, heads):
    rows = tokens.shape[0]
    ext = rows + 2 * EDGE
    late = (2 * BLOCK, SMALL)
    early = (2 * BLOCK, EARLY)
    out_shape = (
        shaped(late, BF16),
        shaped(early, BF16),
        shaped((2, SMALL_ROWS, SMALL_WIDTH)),
        shaped((count, 1, rows), jnp.int32),
        shaped((heads, LANES), jnp.int32),
        shaped((HEAD_DIM, heads * rows), BF16),
        shaped((count * rows, LANES), BF16),
        shaped((rows, D)),
        shaped((rows, 2 * D)),
        shaped((rows, D)),
        shaped((rows, FF)),
        shaped((ext, HALF)),
        shaped((ext, FF)),
        shaped((rows, FF), BF16),
        shaped((rows, D)),
        shaped((rows, D)),
        shaped((4, ext, LANES)),
        shaped((TAPS, ext, LANES)),
    )
    out_specs = (
        [any_spec()] * 2 + [vmem_spec()] * 3 + [any_spec()] * 13
    )
    scratch = [
        pltpu.VMEM((BLOCK, SMALL + EARLY), F32),
        pltpu.VMEM(late, BF16),
        pltpu.VMEM(early, BF16),
        pltpu.VMEM((2, EDGE, D), BF16),
        pltpu.VMEM((2, EDGE, LANES), jnp.int32),
        pltpu.VMEM((ext, D), F32),
        pltpu.VMEM((ext, LANES), jnp.int32),
        pltpu.VMEM((TAPS, ext, LANES), F32),
        pltpu.VMEM((2, SMALL_ROWS, SMALL_WIDTH), F32),
        pltpu.VMEM((ext, D), BF16),
        pltpu.VMEM((rows, D), F32),
        pltpu.VMEM((ext, 2 * D), F32),
        pltpu.VMEM((rows, D), F32),
        pltpu.VMEM((rows, D), F32),
        pltpu.VMEM((3, ext, D), BF16),
        pltpu.VMEM((ext, FF), F32),
        pltpu.VMEM((ext, HALF), F32),
        pltpu.VMEM((ext, FF), F32),
        pltpu.VMEM((ext, FF), F32),
        pltpu.VMEM((rows, FF), BF16),
        pltpu.VMEM((rows, D), F32),
        pltpu.VMEM((rows, D), F32),
        pltpu.VMEM((4, ext, LANES), F32),
        pltpu.VMEM((D, rows), BF16),
        pltpu.VMEM((rows, 2 * D), BF16),
        pltpu.SemaphoreType.DMA((sum(item[3] for item in WEIGHT_COLUMNS),)),
        pltpu.SemaphoreType.DMA((15,)),
    ]
    scratch += sem_pair(len(WEIGHT_COLUMNS) + 1) + sem_pair(4) + sem_pair(count - 1)
    scratch += sem_pair(heads - 1) + sem_pair(count - 1)
    return pl.pallas_call(
        functools.partial(first_body, count, heads),
        out_shape=out_shape,
        in_specs=[vmem_spec()] * 4 + [any_spec()] * 8,
        out_specs=out_specs,
        scratch_shapes=scratch,
        compiler_params=comm_params(1),
        name="first_layers",
    )(tokens, seg_row, seg_col, small, *weights)


def turn_keys(kv_ref, turned):
    @pl.loop(0, kv_ref.shape[0] // KEY_TILE)
    def _(tile):
        here = span(tile, KEY_TILE)
        turned[:, here] = turn(kv_ref[here, :])


def key_segments(seg_ref, segk):
    count, _, rows = seg_ref.shape

    @pl.loop(0, count)
    def _(source):
        for step in range(rows // LANES):
            row = seg_ref[source, :, step * LANES : (step + 1) * LANES].astype(F32)
            column = jnp.broadcast_to(row, (LANES, LANES)).T
            segk[pl.ds(bound(source * rows + step * LANES, LANES), LANES), :] = column


def masked(scores, segk, here, seg_q):
    seg_k = jnp.concatenate([segk[here, :]] * (scores.shape[1] // LANES), axis=1)
    return jnp.where(seg_k == seg_q, scores, MASK_FILL)


def key_tiles(plan_ref, tile):
    return plan_ref[tile, 0] // KEY_TILE, (plan_ref[tile, 1] + KEY_TILE - 1) // KEY_TILE


def attend_body(rows, plan_ref, q_ref, kv_ref, seg_ref, o_ref, low_ref, lse_ref, turned, segk):
    turn_keys(kv_ref, turned)
    key_segments(seg_ref, segk)

    @pl.loop(0, q_ref.shape[1] // rows)
    def _(tile):
        at = span(tile, rows)
        q = q_ref[:, at] * jnp.bfloat16(HEAD_DIM**-0.5)
        q_pad = jnp.concatenate([q, jnp.zeros_like(q)], axis=0)
        seg_q = seg_ref[plan_ref[tile, 2]].astype(F32)

        def block(key_tile, carry):
            top, total, acc = carry
            here = span(key_tile, KEY_TILE)
            scores = masked(matmul(kv_ref[here, :], q_pad), segk, here, seg_q)
            new_top = jnp.maximum(top, jnp.max(scores, axis=0, keepdims=True))
            probs = jnp.exp(scores - new_top)
            shrink = jnp.exp(top - new_top)
            total = total * shrink + jnp.sum(probs, axis=0, keepdims=True)
            acc = acc * shrink + matmul(turned[HEAD_DIM:, here], probs.astype(BF16))
            return (new_top, total, acc)

        first, end = key_tiles(plan_ref, tile)
        top, total, acc = lax.fori_loop(
            first,
            end,
            block,
            (
                jnp.full((1, rows), MASK_FILL, F32),
                jnp.zeros((1, rows), F32),
                jnp.zeros((HEAD_DIM, rows), F32),
            ),
        )
        out = acc / total
        o_ref[:, at] = out
        low_ref[:, at] = out.astype(BF16)
        lse_ref[:, at] = top + jnp.log(total)


def attend(plan, q_t, kv, seg, rows):
    return pl.pallas_call(
        functools.partial(attend_body, rows),
        out_shape=(shaped(q_t.shape), shaped(q_t.shape, BF16), shaped((1, q_t.shape[1]))),
        in_specs=[smem_spec()] + [vmem_spec()] * 3,
        out_specs=(vmem_spec(),) * 3,
        scratch_shapes=[pltpu.VMEM(kv.shape[::-1], BF16), pltpu.VMEM(kv.shape, F32)],
        compiler_params=pltpu.CompilerParams(vmem_limit_bytes=VMEM_MOST),
        name="attend",
    )(plan, q_t, kv, seg)


def attend_back_body(
    rows, plan_ref, q_ref, do_ref, o_ref, lse_ref, kv_ref, seg_ref, dq_ref, dkv_ref, turned, segk, dkv_acc
):
    turn_keys(kv_ref, turned)
    key_segments(seg_ref, segk)
    dkv_acc[...] = jnp.zeros_like(dkv_acc)
    scale = HEAD_DIM**-0.5

    @pl.loop(0, q_ref.shape[1] // rows)
    def _(tile):
        at = span(tile, rows)
        q = q_ref[:, at] * jnp.bfloat16(scale)
        do = do_ref[:, at]
        none = jnp.zeros_like(q)
        both = jnp.concatenate(
            [jnp.concatenate([q, none], axis=1), jnp.concatenate([none, do], axis=1)], axis=0
        )
        delta = jnp.sum(o_ref[:, at] * do.astype(F32), axis=0, keepdims=True)
        lse = lse_ref[:, at]
        seg_q = seg_ref[plan_ref[tile, 2]].astype(F32)

        def block(key_tile, dq):
            here = span(key_tile, KEY_TILE)
            pair = matmul(kv_ref[here, :], both)
            probs = jnp.exp(masked(pair[:, :rows], segk, here, seg_q) - lse)
            score_grad = (probs * (pair[:, rows:] - delta)).astype(BF16)
            joined = jnp.concatenate([score_grad, probs.astype(BF16)], axis=1)
            dkv_acc[here, :] += back_mul(joined, both)
            return dq + matmul(turned[:HEAD_DIM, here], score_grad)

        first, end = key_tiles(plan_ref, tile)
        dq = lax.fori_loop(first, end, block, jnp.zeros((HEAD_DIM, rows), F32))
        dq_ref[:, at] = (dq * scale).astype(BF16)

    dkv_ref[...] = dkv_acc[...].astype(BF16)


def attend_back(plan, q_t, do_t, o_t, lse, kv, seg, rows):
    return pl.pallas_call(
        functools.partial(attend_back_body, rows),
        out_shape=(shaped(q_t.shape, BF16), shaped(kv.shape, BF16)),
        in_specs=[smem_spec()] + [vmem_spec()] * 6,
        out_specs=(vmem_spec(),) * 2,
        scratch_shapes=[
            pltpu.VMEM(kv.shape[::-1], BF16),
            pltpu.VMEM(kv.shape, F32),
            pltpu.VMEM(kv.shape, F32),
        ],
        compiler_params=pltpu.CompilerParams(vmem_limit_bytes=VMEM_MOST),
        name="attend_back",
    )(plan, q_t, do_t, o_t, lse, kv, seg)


def middle_body(
    count,
    heads,
    o_in,
    out_grad,
    small_in,
    x2_in,
    early_in,
    out_ref,
    small_grads,
    dx3_out,
    grads_out,
    do_out,
    weights,
    x2,
    small,
    o_t,
    x3,
    expand_pre,
    hidden,
    dpre,
    do_t,
    grads,
    dx3,
    load_sem,
    o_send,
    o_recv,
    do_send,
    do_recv,
):
    own, core = place()
    parts = count // heads
    head, part = own // parts, lax.rem(own, parts)
    rows = out_grad.shape[0]
    loads = [move(early_in, weights, load_sem.at[0]), move(x2_in, x2, load_sem.at[1])]
    near = [lax.rem(head + gap, heads) for gap in range(1, heads)]
    peers = [(other * parts + part, core) for other in near]
    greet(peers)
    copies = [
        push(o_in.at[:, span(other, rows)], o_t.at[span(head, HEAD_DIM), :], (o_send, o_recv), gap, peer)
        for gap, (other, peer) in enumerate(zip(near, peers))
    ]
    copies.append(move(o_in.at[:, span(head, rows)], o_t.at[span(head, HEAD_DIM), :], load_sem.at[2]))
    widened(small, small_in)
    small_grads[...] = jnp.zeros_like(small_grads)
    for copy in copies + loads:
        copy.wait()

    state = (
        x2[...]
        + matmul(turn(o_t[...]), weights[:, ATTN : ATTN + D])
        + vector(small, ATTNB, D)
    )
    x3[...] = state
    normed, inv_std = norm_fwd(state)
    gain = vector(small, LN5G, D)
    low = (normed * gain + vector(small, LN5B, D)).astype(BF16)
    expand_bias = vector(small, EXPANDB, FF)
    for step in range(FF // 512):
        cols = slice(512 * step, 512 * (step + 1))
        pre = matmul(low, weights[:, EXPAND + 512 * step : EXPAND + 512 * (step + 1)]) + expand_bias[:, cols]
        expand_pre[:, cols] = pre
        hidden[:, cols] = jax.nn.silu(pre).astype(BF16)
    state = x3[...] + vector(small, SHRINKB, D)
    for block in range(FF // BLOCK):
        side, column = block // 4, SHRINK + D * (block % 4)
        state = state + matmul(
            hidden[:, block * BLOCK : (block + 1) * BLOCK],
            weights[side * BLOCK : (side + 1) * BLOCK, column : column + D],
        )
    out_ref[...] = state.astype(BF16)

    dz = out_grad[...]
    for block in range(FF // BLOCK):
        side, column = block // 4, SHRINK + D * (block % 4)
        cols = slice(block * BLOCK, (block + 1) * BLOCK)
        grad = back_mul(dz, weights[side * BLOCK : (side + 1) * BLOCK, column : column + D])
        dpre[:, cols] = (grad * smooth_slope(expand_pre[:, cols])).astype(BF16)
    grad = jnp.concatenate(
        [
            back_mul(dpre[...], weights[side * BLOCK : (side + 1) * BLOCK, EXPAND : EXPAND + FF])
            for side in range(2)
        ],
        axis=1,
    )
    state = dz.astype(F32) + norm_back(grad, normed, inv_std, gain)
    dx3[...] = state
    dy3 = state.astype(BF16)
    do_t[...] = back_mul(weights[:, ATTN : ATTN + D], dy3).astype(BF16)
    slot = do_out.at[:, span(head, rows)]
    copies = [
        push(do_t.at[span(other, HEAD_DIM), :], slot, (do_send, do_recv), gap, peer)
        for gap, (other, peer) in enumerate(zip(near, peers))
    ]
    copies.append(move(do_t.at[span(head, HEAD_DIM), :], slot, load_sem.at[0]))
    copies.append(move(dx3, dx3_out, load_sem.at[1]))

    put_vector(small_grads, LN5G, col_sum(grad * normed))
    put_vector(small_grads, LN5B, col_sum(grad))
    put_vector(small_grads, ATTNB, col_sum(dy3))
    put_vector(small_grads, EXPANDB, col_sum(dpre[...]))
    put_vector(small_grads, SHRINKB, col_sum(dz))
    grads[:, ATTN : ATTN + D] = matmul(o_t[...], dy3).astype(BF16)
    low_t = turn(low)
    for step in range(FF // 512):
        grads[:, EXPAND + 512 * step : EXPAND + 512 * (step + 1)] = matmul(
            low_t, dpre[:, 512 * step : 512 * (step + 1)]
        ).astype(BF16)
    for block in range(FF // BLOCK):
        side, column = block // 4, SHRINK + D * (block % 4)
        grads[side * BLOCK : (side + 1) * BLOCK, column : column + D] = matmul(
            turn(hidden[:, block * BLOCK : (block + 1) * BLOCK]), dz
        ).astype(BF16)
    copies.append(move(grads, grads_out, load_sem.at[2]))
    for copy in copies:
        copy.wait()


def middle_kernel(o_low, out_grad, small, x2, early, count, heads):
    rows = out_grad.shape[0]
    return pl.pallas_call(
        functools.partial(middle_body, count, heads),
        out_shape=(
            shaped((rows, D), BF16),
            shaped((2, SMALL_ROWS, SMALL_WIDTH)),
            shaped((rows, D)),
            shaped(early.shape, BF16),
            shaped((HEAD_DIM, heads * rows), BF16),
        ),
        in_specs=[vmem_spec()] * 3 + [any_spec()] * 2,
        out_specs=[vmem_spec()] * 2 + [any_spec()] * 3,
        scratch_shapes=[
            pltpu.VMEM(early.shape, BF16),
            pltpu.VMEM((rows, D), F32),
            pltpu.VMEM((2, SMALL_ROWS, SMALL_WIDTH), F32),
            pltpu.VMEM((D, rows), BF16),
            pltpu.VMEM((rows, D), F32),
            pltpu.VMEM((rows, FF), F32),
            pltpu.VMEM((rows, FF), BF16),
            pltpu.VMEM((rows, FF), BF16),
            pltpu.VMEM((D, rows), BF16),
            pltpu.VMEM(early.shape, BF16),
            pltpu.VMEM((rows, D), F32),
            pltpu.SemaphoreType.DMA((3,)),
        ]
        + sem_pair(heads - 1)
        + sem_pair(heads - 1),
        compiler_params=comm_params(2),
        name="middle_layers",
    )(o_low, out_grad, small, x2, early)


def column_groups(first, width, bits):
    tiles = width // LANES
    unit = 2 ** max(0, bits - 4)
    long = max(1, round(tiles * 0.36 / unit)) * unit
    orders = [
        list(range(bits)),
        [1, 0] + list(range(2, bits)),
        list(range(2, bits)) + [0, 1],
    ]
    groups = []
    for size, order in zip([long, long, tiles - 2 * long], orders):
        groups.append((first, size * LANES, order))
        first += size * LANES
    return groups


def grad_sets(bits):
    bounds = [LATE, QKV, LEFT, CONV]
    widths = [EARLY, LEFT - QKV, CONV - LEFT, LATE - CONV]
    return [column_groups(first, width, bits) for first, width in zip(bounds, widths)]


class Piece:
    def __init__(self, at, group, links, sums, got, total, sems):
        self.at, (self.first, self.width, self.order) = at, group
        self.core, self.sibling, self.bit_of, self.partner = links
        self.view, self.got, self.total, self.sems = sums, got, total, sems
        self.bits, self.phase, self.trail = len(self.order), 0, []
        self.copy = None

    def whole(self):
        return (0, BLOCK, self.first, self.width)

    def out(self, where):
        row, tall, col, wide = where
        return self.total.at[pl.ds(bound(row, ROW_BLOCK), tall), pl.ds(bound(col, LANES), wide)]

    def start(self, other_half):
        self.copy = push(other_half, self.out(self.whole()), self.sems[0], self.at, self.sibling)

    def add(self, where, source, spot, last):
        row, tall, col, wide = where

        @pl.loop(0, tall // ROW_BLOCK)
        def _(step):
            gap = step * ROW_BLOCK
            here = (row + gap, ROW_BLOCK, col, wide)
            there = source.at[pl.ds(bound(spot + gap, ROW_BLOCK), ROW_BLOCK), pl.ds(self.first, wide)]
            mine = self.view(here)[...].astype(F32)
            added = (mine + there[...].astype(F32)).astype(BF16)
            if last:
                self.out(here)[...] = added
            else:
                self.view(here)[...] = added

    def halve(self, step):
        row, tall, col, wide = self.where
        bit = self.order[step]
        mine = self.bit_of[bit]
        if tall > ROW_BLOCK:
            half = tall // 2
            kept = (row + half * mine, half, col, wide)
            sent = (row + half * (1 - mine), half, col, wide)
        else:
            half = wide // 2
            kept = (row, tall, col + half * mine, half)
            sent = (row, tall, col + half * (1 - mine), half)
        self.copy = push(
            self.view(sent),
            self.got.at[pl.ds(self.spot, sent[1]), pl.ds(self.first, sent[3])],
            self.sems[1],
            self.at * self.bits + step,
            self.partner[bit],
        )
        self.where = kept

    def double(self, step):
        place_out = self.out(self.trail[step])
        self.copy = push(
            place_out,
            place_out,
            self.sems[2],
            self.at * self.bits + step,
            self.partner[self.order[step]],
        )

    def done(self):
        return self.phase > 2 * self.bits

    def advance(self):
        if self.done():
            return
        self.copy.wait()
        if self.phase == 0:
            self.where, self.spot = self.whole(), 0
            self.add(self.where, self.total, 0, False)
            self.halve(0)
        elif self.phase <= self.bits:
            last = self.phase == self.bits
            self.add(self.where, self.got, self.spot, last)
            self.trail.append(self.where)
            self.spot += self.where[1]
            if last:
                self.double(self.bits - 1)
            else:
                self.halve(self.phase)
        elif self.phase < 2 * self.bits:
            self.double(2 * self.bits - 1 - self.phase)
        self.phase += 1


def last_body(count, heads, dq_in, dkv_in, small_in, small_grads_in, *refs):
    (
        early_grads,
        dx3_in,
        late_in,
        n1_in,
        glu_in,
        n2_in,
        left_in,
        conv_in,
        n3_in,
        depth_in,
        n4_in,
        inv_in,
        masks_in,
        total,
        grad_out,
        weights,
        dx3,
        n1,
        glu_pre,
        n2,
        left_pre,
        conv_pre,
        n3,
        depth,
        n4,
        inv,
        masks,
        small,
        small_grads,
        dq_t,
        dkv_parts,
        dqkv,
        sep_own,
        sep_edges,
        sep_ext,
        depth_grad,
        g3_grad,
        row_sums,
        dleft,
        conv_grad,
        conv_taps,
        grads,
        early_own,
        got,
        result,
        load_sem,
        keep_sem,
        dq_send,
        dq_recv,
        dkv_send,
        dkv_recv,
        edge_send,
        edge_recv,
        ws_send,
        ws_recv,
        rs_send,
        rs_recv,
        ag_send,
        ag_recv,
    ) = refs
    own, core = place()
    parts = count // heads
    head, part = own // parts, lax.rem(own, parts)
    rows = dx3.shape[0]
    ext = rows + 2 * EDGE
    mid = slice(EDGE, EDGE + rows)
    sibling = (own, 1 - core)
    peers = others_of(own, core, count)
    bits = count.bit_length() - 1

    sources = (dx3_in, late_in, n4_in, inv_in, depth_in, masks_in, n3_in, left_in, conv_in, n2_in, glu_in, n1_in)
    targets = (dx3, weights, n4, inv, depth, masks, n3, left_pre, conv_pre, n2, glu_pre, n1)
    loads = [move(a, b, load_sem.at[at]) for at, (a, b) in enumerate(zip(sources, targets))]
    greet([sibling] + peers)

    slot = dq_t.at[span(head, HEAD_DIM), :]
    kv_slot = dkv_parts.at[part, :, span(head, LANES)]
    collect = []
    for gap, (peer, _) in enumerate(peers):
        collect.append(push(dkv_in.at[span(peer, rows), :], kv_slot, (dkv_send, dkv_recv), gap, (peer, core)))
    for gap in range(1, heads):
        other = lax.rem(head + gap, heads)
        collect.append(
            push(dq_in.at[:, span(other, rows)], slot, (dq_send, dq_recv), gap - 1, (other * parts + part, core))
        )
    collect.append(move(dq_in.at[:, span(head, rows)], slot, keep_sem.at[0]))
    collect.append(move(dkv_in.at[span(own, rows), :], kv_slot, keep_sem.at[1]))

    bit_of = [lax.rem(own // 2**bit, 2) for bit in range(bits)]
    partner = [(own + 2**bit - 2 * 2**bit * bit_of[bit], core) for bit in range(bits)]
    links = (core, sibling, bit_of, partner)
    sems = ((ws_send, ws_recv), (rs_send, rs_recv), (ag_send, ag_recv))

    def early_view(where):
        row, tall, col, wide = where
        return early_own.at[pl.ds(bound(row, ROW_BLOCK), tall), pl.ds(bound(col - LATE, LANES), wide)]

    def late_view(where):
        row, tall, col, wide = where
        return grads.at[pl.ds(bound(core * BLOCK + row, ROW_BLOCK), tall), pl.ds(bound(col, LANES), wide)]

    sets, at = [], 0
    for number, groups in enumerate(grad_sets(bits)):
        members = []
        for group in groups:
            view = late_view if number else early_view
            members.append(Piece(at, group, links, view, got, total, sems))
            at += 1
        sets.append(members)
    other_rows = pl.ds(bound((1 - core) * BLOCK, BLOCK), BLOCK)
    own_rows = pl.ds(bound(core * BLOCK, BLOCK), BLOCK)

    def start(members, source, shift):
        for piece in members:
            piece.start(source.at[other_rows, pl.ds(piece.first - shift, piece.width)])

    def advance(members):
        for piece in members:
            piece.advance()

    keep = move(early_grads.at[own_rows, :], early_own, keep_sem.at[2])
    start(sets[0], early_grads, LATE)
    widened(small, small_in)
    small_grads[...] = small_grads_in[...]
    keep.wait()
    for copy in loads:
        copy.wait()
    for copy in collect:
        copy.wait()
    advance(sets[0])

    dqkv[:, :D] = turn(dq_t[...])
    lane = lax.broadcasted_iota(jnp.int32, (rows, LANES), 1) < HEAD_DIM
    for step in range(D // LANES):
        pair = []
        for side in range(2):
            first = (2 * step + side) * LANES
            share = dkv_parts[0, :, first : first + LANES].astype(F32)
            for number in range(1, parts):
                share = share + dkv_parts[number, :, first : first + LANES].astype(F32)
            pair.append(share)
        cols = slice(D + step * LANES, D + (step + 1) * LANES)
        dqkv[:, cols] = jnp.where(lane, pair[0], pltpu.roll(pair[1], HEAD_DIM, 1)).astype(BF16)
        cols = slice(2 * D + step * LANES, 2 * D + (step + 1) * LANES)
        dqkv[:, cols] = jnp.where(lane, pltpu.roll(pair[0], HEAD_DIM, 1), pair[1]).astype(BF16)

    def through(grad, column, width):
        return jnp.concatenate(
            [
                back_mul(grad, weights[side * BLOCK : (side + 1) * BLOCK, column : column + width])
                for side in range(2)
            ],
            axis=1,
        )

    def norm_step(grad, normed, inv_std, row):
        put_vector(small_grads, row, col_sum(grad * normed))
        put_vector(small_grads, row + 1, col_sum(grad))
        return norm_back(grad, normed, inv_std, vector(small, row, D))

    grad = through(dqkv[...], QKV, 3 * D)
    dx2 = dx3[...] + norm_step(grad, n4[...], inv[3, :rows, :1], LN4G)
    dx3[...] = dx2
    sep_own[...] = dx2[:, :HALF].astype(BF16)
    right, left = (lax.rem(own + 1, count), core), (lax.rem(own + count - 1, count), core)
    edge_copies = [
        push(sep_own.at[pl.ds(rows - EDGE, EDGE), :], sep_edges.at[0], (edge_send, edge_recv), 0, right),
        push(sep_own.at[pl.ds(0, EDGE), :], sep_edges.at[1], (edge_send, edge_recv), 1, left),
    ]
    low_t = turn(n4[...] * vector(small, LN4G, D) + vector(small, LN4B, D))
    for step in range(3):
        grads[:, QKV + D * step : QKV + D * (step + 1)] = matmul(
            low_t, dqkv[:, D * step : D * (step + 1)]
        ).astype(BF16)
    for block in range(FF // BLOCK):
        side, column = block // 4, POINT + HALF * (block % 4)
        grads[side * BLOCK : (side + 1) * BLOCK, column : column + HALF] = matmul(
            turn(depth[:, block * BLOCK : (block + 1) * BLOCK]), sep_own[...]
        ).astype(BF16)
    put_vector(small_grads, POINTB, col_sum(sep_own[...]))
    start(sets[1], grads, 0)

    for copy in edge_copies:
        copy.wait()
    sep_ext[:EDGE, :] = sep_edges[0]
    sep_ext[mid, :] = sep_own[...]
    sep_ext[EDGE + rows :, :] = sep_edges[1]
    for block in range(FF // BLOCK):
        side, column = block // 4, POINT + HALF * (block % 4)
        depth_grad[:, block * BLOCK : (block + 1) * BLOCK] = (
            back_mul(sep_ext[...], weights[side * BLOCK : (side + 1) * BLOCK, column : column + HALF])
            .astype(BF16)
            .astype(F32)
        )
    advance(sets[0])
    advance(sets[1])

    row_sums[...] = jnp.zeros_like(row_sums)
    half = FF // 2 // LANES

    @pl.loop(0, FF // LANES)
    def _(step):
        cols = span(step, LANES)
        side, lanes = step // half, span(lax.rem(step, half), LANES)
        block = depth_grad[:, cols]
        normed = n3[:, cols]
        gain = small[side, LN3G : LN3G + 1, lanes]
        low = (normed[mid, :] * gain + small[side, LN3B : LN3B + 1, lanes]).astype(BF16).astype(F32)
        summed = jnp.zeros((ext, LANES), F32)
        for tap in range(TAPS):
            row = DEPTH + tap
            moved = pltpu.roll(block, (tap - REACH) % ext, 0) * masks[TAPS - 1 - tap]
            summed = summed + moved * small[side, row : row + 1, lanes]
            small_grads[side, row : row + 1, lanes] = col_sum(low * moved[mid, :])
        g3_grad[:, cols] = summed
        small_grads[side, LN3G : LN3G + 1, lanes] = col_sum(summed[mid, :] * normed[mid, :])
        small_grads[side, LN3B : LN3B + 1, lanes] = col_sum(summed[mid, :])
        scaled = summed * gain
        row_sums[0] = row_sums[0] + scaled
        row_sums[1] = row_sums[1] + scaled * normed

    advance(sets[0])
    inner = jnp.sum(row_sums[0], axis=1, keepdims=True) * (1.0 / FF)
    cross = jnp.sum(row_sums[1], axis=1, keepdims=True) * (1.0 / FF)
    row_sums[0] = jnp.broadcast_to(inner, (ext, LANES))
    row_sums[1] = jnp.broadcast_to(cross, (ext, LANES))

    @pl.loop(0, FF // LANES)
    def _(step):
        cols = span(step, LANES)
        side, lanes = step // half, span(lax.rem(step, half), LANES)
        scaled = g3_grad[mid, cols] * small[side, LN3G : LN3G + 1, lanes]
        mixed_grad = inv[2, mid, :] * (scaled - row_sums[0, mid, :] - n3[mid, cols] * row_sums[1, mid, :])
        low = (mixed_grad * smooth_slope(left_pre[:, cols])).astype(BF16)
        dleft[:, cols] = low
        small_grads[side, LEFTB : LEFTB + 1, lanes] = col_sum(low)

    for step in range(HALF // LANES):
        cols = slice(step * LANES, (step + 1) * LANES)
        scaled = g3_grad[:, cols] * small[0, LN3G : LN3G + 1, cols]
        mixed_grad = inv[2] * (scaled - row_sums[0] - n3[:, cols] * row_sums[1])
        low = (mixed_grad * smooth_slope(conv_pre[:, cols])).astype(BF16).astype(F32)
        conv_grad[:, cols] = low
        for tap in range(3):
            moved = pltpu.roll(low, (tap - 1) % ext, 0) * masks[REACH + 1 - tap]
            conv_taps[:, HALF * tap + step * LANES : HALF * tap + (step + 1) * LANES] = moved[mid, :].astype(BF16)
    put_vector(small_grads, CONVB, col_sum(conv_grad[mid, :]))

    low_t = turn(n2[...] * vector(small, LN2G, D) + vector(small, LN2B, D))
    for step in range(FF // 512):
        grads[:, LEFT + 512 * step : LEFT + 512 * (step + 1)] = matmul(
            low_t, dleft[:, 512 * step : 512 * (step + 1)]
        ).astype(BF16)
    start(sets[2], grads, 0)
    advance(sets[0])
    advance(sets[1])
    for tap in range(3):
        grads[:, CONV + HALF * tap : CONV + HALF * (tap + 1)] = matmul(
            low_t, conv_taps[:, HALF * tap : HALF * (tap + 1)]
        ).astype(BF16)
    grad = through(dleft[...], LEFT, FF) + through(conv_taps[...], CONV, 3 * HALF)
    dx1 = dx3[...] + norm_step(grad, n2[...], inv[1, mid, :1], LN2G)
    gate = jax.nn.sigmoid(glu_pre[:, D:])
    value_grad = dx1 * gate
    dglu = jnp.concatenate([value_grad, value_grad * glu_pre[:, :D] * (1.0 - gate)], axis=1).astype(BF16)
    put_vector(small_grads, GLUB, col_sum(dglu))
    advance(sets[2])
    low_t = turn(n1[...] * vector(small, LN1G, D) + vector(small, LN1B, D))
    for step in range(2):
        grads[:, GLU + D * step : GLU + D * (step + 1)] = matmul(
            low_t, dglu[:, D * step : D * (step + 1)]
        ).astype(BF16)
    grad = through(dglu, GLU, 2 * D)
    result[...] = dx1 + norm_step(grad, n1[...], inv[0, mid, :1], LN1G)
    keep = move(result, grad_out, keep_sem.at[0])
    for side in range(2):
        for block in range(SMALL_WIDTH // BLOCK):
            first = side * BLOCK + block * SMALL_ROWS
            grads[first : first + SMALL_ROWS, SMALL : SMALL + BLOCK] = small_grads[
                side, :, block * BLOCK : (block + 1) * BLOCK
            ].astype(BF16)
        first = side * BLOCK + SMALL_WIDTH // BLOCK * SMALL_ROWS
        grads[first : (side + 1) * BLOCK, SMALL : SMALL + BLOCK] = jnp.zeros(
            ((side + 1) * BLOCK - first, BLOCK), BF16
        )
    start(sets[3], grads, 0)
    while not all(piece.done() for members in sets for piece in members):
        for members in sets:
            advance(members)
    keep.wait()


def last_kernel(dq, dkv, small, small_grads, tensors, count, heads):
    rows = dkv.shape[0] // count
    ext = rows + 2 * EDGE
    bits = count.bit_length() - 1
    pieces = sum(len(groups) for groups in grad_sets(bits))
    early = tensors[0].shape
    scratch = [
        pltpu.VMEM(tensors[2].shape, BF16),
        pltpu.VMEM((rows, D), F32),
        pltpu.VMEM((rows, D), F32),
        pltpu.VMEM((rows, 2 * D), F32),
        pltpu.VMEM((rows, D), F32),
        pltpu.VMEM((rows, FF), F32),
        pltpu.VMEM((ext, HALF), F32),
        pltpu.VMEM((ext, FF), F32),
        pltpu.VMEM((rows, FF), BF16),
        pltpu.VMEM((rows, D), F32),
        pltpu.VMEM((4, ext, LANES), F32),
        pltpu.VMEM((TAPS, ext, LANES), F32),
        pltpu.VMEM((2, SMALL_ROWS, SMALL_WIDTH), F32),
        pltpu.VMEM((2, SMALL_ROWS, SMALL_WIDTH), F32),
        pltpu.VMEM((D, rows), BF16),
        pltpu.VMEM((count // heads, rows, 2 * D), BF16),
        pltpu.VMEM((rows, 3 * D), BF16),
        pltpu.VMEM((rows, HALF), BF16),
        pltpu.VMEM((2, EDGE, HALF), BF16),
        pltpu.VMEM((ext, HALF), BF16),
        pltpu.VMEM((ext, FF), F32),
        pltpu.VMEM((ext, FF), F32),
        pltpu.VMEM((2, ext, LANES), F32),
        pltpu.VMEM((rows, FF), BF16),
        pltpu.VMEM((ext, HALF), F32),
        pltpu.VMEM((rows, 3 * HALF), BF16),
        pltpu.VMEM((2 * BLOCK, LATE), BF16),
        pltpu.VMEM((BLOCK, EARLY), BF16),
        pltpu.VMEM((BLOCK + ROW_BLOCK * max(0, bits - 4), WIDTH), BF16),
        pltpu.VMEM((rows, D), F32),
        pltpu.SemaphoreType.DMA((12,)),
        pltpu.SemaphoreType.DMA((3,)),
    ]
    scratch += sem_pair(heads - 1) + sem_pair(count - 1) + sem_pair(2) + sem_pair(pieces)
    scratch += sem_pair(pieces * bits) + sem_pair(pieces * bits)
    return pl.pallas_call(
        functools.partial(last_body, count, heads),
        out_shape=(shaped((BLOCK, WIDTH), BF16), shaped((rows, D))),
        in_specs=[vmem_spec()] * 4 + [any_spec()] * len(tensors),
        out_specs=[vmem_spec(), any_spec()],
        scratch_shapes=scratch,
        compiler_params=comm_params(3),
        name="last_layers",
    )(dq, dkv, small, small_grads, *tensors)


VECTORS = [
    (LN1G, 1, 256),
    (LN1B, 1, 256),
    (GLUB, 1, 512),
    (LN2G, 1, 256),
    (LN2B, 1, 256),
    (LEFTB, 1, 1024),
    (CONVB, 1, 128),
    (LN3G, 1, 1024),
    (LN3B, 1, 1024),
    (DEPTH, TAPS, 1024),
    (POINTB, 1, 128),
    (LN4G, 1, 256),
    (LN4B, 1, 256),
    (ATTNB, 1, 256),
    (LN5G, 1, 256),
    (LN5B, 1, 256),
    (EXPANDB, 1, 1024),
    (SHRINKB, 1, 256),
]
MATRICES = [
    (GLU, 1024, 1),
    (LEFT, 2048, 1),
    (CONV, 256, 3),
    (POINT, 256, 4),
    (QKV, 1536, 1),
    (LATE + ATTN, 512, 1),
    (LATE + EXPAND, 2048, 1),
    (LATE + SHRINK, 512, 4),
]


def unpack_body(packed, *outs):
    for (first, width, blocks), out in zip(MATRICES, outs):
        for block in range(blocks):

            @pl.loop(0, BLOCK // ROW_BLOCK)
            def _(step):
                value = packed[span(step, ROW_BLOCK), first + block * width : first + (block + 1) * width].astype(F32)
                if blocks == 3:
                    out[block, span(step, ROW_BLOCK), :] = value
                else:
                    out[pl.ds(bound(block * BLOCK + step * ROW_BLOCK, ROW_BLOCK), ROW_BLOCK), :] = value

    small = jnp.concatenate(
        [
            packed[block * SMALL_ROWS : (block + 1) * SMALL_ROWS, SMALL : SMALL + BLOCK].astype(F32)
            for block in range(SMALL_WIDTH // BLOCK)
        ],
        axis=1,
    )
    for (row, tall, size), out in zip(VECTORS, outs[len(MATRICES) :]):
        out[...] = small[row : row + tall, :size]


def unpack(packed):
    shapes = []
    for _, width, blocks in MATRICES:
        shapes.append((3, BLOCK, width) if blocks == 3 else (blocks * BLOCK, width))
    shapes += [(tall, size) for _, tall, size in VECTORS]
    return pl.pallas_call(
        unpack_body,
        out_shape=tuple(shaped(shape) for shape in shapes),
        in_specs=[vmem_spec()],
        out_specs=(vmem_spec(),) * len(shapes),
        compiler_params=pltpu.CompilerParams(vmem_limit_bytes=VMEM_MOST),
        name="unpack",
    )(packed)


def body(tokens, segment_ids, out_grad, *params):
    (
        ln1g, ln1b, glu_w, glu_b, ln2g, ln2b, left_w, left_b, conv_w, conv_b, ln3g, ln3b, depth_w,
        point_w, point_b, ln4g, ln4b, qkv_w, attn_w, attn_b, ln5g, ln5b, expand_w, expand_b,
        shrink_w, shrink_b,
    ) = params
    count = lax.axis_size("ctx")
    heads = D // HEAD_DIM
    rows = tokens.shape[1]
    vectors = [
        ln1g, ln1b, glu_b, ln2g, ln2b, left_b, conv_b, ln3g, ln3b, depth_w,
        point_b, ln4g, ln4b, attn_b, ln5g, ln5b, expand_b, shrink_b,
    ]
    lines = []
    for value in vectors:
        value = value.reshape(-1, value.shape[-1])
        lines.append(jnp.pad(value, ((0, 0), (0, SMALL_WIDTH - value.shape[1]))))
    small = jnp.concatenate(lines, axis=0)
    small = jnp.pad(small, ((0, SMALL_ROWS - small.shape[0]), (0, 0)))
    seg_col = jnp.broadcast_to(segment_ids[0][:, None], (rows, LANES))
    weights = (glu_w, left_w, conv_w, point_w, qkv_w, attn_w, expand_w, shrink_w)
    (
        late, early, small, seg, plan, q_head, kv_head, n1, glu_pre, n2, left_pre, conv_pre, n3,
        depth, n4, x2, inv, masks,
    ) = first_kernel(tokens[0], segment_ids, seg_col, small, weights, count, heads)
    o_head, o_low, log_sum = attend(plan, q_head, kv_head, seg, rows)
    output, small_grads, dx3, early_grads, do_head = middle_kernel(
        o_low, out_grad[0], small, x2, early, count, heads
    )
    dq_head, dkv_head = attend_back(plan, q_head, do_head, o_head, log_sum, kv_head, seg, rows)
    tensors = (
        early_grads, dx3, late, n1, glu_pre, n2, left_pre, conv_pre, n3, depth, n4, inv, masks,
    )
    total, input_grad = last_kernel(dq_head, dkv_head, small, small_grads, tensors, count, heads)
    pieces = unpack(total)
    matrices, lines = pieces[: len(MATRICES)], pieces[len(MATRICES) :]
    lines = [line if line.shape[0] > 1 else line.reshape(-1) for line in lines]
    g_glu, g_left, g_conv, g_point, g_qkv, g_attn, g_expand, g_shrink = matrices
    (
        g_ln1g, g_ln1b, g_glu_b, g_ln2g, g_ln2b, g_left_b, g_conv_b, g_ln3g, g_ln3b, g_depth,
        g_point_b, g_ln4g, g_ln4b, g_attn_b, g_ln5g, g_ln5b, g_expand_b, g_shrink_b,
    ) = lines
    return (
        output[None], input_grad[None], g_ln1g, g_ln1b, g_glu, g_glu_b, g_ln2g, g_ln2b, g_left,
        g_left_b, g_conv, g_conv_b, g_ln3g, g_ln3b, g_depth, g_point, g_point_b, g_ln4g, g_ln4b,
        g_qkv, g_attn, g_attn_b, g_ln5g, g_ln5b, g_expand, g_expand_b, g_shrink, g_shrink_b,
    )


def solution(mesh):
    return jax.shard_map(
        body,
        mesh=mesh,
        in_specs=(
            P("ws", "ctx", None),
            P("ws", "ctx"),
            P("ws", "ctx", None),
            P("ws"),
            P("ws"),
            P("ws", None),
            P("ws"),
            P("ws"),
            P("ws"),
            P("ws", None),
            P("ws"),
            P(None, "ws", None),
            P("ws"),
            P("ws"),
            P("ws"),
            P(None, "ws"),
            P("ws", None),
            P("ws"),
            P("ws"),
            P("ws"),
            P("ws", None),
            P("ws", None),
            P("ws"),
            P("ws"),
            P("ws"),
            P("ws", None),
            P("ws"),
            P("ws", None),
            P("ws"),
        ),
        out_specs=(
            P("ws", "ctx", None),
            P("ws", "ctx", None),
            P("ws"),
            P("ws"),
            P("ws", None),
            P("ws"),
            P("ws"),
            P("ws"),
            P("ws", None),
            P("ws"),
            P(None, "ws", None),
            P("ws"),
            P("ws"),
            P("ws"),
            P(None, "ws"),
            P("ws", None),
            P("ws"),
            P("ws"),
            P("ws"),
            P("ws", None),
            P("ws", None),
            P("ws"),
            P("ws"),
            P("ws"),
            P("ws", None),
            P("ws"),
            P("ws", None),
            P("ws"),
        ),
        check_vma=False,
    )
```

time: 1300 us -> 279 us (0.21); the launches traced: 1290 us -> 279 us
  blocking collectives: 555 us -> 0 us
  Pallas kernels: 0 us -> 263 us
  waiting for transfers between devices: 263 us -> 0 us
  matrix products: 192 us -> 0 us
  other arithmetic: 156 us -> 0 us
  local copies, waits for them, and re-layouts: 76.9 us -> 15.6 us
  starting transfers between devices: 20.8 us -> 0 us
  between operations: 19 us -> 0.74 us
    psum x1 -> x0, blocking collectives: 472 us -> none  [body(): lax.psum((pair_share[0], pair_share[1], pair_share[2], pair_share[3], pai...]
    pallas_call x0 -> x6, Pallas kernels: none -> 263 us  [the longest x1 138 us: last_kernel(): pl.pallas_call(functools.partial(last_body, count, heads), out_shape=(sha...]
    dot_general x118 -> x0, matrix products: 192 us -> none  [the longest x20 48.5 us: score_block(): jnp.einsum('qhd,khd->hqk', queries, key_heads, preferred_element_type=jnp...]
    ppermute x40 -> x0, waiting for transfers between devices: 138 us -> none  [the longest x32 135 us: passed_along(): return lax.ppermute(block, axis, route)]
    convert_element_type x129 -> x0, other arithmetic: 105 us -> none  [the longest x16 28.4 us: cycle_turn(): passed_along(key_acc.astype(jnp.bfloat16), 'ctx', 1).astype(key_acc.dtype)]
    all_gather x8 -> x0, waiting for transfers between devices: 81.8 us -> none  [the longest x1 58.6 us: body(): lax.all_gather(keys_flat, 'ctx', axis=0, tiled=True)]
    all_gather x21 -> x0, blocking collectives: 79.5 us -> none  [the longest x1 42.2 us: body(): seg_all = lax.all_gather(seg_own, 'ctx', axis=0, tiled=True)]
    dynamic_slice x65 -> x0, local copies, waits for them, and re-layouts: 49 us -> none  [the longest x8 16.3 us: block_turn(): lax.dynamic_slice_in_dim(keys_whole, first_row, block_rows)]
  transfers between devices with their start and end apart: 57 -> 0, of which waited for: 39 -> 0; matrix products, arithmetic and copies ran while one was open for 21% -> 0% of each run, Pallas kernels for 0% -> 0%
where the time goes in v2:
time: 279 us
  Pallas kernels  263 us (94%)
  local copies, waits for them, and re-layouts  15.6 us (6%)
    pallas_call x1, Pallas kernels, last_kernel(): pl.pallas_call(functools.partial(last_body, count, heads), out_shape=(sha...  138 us
    pallas_call x1, Pallas kernels, first_kernel(): pl.pallas_call(functools.partial(first_body, count, heads), out_shape=out...  53 us
    pallas_call x1, Pallas kernels, middle_kernel(): pl.pallas_call(functools.partial(middle_body, count, heads), out_shape=(s...  21.7 us
    pallas_call x1, Pallas kernels, attend(): pl.pallas_call(functools.partial(attend_body, rows), out_shape=(shaped(q_...  20.8 us
    pallas_call x1, Pallas kernels, attend_back(): pl.pallas_call(functools.partial(attend_back_body, rows), out_shape=(shap...  20.8 us
    pallas_call x1, Pallas kernels, unpack(): pl.pallas_call(unpack_body, out_shape=tuple((shaped(shape) for shape in s...  8.89 us
    pad x13, local copies, waits for them, and re-layouts, body(): lines.append(jnp.pad(value, ((0, 0), (0, SMALL_WIDTH - value.shape[1]))))  8.83 us

profile of v2, /device:TPU:0, one launch (start us, length us, event | category | flops | bytes accessed | tf_op | source)
XLA Modules:
  0.0 279.2 jit_solution(14021491313525724894)
XLA Ops:
  0.7 0.7 pad.46
  1.4 0.7 pad.47
  2.0 0.7 pad.48
  2.7 0.7 pad.49
  3.4 0.7 pad.50
  4.1 0.7 pad.51
  4.7 0.7 pad.52
  5.4 0.7 pad.53
  6.1 0.7 pad.54
  6.8 0.7 pad.55
  7.5 0.7 pad.56
  8.1 0.7 pad.57
  8.8 0.7 pad.58
  9.5 3.1 %concatenate.3 = f32[26,1024]{1,0:T(8,128)S(1)} concatenate(f32[1,1024]{1,0:T(1,128)S(1)} %pad.46, f32[1,1024]{1,0:T(1,128)S(1)} %pad.47, f32[1,1024]{1,0:T(1,128)S(1)} %pad.48, f32[1,1024]{1,0:T(1,128)S(1)} %pad.49, f32[1,1024]{1,0:T(1,128)S(1)} %pad.50, f32[1,1024]{1,0:T(1,128)} %bitcast.43, f32[1,1024]{1,0:T(1,128)S(1)} %pad.51, f32[1,1024]{1,0:T(1,128)} %bitcast.44, ...), dimensions={0} | concatenate | bytes 212992 | tf_op jit(solution)/shard_map/concatenate | solution.py:1380
  12.7 0.7 pad.59.small_in
  13.3 1.4 broadcast_in_dim.14.seg_col_ref
  14.8 53.0 %first_layers.1 = (bf16[512,6400]{1,0:T(8,128)(2,1)}, bf16[512,4608]{1,0:T(8,128)(2,1)}, f32[2,32,1024]{2,1,0:T(8,128)}, s32[16,1,256]{2,1,0:T(1,128)}, s32[8,12...) custom-call(bf16[256,512]{1,0:T(8,128)(2,1)} %bitcast.40, ...), custom_call_target="tpu_custom_call" | custom-call | tf_op jit(solution)/shard_map/first_layers/pallas_call | solution.py:541
  67.8 20.8 %attend.1 = (f32[64,2048]{1,0:T(8,128)}, bf16[64,2048]{1,0:T(8,128)(2,1)}, f32[1,2048]{1,0:T(1,128)}) custom-call(s32[8,128]{1,0:T(8,128)} %get-tuple-element.84.plan_ref, bf16[64,2048]{1,0:T(8,128)(2,1)} %get-tuple-element.85.q_ref, bf16[4096,128]{1,0:T(8,128)(2,1)} %get-tuple-element.86.kv_ref, s32[16,1,256]{2,1,0:T(1,128)} %get-tuple-element.87.seg_ref), custom_call_target="tpu_custom_call" | custom-call | tf_op jit(solution)/shard_map/attend/pallas_call | solution.py:619
  88.6 21.7 %middle_layers.1 = (bf16[256,512]{1,0:T(8,128)(2,1)}, f32[2,32,1024]{2,1,0:T(8,128)}, f32[256,512]{1,0:T(8,128)}, bf16[512,4608]{1,0:T(8,128)(2,1)}, bf16[64,2048]{1,0:T(8,128)(2,1)}) custom-call(bf16[64,2048]{1,0:T(8,128)(2,1)} %get-tuple-element.88.o_in, bf16[256,512]{1,0:T(8,128)(2,1)} %bitcast.41, f32[2,32,1024]{2,1,0:T(8,128)} %get-tuple-element.89.small_in, ...), custom_call_target="tpu_custom_call" | custom-call | tf_op jit(solution)/shard_map/middle_layers/pallas_call | solution.py:803
  110.3 20.8 %attend_back.1 = (bf16[64,2048]{1,0:T(8,128)(2,1)}, bf16[4096,128]{1,0:T(8,128)(2,1)}) custom-call(s32[8,128]{1,0:T(8,128)} %get-tuple-element.84.plan_ref, bf16[64,2048]{1,0:T(8,128)(2,1)} %get-tuple-element.85.q_ref, bf16[64,2048]{1,0:T(8,128)(2,1)} %get-tuple-element.93.do_ref, f32[64,2048]{1,0:T(8,128)} %get-tuple-element.94.o_ref, ...), custom_call_target="tpu_custom_call" | custom-call | tf_op jit(solution)/shard_map/attend_back/pallas_call | solution.py:668
  131.0 137.7 %last_layers.1 = (bf16[256,11264]{1,0:T(8,128)(2,1)}, f32[256,512]{1,0:T(8,128)}) custom-call(bf16[64,2048]{1,0:T(8,128)(2,1)} %get-tuple-element.96.dq_in, bf16[4096,128]{1,0:T(8,128)(2,1)} %get-tuple-element.97.dkv_in, f32[2,32,1024]{2,1,0:T(8,128)} %get-tuple-element.89.small_in, f32[2,32,1024]{2,1,0:T(8,128)} %get-tuple-element.98.small_grads_in, ...), custom_call_target="tpu_custom_call" | custom-call | tf_op jit(solution)/shard_map/last_layers/pallas_call | solution.py:1282
  268.7 0.0 copy-start.1
  268.7 0.0 copy-start
  268.8 8.9 %unpack.1 = (f32[256,1024]{1,0:T(8,128)}, f32[256,2048]{1,0:T(8,128)}, f32[3,256,256]{2,1,0:T(8,128)}, f32[1024,256]{1,0:T(8,128)}, f32[256,1536]{1,0:T(8,128)},...) custom-call(bf16[256,11264]{1,0:T(8,128)(2,1)} %get-tuple-element.11, ...), custom_call_target="tpu_custom_call" | custom-call | tf_op jit(solution)/shard_map/unpack/pallas_call | solution.py:1353
  277.7 0.0 copy-done.1
  277.7 0.7 copy.59
  278.4 0.0 copy-done
  278.4 0.8 copy.60
Async XLA Ops:
  268.7 8.9 %copy-start.1 = (bf16[256,512]{1,0:T(8,128)(2,1)S(1)}, bf16[256,512]{1,0:T(8,128)(2,1)}, u32[]{:S(2)}) copy-start(bf16[256,512]{1,0:T(8,128)(2,1)} %get-tuple-element.92) | copy-start | bytes 786436
  268.7 9.6 %copy-start = (f32[256,512]{1,0:T(8,128)S(1)}, f32[256,512]{1,0:T(8,128)}, u32[]{:S(2)}) copy-start(f32[256,512]{1,0:T(8,128)} %get-tuple-element.112) | copy-start | bytes 1572868

commit v3 on v2

--- a/solution.py
+++ b/solution.py
@@ -37,6 +37,38 @@
 (POINTB, LN4G, LN4B, ATTNB, LN5G, LN5B, EXPANDB, SHRINKB) = range(DEPTH + TAPS, DEPTH + TAPS + 8)
 
 
+VECTORS = [
+    (LN1G, 1, 256),
+    (LN1B, 1, 256),
+    (GLUB, 1, 512),
+    (LN2G, 1, 256),
+    (LN2B, 1, 256),
+    (LEFTB, 1, 1024),
+    (CONVB, 1, 128),
+    (LN3G, 1, 1024),
+    (LN3B, 1, 1024),
+    (DEPTH, TAPS, 1024),
+    (POINTB, 1, 128),
+    (LN4G, 1, 256),
+    (LN4B, 1, 256),
+    (ATTNB, 1, 256),
+    (LN5G, 1, 256),
+    (LN5B, 1, 256),
+    (EXPANDB, 1, 1024),
+    (SHRINKB, 1, 256),
+]
+MATRICES = [
+    (GLU, 1024, 1),
+    (LEFT, 2048, 1),
+    (CONV, 256, 3),
+    (POINT, 256, 4),
+    (QKV, 1536, 1),
+    (LATE + ATTN, 512, 1),
+    (LATE + EXPAND, 2048, 1),
+    (LATE + SHRINK, 512, 4),
+]
+
+
 def vmem_spec():
     return pl.BlockSpec(memory_space=pltpu.VMEM)
 
@@ -162,6 +194,13 @@
         dst_ref[core] = src_ref[core].astype(BF16).astype(F32)
 
 
+def turned_segments(out_ref, first, row):
+    for step in range(row.shape[1] // LANES):
+        part = row[:, step * LANES : (step + 1) * LANES].astype(F32)
+        here = pl.ds(bound(first + step * LANES, LANES), LANES)
+        out_ref[here, :] = jnp.broadcast_to(part, (LANES, LANES)).T
+
+
 WEIGHT_COLUMNS = [
     (0, GLU, 1024, 1, False),
     (1, LEFT, 2048, 1, False),
@@ -186,10 +225,9 @@
     heads,
     tok_ref,
     seg_row_ref,
-    seg_col_ref,
-    small_in,
     *refs,
 ):
+    vectors, refs = refs[: len(VECTORS)], refs[len(VECTORS) :]
     weights, refs = refs[:8], refs[8:]
     outs, refs = refs[:18], refs[18:]
     (
@@ -218,6 +256,8 @@
         early,
         edges,
         seg_edges,
+        seg_col,
+        small_own,
         x_ext,
         seg_ext,
         masks,
@@ -278,6 +318,10 @@
                 )
             )
             column += width
+    small_own[...] = jnp.zeros_like(small_own)
+    for (row, tall, size), vector_ref in zip(VECTORS, vectors):
+        small_own[row : row + tall, :size] = vector_ref[...]
+    turned_segments(seg_col, 0, seg_row_ref[...])
     greet([sibling] + peers)
 
     copies = []
@@ -285,11 +329,11 @@
     edge_copies = [
         push(tok_ref.at[pl.ds(rows - EDGE, EDGE), :], edges.at[0], (edge_send, edge_recv), 0, right),
         push(tok_ref.at[pl.ds(0, EDGE), :], edges.at[1], (edge_send, edge_recv), 1, left),
-        push(seg_col_ref.at[pl.ds(rows - EDGE, EDGE), :], seg_edges.at[0], (edge_send, edge_recv), 2, right),
-        push(seg_col_ref.at[pl.ds(0, EDGE), :], seg_edges.at[1], (edge_send, edge_recv), 3, left),
+        push(seg_col.at[pl.ds(rows - EDGE, EDGE), :], seg_edges.at[0], (edge_send, edge_recv), 2, right),
+        push(seg_col.at[pl.ds(0, EDGE), :], seg_edges.at[1], (edge_send, edge_recv), 3, left),
     ]
-    small_copy = push(small_in, small_out.at[core], (ws_send, ws_recv), len(WEIGHT_COLUMNS), sibling)
-    small_out[core] = small_in[...]
+    small_copy = push(small_own, small_out.at[core], (ws_send, ws_recv), len(WEIGHT_COLUMNS), sibling)
+    small_out[core] = small_own[...]
 
     at, weight_copies = 0, []
     for (number, first, width, blocks, is_early), column in zip(WEIGHT_COLUMNS, stage_at):
@@ -322,9 +366,9 @@
     x_ext[:EDGE, :] = edges[0].astype(F32)
     x_ext[mid, :] = tok_ref[...].astype(F32)
     x_ext[EDGE + rows :, :] = edges[1].astype(F32)
-    seg_ext[:EDGE, :] = jnp.where(own == 0, -1, seg_edges[0])
-    seg_ext[mid, :] = seg_col_ref[...]
-    seg_ext[EDGE + rows :, :] = jnp.where(own == count - 1, -1, seg_edges[1])
+    seg_ext[:EDGE, :] = jnp.where(own == 0, -1.0, seg_edges[0])
+    seg_ext[mid, :] = seg_col[...]
+    seg_ext[EDGE + rows :, :] = jnp.where(own == count - 1, -1.0, seg_edges[1])
     tap_masks(masks, seg_ext)
 
     normed, inv_std = norm_fwd(x_ext[...])
@@ -479,7 +523,7 @@
         copy.wait()
 
 
-def first_kernel(tokens, seg_row, seg_col, small, weights, count, heads):
+def first_kernel(tokens, seg_row, vectors, weights, count, heads):
     rows = tokens.shape[0]
     ext = rows + 2 * EDGE
     late = (2 * BLOCK, SMALL)
@@ -512,9 +556,11 @@
         pltpu.VMEM(late, BF16),
         pltpu.VMEM(early, BF16),
         pltpu.VMEM((2, EDGE, D), BF16),
-        pltpu.VMEM((2, EDGE, LANES), jnp.int32),
+        pltpu.VMEM((2, EDGE, LANES), F32),
+        pltpu.VMEM((rows, LANES), F32),
+        pltpu.VMEM((SMALL_ROWS, SMALL_WIDTH), F32),
         pltpu.VMEM((ext, D), F32),
-        pltpu.VMEM((ext, LANES), jnp.int32),
+        pltpu.VMEM((ext, LANES), F32),
         pltpu.VMEM((TAPS, ext, LANES), F32),
         pltpu.VMEM((2, SMALL_ROWS, SMALL_WIDTH), F32),
         pltpu.VMEM((ext, D), BF16),
@@ -541,12 +587,12 @@
     return pl.pallas_call(
         functools.partial(first_body, count, heads),
         out_shape=out_shape,
-        in_specs=[vmem_spec()] * 4 + [any_spec()] * 8,
+        in_specs=[vmem_spec()] * (2 + len(vectors)) + [any_spec()] * 8,
         out_specs=out_specs,
         scratch_shapes=scratch,
         compiler_params=comm_params(1),
         name="first_layers",
-    )(tokens, seg_row, seg_col, small, *weights)
+    )(tokens, seg_row, *vectors, *weights)
 
 
 def turn_keys(kv_ref, turned):
@@ -561,10 +607,7 @@
 
     @pl.loop(0, count)
     def _(source):
-        for step in range(rows // LANES):
-            row = seg_ref[source, :, step * LANES : (step + 1) * LANES].astype(F32)
-            column = jnp.broadcast_to(row, (LANES, LANES)).T
-            segk[pl.ds(bound(source * rows + step * LANES, LANES), LANES), :] = column
+        turned_segments(segk, source * rows, seg_ref[source])
 
 
 def masked(scores, segk, here, seg_q):
@@ -1020,6 +1063,40 @@
     loads = [move(a, b, load_sem.at[at]) for at, (a, b) in enumerate(zip(sources, targets))]
     greet([sibling] + peers)
 
+    bit_of = [lax.rem(own // 2**bit, 2) for bit in range(bits)]
+    partner = [(own + 2**bit - 2 * 2**bit * bit_of[bit], core) for bit in range(bits)]
+    links = (core, sibling, bit_of, partner)
+    sems = ((ws_send, ws_recv), (rs_send, rs_recv), (ag_send, ag_recv))
+
+    def early_view(where):
+        row, tall, col, wide = where
+        return early_own.at[pl.ds(bound(row, ROW_BLOCK), tall), pl.ds(bound(col - LATE, LANES), wide)]
+
+    def late_view(where):
+        row, tall, col, wide = where
+        return grads.at[pl.ds(bound(core * BLOCK + row, ROW_BLOCK), tall), pl.ds(bound(col, LANES), wide)]
+
+    sets, at = [], 0
+    for number, groups in enumerate(grad_sets(bits)):
+        members = []
+        for group in groups:
+            view = late_view if number else early_view
+            members.append(Piece(at, group, links, view, got, total, sems))
+            at += 1
+        sets.append(members)
+    other_rows = pl.ds(bound((1 - core) * BLOCK, BLOCK), BLOCK)
+    own_rows = pl.ds(bound(core * BLOCK, BLOCK), BLOCK)
+
+    def start(members, source, shift):
+        for piece in members:
+            piece.start(source.at[other_rows, pl.ds(piece.first - shift, piece.width)])
+
+    def advance(members):
+        for piece in members:
+            piece.advance()
+
+    keep = move(early_grads.at[own_rows, :], early_own, keep_sem.at[2])
+    start(sets[0], early_grads, LATE)
     slot = dq_t.at[span(head, HEAD_DIM), :]
     kv_slot = dkv_parts.at[part, :, span(head, LANES)]
     collect = []
@@ -1033,45 +1110,13 @@
     collect.append(move(dq_in.at[:, span(head, rows)], slot, keep_sem.at[0]))
     collect.append(move(dkv_in.at[span(own, rows), :], kv_slot, keep_sem.at[1]))
 
-    bit_of = [lax.rem(own // 2**bit, 2) for bit in range(bits)]
-    partner = [(own + 2**bit - 2 * 2**bit * bit_of[bit], core) for bit in range(bits)]
-    links = (core, sibling, bit_of, partner)
-    sems = ((ws_send, ws_recv), (rs_send, rs_recv), (ag_send, ag_recv))
-
-    def early_view(where):
-        row, tall, col, wide = where
-        return early_own.at[pl.ds(bound(row, ROW_BLOCK), tall), pl.ds(bound(col - LATE, LANES), wide)]
-
-    def late_view(where):
-        row, tall, col, wide = where
-        return grads.at[pl.ds(bound(core * BLOCK + row, ROW_BLOCK), tall), pl.ds(bound(col, LANES), wide)]
-
-    sets, at = [], 0
-    for number, groups in enumerate(grad_sets(bits)):
-        members = []
-        for group in groups:
-            view = late_view if number else early_view
-            members.append(Piece(at, group, links, view, got, total, sems))
-            at += 1
-        sets.append(members)
-    other_rows = pl.ds(bound((1 - core) * BLOCK, BLOCK), BLOCK)
-    own_rows = pl.ds(bound(core * BLOCK, BLOCK), BLOCK)
-
-    def start(members, source, shift):
-        for piece in members:
-            piece.start(source.at[other_rows, pl.ds(piece.first - shift, piece.width)])
-
-    def advance(members):
-        for piece in members:
-            piece.advance()
-
-    keep = move(early_grads.at[own_rows, :], early_own, keep_sem.at[2])
-    start(sets[0], early_grads, LATE)
     widened(small, small_in)
     small_grads[...] = small_grads_in[...]
     keep.wait()
+    advance(sets[0])
     for copy in loads:
         copy.wait()
+    advance(sets[0][:2])
     for copy in collect:
         copy.wait()
     advance(sets[0])
@@ -1114,6 +1159,7 @@
         push(sep_own.at[pl.ds(rows - EDGE, EDGE), :], sep_edges.at[0], (edge_send, edge_recv), 0, right),
         push(sep_own.at[pl.ds(0, EDGE), :], sep_edges.at[1], (edge_send, edge_recv), 1, left),
     ]
+    advance(sets[0])
     low_t = turn(n4[...] * vector(small, LN4G, D) + vector(small, LN4B, D))
     for step in range(3):
         grads[:, QKV + D * step : QKV + D * (step + 1)] = matmul(
@@ -1290,50 +1336,36 @@
     )(dq, dkv, small, small_grads, *tensors)
 
 
-VECTORS = [
-    (LN1G, 1, 256),
-    (LN1B, 1, 256),
-    (GLUB, 1, 512),
-    (LN2G, 1, 256),
-    (LN2B, 1, 256),
-    (LEFTB, 1, 1024),
-    (CONVB, 1, 128),
-    (LN3G, 1, 1024),
-    (LN3B, 1, 1024),
-    (DEPTH, TAPS, 1024),
-    (POINTB, 1, 128),
-    (LN4G, 1, 256),
-    (LN4B, 1, 256),
-    (ATTNB, 1, 256),
-    (LN5G, 1, 256),
-    (LN5B, 1, 256),
-    (EXPANDB, 1, 1024),
-    (SHRINKB, 1, 256),
-]
-MATRICES = [
-    (GLU, 1024, 1),
-    (LEFT, 2048, 1),
-    (CONV, 256, 3),
-    (POINT, 256, 4),
-    (QKV, 1536, 1),
-    (LATE + ATTN, 512, 1),
-    (LATE + EXPAND, 2048, 1),
-    (LATE + SHRINK, 512, 4),
-]
-
-
-def unpack_body(packed, *outs):
-    for (first, width, blocks), out in zip(MATRICES, outs):
+def unpack_body(output_in, grad_in, packed_in, *refs):
+    size = len(MATRICES) + len(VECTORS) + 2
+    outs, (packed, *stages, load_sem, out_sem) = refs[:size], refs[size:]
+    output_ref, grad_ref, *outs = outs
+    order = [len(MATRICES)] + list(range(len(MATRICES)))
+    bounds = [(first, width * blocks) for first, width, blocks in MATRICES] + [(SMALL, BLOCK)]
+    loads = {}
+    for at in order:
+        cols = pl.ds(*bounds[at])
+        loads[at] = move(packed_in.at[:, cols], packed.at[:, cols], load_sem.at[at])
+    stores = [
+        move(output_in, output_ref, out_sem.at[len(MATRICES)]),
+        move(grad_in, grad_ref, out_sem.at[len(MATRICES) + 1]),
+    ]
+    for at, (first, width, blocks) in enumerate(MATRICES):
+        loads[at].wait()
+        stage = stages[at]
         for block in range(blocks):
 
             @pl.loop(0, BLOCK // ROW_BLOCK)
             def _(step):
                 value = packed[span(step, ROW_BLOCK), first + block * width : first + (block + 1) * width].astype(F32)
                 if blocks == 3:
-                    out[block, span(step, ROW_BLOCK), :] = value
+                    stage[block, span(step, ROW_BLOCK), :] = value
                 else:
-                    out[pl.ds(bound(block * BLOCK + step * ROW_BLOCK, ROW_BLOCK), ROW_BLOCK), :] = value
-
+                    stage[pl.ds(bound(block * BLOCK + step * ROW_BLOCK, ROW_BLOCK), ROW_BLOCK), :] = value
+
+        stores.append(move(stage, outs[at], out_sem.at[at]))
+
+    loads[len(MATRICES)].wait()
     small = jnp.concatenate(
         [
             packed[block * SMALL_ROWS : (block + 1) * SMALL_ROWS, SMALL : SMALL + BLOCK].astype(F32)
@@ -1343,21 +1375,27 @@
     )
     for (row, tall, size), out in zip(VECTORS, outs[len(MATRICES) :]):
         out[...] = small[row : row + tall, :size]
-
-
-def unpack(packed):
+    for copy in stores:
+        copy.wait()
+
+
+def unpack(output, grad, packed):
     shapes = []
     for _, width, blocks in MATRICES:
         shapes.append((3, BLOCK, width) if blocks == 3 else (blocks * BLOCK, width))
-    shapes += [(tall, size) for _, tall, size in VECTORS]
+    vectors = [(tall, size) for _, tall, size in VECTORS]
     return pl.pallas_call(
         unpack_body,
-        out_shape=tuple(shaped(shape) for shape in shapes),
-        in_specs=[vmem_spec()],
-        out_specs=(vmem_spec(),) * len(shapes),
+        out_shape=(shaped(output.shape, output.dtype), shaped(grad.shape))
+        + tuple(shaped(shape) for shape in shapes + vectors),
+        in_specs=[vmem_spec()] * 2 + [any_spec()],
+        out_specs=[any_spec()] * (2 + len(shapes)) + [vmem_spec()] * len(vectors),
+        scratch_shapes=[pltpu.VMEM(packed.shape, packed.dtype)]
+        + [pltpu.VMEM(shape, F32) for shape in shapes]
+        + [pltpu.SemaphoreType.DMA((len(shapes) + 1,)), pltpu.SemaphoreType.DMA((len(shapes) + 2,))],
         compiler_params=pltpu.CompilerParams(vmem_limit_bytes=VMEM_MOST),
         name="unpack",
-    )(packed)
+    )(output, grad, packed)
 
 
 def body(tokens, segment_ids, out_grad, *params):
@@ -1373,18 +1411,12 @@
         ln1g, ln1b, glu_b, ln2g, ln2b, left_b, conv_b, ln3g, ln3b, depth_w,
         point_b, ln4g, ln4b, attn_b, ln5g, ln5b, expand_b, shrink_b,
     ]
-    lines = []
-    for value in vectors:
-        value = value.reshape(-1, value.shape[-1])
-        lines.append(jnp.pad(value, ((0, 0), (0, SMALL_WIDTH - value.shape[1]))))
-    small = jnp.concatenate(lines, axis=0)
-    small = jnp.pad(small, ((0, SMALL_ROWS - small.shape[0]), (0, 0)))
-    seg_col = jnp.broadcast_to(segment_ids[0][:, None], (rows, LANES))
+    vectors = [value.reshape(-1, value.shape[-1]) for value in vectors]
     weights = (glu_w, left_w, conv_w, point_w, qkv_w, attn_w, expand_w, shrink_w)
     (
         late, early, small, seg, plan, q_head, kv_head, n1, glu_pre, n2, left_pre, conv_pre, n3,
         depth, n4, x2, inv, masks,
-    ) = first_kernel(tokens[0], segment_ids, seg_col, small, weights, count, heads)
+    ) = first_kernel(tokens[0], segment_ids, vectors, weights, count, heads)
     o_head, o_low, log_sum = attend(plan, q_head, kv_head, seg, rows)
     output, small_grads, dx3, early_grads, do_head = middle_kernel(
         o_low, out_grad[0], small, x2, early, count, heads
@@ -1394,7 +1426,7 @@
         early_grads, dx3, late, n1, glu_pre, n2, left_pre, conv_pre, n3, depth, n4, inv, masks,
     )
     total, input_grad = last_kernel(dq_head, dkv_head, small, small_grads, tensors, count, heads)
-    pieces = unpack(total)
+    output, input_grad, *pieces = unpack(output, input_grad, total)
     matrices, lines = pieces[: len(MATRICES)], pieces[len(MATRICES) :]
     lines = [line if line.shape[0] > 1 else line.reshape(-1) for line in lines]
     g_glu, g_left, g_conv, g_point, g_qkv, g_attn, g_expand, g_shrink = matrices

time: 279 us -> 268 us (0.961)
  local copies, waits for them, and re-layouts: 15.6 us -> 0 us
  Pallas kernels: 263 us -> 267 us
    pad x14 -> x0, local copies, waits for them, and re-layouts: 9.5 us -> none  [the longest x13 8.83 us: body(): lines.append(jnp.pad(value, ((0, 0), (0, SMALL_WIDTH - value.shape[1]))))]
    pallas_call x1, Pallas kernels: 138 us -> 146 us  [last_kernel(): pl.pallas_call(functools.partial(last_body, count, heads), out_shape=(sha...]
    concatenate x1 -> x0, local copies, waits for them, and re-layouts: 3.15 us -> none  [body(): small = jnp.concatenate(lines, axis=0)]
where the time goes in v3:
time: 268 us
  Pallas kernels  267 us (100%)
    pallas_call x1, Pallas kernels, last_kernel(): pl.pallas_call(functools.partial(last_body, count, heads), out_shape=(sha...  146 us
    pallas_call x1, Pallas kernels, first_kernel(): pl.pallas_call(functools.partial(first_body, count, heads), out_shape=out...  53.2 us
    pallas_call x1, Pallas kernels, middle_kernel(): pl.pallas_call(functools.partial(middle_body, count, heads), out_shape=(s...  23.2 us
    pallas_call x1, Pallas kernels, attend_back(): pl.pallas_call(functools.partial(attend_back_body, rows), out_shape=(shap...  18.3 us
    pallas_call x1, Pallas kernels, attend(): pl.pallas_call(functools.partial(attend_body, rows), out_shape=(shaped(q_...  18.3 us
    pallas_call x1, Pallas kernels, unpack(): pl.pallas_call(unpack_body, out_shape=(shaped(output.shape, output.dtype)...  7.98 us

profile of v3, /device:TPU:0, one launch (start us, length us, event | category | flops | bytes accessed | tf_op | source)
XLA Modules:
  0.0 267.5 jit_solution(171022764379149397)
XLA Ops:
  0.7 53.2 %first_layers.1 = (bf16[512,6400]{1,0:T(8,128)(2,1)}, bf16[512,4608]{1,0:T(8,128)(2,1)}, f32[2,32,1024]{2,1,0:T(8,128)}, s32[16,1,256]{2,1,0:T(1,128)}, s32[8,12...) custom-call(bf16[256,512]{1,0:T(8,128)(2,1)} %bitcast.38, ...), custom_call_target="tpu_custom_call" | custom-call | tf_op jit(solution)/shard_map/first_layers/pallas_call | solution.py:587
  53.9 18.3 %attend.1 = (f32[64,2048]{1,0:T(8,128)}, bf16[64,2048]{1,0:T(8,128)(2,1)}, f32[1,2048]{1,0:T(1,128)}) custom-call(s32[8,128]{1,0:T(8,128)} %get-tuple-element.86.plan_ref, bf16[64,2048]{1,0:T(8,128)(2,1)} %get-tuple-element.87.q_ref, bf16[4096,128]{1,0:T(8,128)(2,1)} %get-tuple-element.88.kv_ref, s32[16,1,256]{2,1,0:T(1,128)} %get-tuple-element.89.seg_ref), custom_call_target="tpu_custom_call" | custom-call | tf_op jit(solution)/shard_map/attend/pallas_call | solution.py:662
  72.3 23.2 %middle_layers.1 = (bf16[256,512]{1,0:T(8,128)(2,1)}, f32[2,32,1024]{2,1,0:T(8,128)}, f32[256,512]{1,0:T(8,128)}, bf16[512,4608]{1,0:T(8,128)(2,1)}, bf16[64,2048]{1,0:T(8,128)(2,1)}) custom-call(bf16[64,2048]{1,0:T(8,128)(2,1)} %get-tuple-element.90.o_in, bf16[256,512]{1,0:T(8,128)(2,1)} %bitcast.39, f32[2,32,1024]{2,1,0:T(8,128)} %get-tuple-element.91.small_in, ...), custom_call_target="tpu_custom_call" | custom-call | tf_op jit(solution)/shard_map/middle_layers/pallas_call | solution.py:846
  95.5 18.3 %attend_back.1 = (bf16[64,2048]{1,0:T(8,128)(2,1)}, bf16[4096,128]{1,0:T(8,128)(2,1)}) custom-call(s32[8,128]{1,0:T(8,128)} %get-tuple-element.86.plan_ref, bf16[64,2048]{1,0:T(8,128)(2,1)} %get-tuple-element.87.q_ref, bf16[64,2048]{1,0:T(8,128)(2,1)} %get-tuple-element.95.do_ref, f32[64,2048]{1,0:T(8,128)} %get-tuple-element.96.o_ref, ...), custom_call_target="tpu_custom_call" | custom-call | tf_op jit(solution)/shard_map/attend_back/pallas_call | solution.py:711
  113.8 145.5 %last_layers.1 = (bf16[256,11264]{1,0:T(8,128)(2,1)}, f32[256,512]{1,0:T(8,128)}) custom-call(bf16[64,2048]{1,0:T(8,128)(2,1)} %get-tuple-element.98.dq_in, bf16[4096,128]{1,0:T(8,128)(2,1)} %get-tuple-element.99.dkv_in, f32[2,32,1024]{2,1,0:T(8,128)} %get-tuple-element.91.small_in, f32[2,32,1024]{2,1,0:T(8,128)} %get-tuple-element.100.small_grads_in, ...), custom_call_target="tpu_custom_call" | custom-call | tf_op jit(solution)/shard_map/last_layers/pallas_call | solution.py:1328
  259.4 8.0 %unpack.1 = (bf16[256,512]{1,0:T(8,128)(2,1)}, f32[256,512]{1,0:T(8,128)}, f32[256,1024]{1,0:T(8,128)}, f32[256,2048]{1,0:T(8,128)}, f32[3,256,256]{2,1,0:T(8,12...) custom-call(bf16[256,512]{1,0:T(8,128)(2,1)} %get-tuple-element.94.o, ...), custom_call_target="tpu_custom_call" | custom-call | tf_op jit(solution)/shard_map/unpack/pallas_call | solution.py:1387

commit v4 on v3

--- a/solution.py
+++ b/solution.py
@@ -17,7 +17,7 @@
 LANES = 128
 ROW_BLOCK = 16
 EDGE = 16
-KEY_TILE = 512
+KEY_TILE = 1024
 BLOCK = 256
 VMEM_MOST = 60 * 1024 * 1024
 
@@ -290,6 +290,8 @@
         q_recv,
         kv_send,
         kv_recv,
+        pass_send,
+        pass_recv,
     ) = refs
     own, core = place()
     parts = count // heads
@@ -485,9 +487,16 @@
 
     q_slot = q_out.at[:, span(head, rows)]
     kv_slot = kv_out.at[span(own, rows), :]
-    for gap, (peer, _) in enumerate(peers):
+    arriving = []
+    for gap in range(1, heads):
+        other = lax.rem(head + gap, heads)
+        arriving.append(
+            push(kv_own.at[:, span(other, LANES)], kv_slot, (kv_send, kv_recv), gap - 1, (other * parts + part, core))
+        )
+    twins = [(head * parts + lax.rem(part + gap, parts), core) for gap in range(1, parts)]
+    for at, twin in enumerate(twins):
         copies.append(
-            push(kv_own.at[:, span(peer // parts, LANES)], kv_slot, (kv_send, kv_recv), gap, (peer, core))
+            push(kv_own.at[:, span(head, LANES)], kv_slot, (pass_send, pass_recv), at * heads, twin)
         )
     for gap in range(1, heads):
         other = lax.rem(head + gap, heads)
@@ -504,6 +513,12 @@
         copy.wait()
     saves.append(move(late, late_out, out_sem.at[12]))
     saves.append(move(early, early_out, out_sem.at[13]))
+    for gap in range(1, heads):
+        arriving[gap - 1].wait()
+        source = lax.rem(head + heads - gap, heads) * parts + part
+        block = kv_out.at[span(source, rows), :]
+        for at, twin in enumerate(twins):
+            copies.append(push(block, block, (pass_send, pass_recv), at * heads + gap, twin))
 
     for copy in row_copies:
         copy.wait()
@@ -526,6 +541,7 @@
 def first_kernel(tokens, seg_row, vectors, weights, count, heads):
     rows = tokens.shape[0]
     ext = rows + 2 * EDGE
+    parts = count // heads
     late = (2 * BLOCK, SMALL)
     early = (2 * BLOCK, EARLY)
     out_shape = (
@@ -583,7 +599,7 @@
         pltpu.SemaphoreType.DMA((15,)),
     ]
     scratch += sem_pair(len(WEIGHT_COLUMNS) + 1) + sem_pair(4) + sem_pair(count - 1)
-    scratch += sem_pair(heads - 1) + sem_pair(count - 1)
+    scratch += sem_pair(heads - 1) + sem_pair(heads - 1) + sem_pair((parts - 1) * heads)
     return pl.pallas_call(
         functools.partial(first_body, count, heads),
         out_shape=out_shape,
@@ -892,8 +908,8 @@
 
 
 def grad_sets(bits):
-    bounds = [LATE, QKV, LEFT, CONV]
-    widths = [EARLY, LEFT - QKV, CONV - LEFT, LATE - CONV]
+    bounds = [LATE, LATE + SHRINK, QKV, LEFT, CONV]
+    widths = [SHRINK, EARLY - SHRINK, LEFT - QKV, CONV - LEFT, LATE - CONV]
     return [column_groups(first, width, bits) for first, width in zip(bounds, widths)]
 
 
@@ -1018,7 +1034,9 @@
         small,
         small_grads,
         dq_t,
-        dkv_parts,
+        dkv_own,
+        shared,
+        summed,
         dqkv,
         sep_own,
         sep_edges,
@@ -1039,6 +1057,8 @@
         dq_recv,
         dkv_send,
         dkv_recv,
+        pass_send,
+        pass_recv,
         edge_send,
         edge_recv,
         ws_send,
@@ -1080,7 +1100,7 @@
     for number, groups in enumerate(grad_sets(bits)):
         members = []
         for group in groups:
-            view = late_view if number else early_view
+            view = late_view if number > 1 else early_view
             members.append(Piece(at, group, links, view, got, total, sems))
             at += 1
         sets.append(members)
@@ -1095,31 +1115,59 @@
         for piece in members:
             piece.advance()
 
-    keep = move(early_grads.at[own_rows, :], early_own, keep_sem.at[2])
-    start(sets[0], early_grads, LATE)
+    keep = move(early_grads.at[own_rows, :], early_own, keep_sem.at[1])
+    start(sets[0] + sets[1], early_grads, LATE)
     slot = dq_t.at[span(head, HEAD_DIM), :]
-    kv_slot = dkv_parts.at[part, :, span(head, LANES)]
+    heads_on = [lax.rem(head + gap, heads) for gap in range(heads)]
+    sharing = []
+    for gap, other in enumerate(heads_on[1:] + heads_on[:1]):
+        for at in range(parts - 1):
+            twin = lax.rem(part + at + 1, parts)
+            sharing.append(
+                push(
+                    dkv_in.at[span(other * parts + twin, rows), :],
+                    shared.at[at, other],
+                    (pass_send, pass_recv),
+                    at * heads + gap,
+                    (head * parts + twin, core),
+                )
+            )
     collect = []
-    for gap, (peer, _) in enumerate(peers):
-        collect.append(push(dkv_in.at[span(peer, rows), :], kv_slot, (dkv_send, dkv_recv), gap, (peer, core)))
-    for gap in range(1, heads):
-        other = lax.rem(head + gap, heads)
+    for gap, other in enumerate(heads_on[1:]):
         collect.append(
-            push(dq_in.at[:, span(other, rows)], slot, (dq_send, dq_recv), gap - 1, (other * parts + part, core))
+            push(dq_in.at[:, span(other, rows)], slot, (dq_send, dq_recv), gap, (other * parts + part, core))
         )
     collect.append(move(dq_in.at[:, span(head, rows)], slot, keep_sem.at[0]))
-    collect.append(move(dkv_in.at[span(own, rows), :], kv_slot, keep_sem.at[1]))
-
     widened(small, small_in)
     small_grads[...] = small_grads_in[...]
     keep.wait()
     advance(sets[0])
+    advance(sets[1])
+    for gap, other in enumerate(heads_on[1:] + heads_on[:1]):
+        for copy in sharing[gap * (parts - 1) : (gap + 1) * (parts - 1)]:
+            copy.wait()
+        total_kv = dkv_in[span(other * parts + part, rows), :].astype(F32)
+        for at in range(parts - 1):
+            total_kv = total_kv + shared[at, other].astype(F32)
+        if gap < heads - 1:
+            summed[other] = total_kv.astype(BF16)
+            collect.append(
+                push(
+                    summed.at[other],
+                    dkv_own.at[:, span(head, LANES)],
+                    (dkv_send, dkv_recv),
+                    gap,
+                    (other * parts + part, core),
+                )
+            )
+        else:
+            dkv_own[:, span(head, LANES)] = total_kv.astype(BF16)
     for copy in loads:
         copy.wait()
     advance(sets[0][:2])
     for copy in collect:
         copy.wait()
-    advance(sets[0])
+    advance(sets[1][:2])
 
     dqkv[:, :D] = turn(dq_t[...])
     lane = lax.broadcasted_iota(jnp.int32, (rows, LANES), 1) < HEAD_DIM
@@ -1127,10 +1175,7 @@
         pair = []
         for side in range(2):
             first = (2 * step + side) * LANES
-            share = dkv_parts[0, :, first : first + LANES].astype(F32)
-            for number in range(1, parts):
-                share = share + dkv_parts[number, :, first : first + LANES].astype(F32)
-            pair.append(share)
+            pair.append(dkv_own[:, first : first + LANES].astype(F32))
         cols = slice(D + step * LANES, D + (step + 1) * LANES)
         dqkv[:, cols] = jnp.where(lane, pair[0], pltpu.roll(pair[1], HEAD_DIM, 1)).astype(BF16)
         cols = slice(2 * D + step * LANES, 2 * D + (step + 1) * LANES)
@@ -1171,7 +1216,8 @@
             turn(depth[:, block * BLOCK : (block + 1) * BLOCK]), sep_own[...]
         ).astype(BF16)
     put_vector(small_grads, POINTB, col_sum(sep_own[...]))
-    start(sets[1], grads, 0)
+    start(sets[2], grads, 0)
+    advance(sets[1])
 
     for copy in edge_copies:
         copy.wait()
@@ -1185,14 +1231,13 @@
             .astype(BF16)
             .astype(F32)
         )
+    advance(sets[2])
     advance(sets[0])
-    advance(sets[1])
 
     row_sums[...] = jnp.zeros_like(row_sums)
     half = FF // 2 // LANES
 
-    @pl.loop(0, FF // LANES)
-    def _(step):
+    def tap_block(step):
         cols = span(step, LANES)
         side, lanes = step // half, span(lax.rem(step, half), LANES)
         block = depth_grad[:, cols]
@@ -1212,6 +1257,10 @@
         row_sums[0] = row_sums[0] + scaled
         row_sums[1] = row_sums[1] + scaled * normed
 
+    pl.loop(0, half)(tap_block)
+    advance(sets[1])
+    advance(sets[2])
+    pl.loop(half, 2 * half)(tap_block)
     advance(sets[0])
     inner = jnp.sum(row_sums[0], axis=1, keepdims=True) * (1.0 / FF)
     cross = jnp.sum(row_sums[1], axis=1, keepdims=True) * (1.0 / FF)
@@ -1228,6 +1277,7 @@
         dleft[:, cols] = low
         small_grads[side, LEFTB : LEFTB + 1, lanes] = col_sum(low)
 
+    advance(sets[1])
     for step in range(HALF // LANES):
         cols = slice(step * LANES, (step + 1) * LANES)
         scaled = g3_grad[:, cols] * small[0, LN3G : LN3G + 1, cols]
@@ -1244,25 +1294,30 @@
         grads[:, LEFT + 512 * step : LEFT + 512 * (step + 1)] = matmul(
             low_t, dleft[:, 512 * step : 512 * (step + 1)]
         ).astype(BF16)
-    start(sets[2], grads, 0)
+    start(sets[3], grads, 0)
+    advance(sets[2])
     advance(sets[0])
-    advance(sets[1])
     for tap in range(3):
         grads[:, CONV + HALF * tap : CONV + HALF * (tap + 1)] = matmul(
             low_t, conv_taps[:, HALF * tap : HALF * (tap + 1)]
         ).astype(BF16)
+    advance(sets[3])
+    advance(sets[1])
     grad = through(dleft[...], LEFT, FF) + through(conv_taps[...], CONV, 3 * HALF)
     dx1 = dx3[...] + norm_step(grad, n2[...], inv[1, mid, :1], LN2G)
     gate = jax.nn.sigmoid(glu_pre[:, D:])
     value_grad = dx1 * gate
     dglu = jnp.concatenate([value_grad, value_grad * glu_pre[:, :D] * (1.0 - gate)], axis=1).astype(BF16)
     put_vector(small_grads, GLUB, col_sum(dglu))
+    advance(sets[0])
     advance(sets[2])
     low_t = turn(n1[...] * vector(small, LN1G, D) + vector(small, LN1B, D))
     for step in range(2):
         grads[:, GLU + D * step : GLU + D * (step + 1)] = matmul(
             low_t, dglu[:, D * step : D * (step + 1)]
         ).astype(BF16)
+    advance(sets[1])
+    advance(sets[3])
     grad = through(dglu, GLU, 2 * D)
     result[...] = dx1 + norm_step(grad, n1[...], inv[0, mid, :1], LN1G)
     keep = move(result, grad_out, keep_sem.at[0])
@@ -1276,7 +1331,7 @@
         grads[first : (side + 1) * BLOCK, SMALL : SMALL + BLOCK] = jnp.zeros(
             ((side + 1) * BLOCK - first, BLOCK), BF16
         )
-    start(sets[3], grads, 0)
+    start(sets[4], grads, 0)
     while not all(piece.done() for members in sets for piece in members):
         for members in sets:
             advance(members)
@@ -1286,6 +1341,7 @@
 def last_kernel(dq, dkv, small, small_grads, tensors, count, heads):
     rows = dkv.shape[0] // count
     ext = rows + 2 * EDGE
+    parts = count // heads
     bits = count.bit_length() - 1
     pieces = sum(len(groups) for groups in grad_sets(bits))
     early = tensors[0].shape
@@ -1305,7 +1361,9 @@
         pltpu.VMEM((2, SMALL_ROWS, SMALL_WIDTH), F32),
         pltpu.VMEM((2, SMALL_ROWS, SMALL_WIDTH), F32),
         pltpu.VMEM((D, rows), BF16),
-        pltpu.VMEM((count // heads, rows, 2 * D), BF16),
+        pltpu.VMEM((rows, 2 * D), BF16),
+        pltpu.VMEM((parts - 1, heads, rows, LANES), BF16),
+        pltpu.VMEM((heads, rows, LANES), BF16),
         pltpu.VMEM((rows, 3 * D), BF16),
         pltpu.VMEM((rows, HALF), BF16),
         pltpu.VMEM((2, EDGE, HALF), BF16),
@@ -1323,7 +1381,8 @@
         pltpu.SemaphoreType.DMA((12,)),
         pltpu.SemaphoreType.DMA((3,)),
     ]
-    scratch += sem_pair(heads - 1) + sem_pair(count - 1) + sem_pair(2) + sem_pair(pieces)
+    scratch += sem_pair(heads - 1) + sem_pair(heads - 1) + sem_pair((parts - 1) * heads)
+    scratch += sem_pair(2) + sem_pair(pieces)
     scratch += sem_pair(pieces * bits) + sem_pair(pieces * bits)
     return pl.pallas_call(
         functools.partial(last_body, count, heads),

time: 268 us -> 245 us (0.914)
  Pallas kernels: 267 us -> 244 us
    pallas_call x1, Pallas kernels: 146 us -> 129 us  [last_kernel(): pl.pallas_call(functools.partial(last_body, count, heads), out_shape=(sha...]
    pallas_call x1, Pallas kernels: 53.2 us -> 42.2 us  [first_kernel(): pl.pallas_call(functools.partial(first_body, count, heads), out_shape=out...]
    pallas_call x1, Pallas kernels: 23.2 us -> 26.7 us  [middle_kernel(): pl.pallas_call(functools.partial(middle_body, count, heads), out_shape=(s...]
where the time goes in v4:
time: 245 us
  Pallas kernels  244 us (100%)
    pallas_call x1, Pallas kernels, last_kernel(): pl.pallas_call(functools.partial(last_body, count, heads), out_shape=(sha...  129 us
    pallas_call x1, Pallas kernels, first_kernel(): pl.pallas_call(functools.partial(first_body, count, heads), out_shape=out...  42.2 us
    pallas_call x1, Pallas kernels, middle_kernel(): pl.pallas_call(functools.partial(middle_body, count, heads), out_shape=(s...  26.7 us
    pallas_call x1, Pallas kernels, attend_back(): pl.pallas_call(functools.partial(attend_back_body, rows), out_shape=(shap...  19.8 us
    pallas_call x1, Pallas kernels, attend(): pl.pallas_call(functools.partial(attend_body, rows), out_shape=(shaped(q_...  18.6 us
    pallas_call x1, Pallas kernels, unpack(): pl.pallas_call(unpack_body, out_shape=(shaped(output.shape, output.dtype)...  7.98 us

profile of v4, /device:TPU:0, one launch (start us, length us, event | category | flops | bytes accessed | tf_op | source)
XLA Modules:
  0.0 245.1 jit_solution(5508333220186254941)
XLA Ops:
  0.7 42.2 %first_layers.1 = (bf16[512,6400]{1,0:T(8,128)(2,1)}, bf16[512,4608]{1,0:T(8,128)(2,1)}, f32[2,32,1024]{2,1,0:T(8,128)}, s32[16,1,256]{2,1,0:T(1,128)}, s32[8,12...) custom-call(bf16[256,512]{1,0:T(8,128)(2,1)} %bitcast.38, ...), custom_call_target="tpu_custom_call" | custom-call | tf_op jit(solution)/shard_map/first_layers/pallas_call | solution.py:603
  42.9 18.6 %attend.1 = (f32[64,2048]{1,0:T(8,128)}, bf16[64,2048]{1,0:T(8,128)(2,1)}, f32[1,2048]{1,0:T(1,128)}) custom-call(s32[8,128]{1,0:T(8,128)} %get-tuple-element.86.plan_ref, bf16[64,2048]{1,0:T(8,128)(2,1)} %get-tuple-element.87.q_ref, bf16[4096,128]{1,0:T(8,128)(2,1)} %get-tuple-element.88.kv_ref, s32[16,1,256]{2,1,0:T(1,128)} %get-tuple-element.89.seg_ref), custom_call_target="tpu_custom_call" | custom-call | tf_op jit(solution)/shard_map/attend/pallas_call | solution.py:678
  61.4 26.7 %middle_layers.1 = (bf16[256,512]{1,0:T(8,128)(2,1)}, f32[2,32,1024]{2,1,0:T(8,128)}, f32[256,512]{1,0:T(8,128)}, bf16[512,4608]{1,0:T(8,128)(2,1)}, bf16[64,2048]{1,0:T(8,128)(2,1)}) custom-call(bf16[64,2048]{1,0:T(8,128)(2,1)} %get-tuple-element.90.o_in, bf16[256,512]{1,0:T(8,128)(2,1)} %bitcast.39, f32[2,32,1024]{2,1,0:T(8,128)} %get-tuple-element.91.small_in, ...), custom_call_target="tpu_custom_call" | custom-call | tf_op jit(solution)/shard_map/middle_layers/pallas_call | solution.py:862
  88.1 19.8 %attend_back.1 = (bf16[64,2048]{1,0:T(8,128)(2,1)}, bf16[4096,128]{1,0:T(8,128)(2,1)}) custom-call(s32[8,128]{1,0:T(8,128)} %get-tuple-element.86.plan_ref, bf16[64,2048]{1,0:T(8,128)(2,1)} %get-tuple-element.87.q_ref, bf16[64,2048]{1,0:T(8,128)(2,1)} %get-tuple-element.95.do_ref, f32[64,2048]{1,0:T(8,128)} %get-tuple-element.96.o_ref, ...), custom_call_target="tpu_custom_call" | custom-call | tf_op jit(solution)/shard_map/attend_back/pallas_call | solution.py:727
  107.9 129.0 %last_layers.1 = (bf16[256,11264]{1,0:T(8,128)(2,1)}, f32[256,512]{1,0:T(8,128)}) custom-call(bf16[64,2048]{1,0:T(8,128)(2,1)} %get-tuple-element.98.dq_in, bf16[4096,128]{1,0:T(8,128)(2,1)} %get-tuple-element.99.dkv_in, f32[2,32,1024]{2,1,0:T(8,128)} %get-tuple-element.91.small_in, f32[2,32,1024]{2,1,0:T(8,128)} %get-tuple-element.100.small_grads_in, ...), custom_call_target="tpu_custom_call" | custom-call | tf_op jit(solution)/shard_map/last_layers/pallas_call | solution.py:1387
  236.9 8.0 %unpack.1 = (bf16[256,512]{1,0:T(8,128)(2,1)}, f32[256,512]{1,0:T(8,128)}, f32[256,1024]{1,0:T(8,128)}, f32[256,2048]{1,0:T(8,128)}, f32[3,256,256]{2,1,0:T(8,12...) custom-call(bf16[256,512]{1,0:T(8,128)(2,1)} %get-tuple-element.94.o, ...), custom_call_target="tpu_custom_call" | custom-call | tf_op jit(solution)/shard_map/unpack/pallas_call | solution.py:1446

commit v5 on v4

--- a/solution.py
+++ b/solution.py
@@ -201,6 +201,20 @@
         out_ref[here, :] = jnp.broadcast_to(part, (LANES, LANES)).T
 
 
+def mark_segments(marks, columns, seg_ref):
+    count, _, rows = seg_ref.shape
+
+    @pl.loop(0, count)
+    def _(source):
+        row = seg_ref[source].astype(F32)
+        for step in range(rows // LANES):
+            part = jnp.broadcast_to(row[:, step * LANES : (step + 1) * LANES], (LANES, LANES)).T
+            number = lax.broadcasted_iota(jnp.int32, (LANES, LANES), 1).astype(F32)
+            here = pl.ds(bound(source * rows + step * LANES, LANES), LANES)
+            columns[here, :] = part
+            marks[here, :] = jnp.where(part == number, 1.0, 0.0).astype(BF16)
+
+
 WEIGHT_COLUMNS = [
     (0, GLU, 1024, 1, False),
     (1, LEFT, 2048, 1, False),
@@ -229,7 +243,7 @@
 ):
     vectors, refs = refs[: len(VECTORS)], refs[len(VECTORS) :]
     weights, refs = refs[:8], refs[8:]
-    outs, refs = refs[:18], refs[18:]
+    outs, refs = refs[:19], refs[19:]
     (
         late_out,
         early_out,
@@ -249,6 +263,7 @@
         x2_out,
         inv_out,
         masks_out,
+        seg_out,
     ) = outs
     (
         staged,
@@ -278,6 +293,8 @@
         inv,
         q_turned,
         kv_own,
+        marks,
+        columns,
         load_sem,
         out_sem,
         ws_send,
@@ -313,18 +330,22 @@
             elif blocks > 1:
                 source = source.at[pl.ds(block * BLOCK, BLOCK), :]
             loads.append(
-                move(
+                pltpu.make_async_copy(
                     source,
                     staged.at[:, pl.ds(column, width)],
                     load_sem.at[len(loads)],
                 )
             )
+            if number < 3:
+                loads[-1].start()
             column += width
     small_own[...] = jnp.zeros_like(small_own)
     for (row, tall, size), vector_ref in zip(VECTORS, vectors):
         small_own[row : row + tall, :size] = vector_ref[...]
     turned_segments(seg_col, 0, seg_row_ref[...])
     greet([sibling] + peers)
+    for load in loads[5:]:
+        load.start()
 
     copies = []
     right, left = (lax.rem(own + 1, count), core), (lax.rem(own + count - 1, count), core)
@@ -486,7 +507,7 @@
         ).astype(BF16)
 
     q_slot = q_out.at[:, span(head, rows)]
-    kv_slot = kv_out.at[span(own, rows), :]
+    kv_slot = kv_out.at[span(own, rows), pl.ds(0, LANES)]
     arriving = []
     for gap in range(1, heads):
         other = lax.rem(head + gap, heads)
@@ -509,17 +530,6 @@
     saves.append(move(x2, x2_out, out_sem.at[10]))
     saves.append(move(inv, inv_out, out_sem.at[11]))
     saves.append(move(masks, masks_out, out_sem.at[14]))
-    for copy in weight_copies[5:]:
-        copy.wait()
-    saves.append(move(late, late_out, out_sem.at[12]))
-    saves.append(move(early, early_out, out_sem.at[13]))
-    for gap in range(1, heads):
-        arriving[gap - 1].wait()
-        source = lax.rem(head + heads - gap, heads) * parts + part
-        block = kv_out.at[span(source, rows), :]
-        for at, twin in enumerate(twins):
-            copies.append(push(block, block, (pass_send, pass_recv), at * heads + gap, twin))
-
     for copy in row_copies:
         copy.wait()
     lane = lax.broadcasted_iota(jnp.int32, (1, LANES), 1)
@@ -534,6 +544,20 @@
         plan_out[tile : tile + 1, :] = jnp.where(
             lane == 0, below, jnp.where(lane == 1, upto, source)
         )
+    mark_segments(marks, columns, seg_all)
+    saves.append(move(columns, seg_out, out_sem.at[16]))
+    saves.append(move(marks, kv_out.at[:, pl.ds(LANES, LANES)], out_sem.at[15]))
+    for copy in weight_copies[5:]:
+        copy.wait()
+    saves.append(move(late, late_out, out_sem.at[12]))
+    saves.append(move(early, early_out, out_sem.at[13]))
+    for gap in range(1, heads):
+        arriving[gap - 1].wait()
+        source = lax.rem(head + heads - gap, heads) * parts + part
+        block = kv_out.at[span(source, rows), pl.ds(0, LANES)]
+        for at, twin in enumerate(twins):
+            copies.append(push(block, block, (pass_send, pass_recv), at * heads + gap, twin))
+
     for copy in copies + saves:
         copy.wait()
 
@@ -551,7 +575,7 @@
         shaped((count, 1, rows), jnp.int32),
         shaped((heads, LANES), jnp.int32),
         shaped((HEAD_DIM, heads * rows), BF16),
-        shaped((count * rows, LANES), BF16),
+        shaped((count * rows, 2 * LANES), BF16),
         shaped((rows, D)),
         shaped((rows, 2 * D)),
         shaped((rows, D)),
@@ -563,9 +587,10 @@
         shaped((rows, D)),
         shaped((4, ext, LANES)),
         shaped((TAPS, ext, LANES)),
+        shaped((count * rows, LANES)),
     )
     out_specs = (
-        [any_spec()] * 2 + [vmem_spec()] * 3 + [any_spec()] * 13
+        [any_spec()] * 2 + [vmem_spec()] * 3 + [any_spec()] * 14
     )
     scratch = [
         pltpu.VMEM((BLOCK, SMALL + EARLY), F32),
@@ -595,8 +620,10 @@
         pltpu.VMEM((4, ext, LANES), F32),
         pltpu.VMEM((D, rows), BF16),
         pltpu.VMEM((rows, 2 * D), BF16),
+        pltpu.VMEM((count * rows, LANES), BF16),
+        pltpu.VMEM((count * rows, LANES), F32),
         pltpu.SemaphoreType.DMA((sum(item[3] for item in WEIGHT_COLUMNS),)),
-        pltpu.SemaphoreType.DMA((15,)),
+        pltpu.SemaphoreType.DMA((17,)),
     ]
     scratch += sem_pair(len(WEIGHT_COLUMNS) + 1) + sem_pair(4) + sem_pair(count - 1)
     scratch += sem_pair(heads - 1) + sem_pair(heads - 1) + sem_pair((parts - 1) * heads)
@@ -615,41 +642,32 @@
     @pl.loop(0, kv_ref.shape[0] // KEY_TILE)
     def _(tile):
         here = span(tile, KEY_TILE)
-        turned[:, here] = turn(kv_ref[here, :])
-
-
-def key_segments(seg_ref, segk):
-    count, _, rows = seg_ref.shape
-
-    @pl.loop(0, count)
-    def _(source):
-        turned_segments(segk, source * rows, seg_ref[source])
-
-
-def masked(scores, segk, here, seg_q):
-    seg_k = jnp.concatenate([segk[here, :]] * (scores.shape[1] // LANES), axis=1)
-    return jnp.where(seg_k == seg_q, scores, MASK_FILL)
+        turned[:, here] = turn(kv_ref[here, :LANES])
+
+
+def other_segments(seg_q):
+    number = lax.broadcasted_iota(jnp.int32, (LANES, seg_q.shape[1]), 0)
+    return jnp.where(number == seg_q, 0.0, MASK_FILL).astype(BF16)
 
 
 def key_tiles(plan_ref, tile):
     return plan_ref[tile, 0] // KEY_TILE, (plan_ref[tile, 1] + KEY_TILE - 1) // KEY_TILE
 
 
-def attend_body(rows, plan_ref, q_ref, kv_ref, seg_ref, o_ref, low_ref, lse_ref, turned, segk):
+def attend_body(rows, plan_ref, q_ref, kv_ref, seg_ref, o_ref, low_ref, lse_ref, turned):
     turn_keys(kv_ref, turned)
-    key_segments(seg_ref, segk)
 
     @pl.loop(0, q_ref.shape[1] // rows)
     def _(tile):
         at = span(tile, rows)
         q = q_ref[:, at] * jnp.bfloat16(HEAD_DIM**-0.5)
-        q_pad = jnp.concatenate([q, jnp.zeros_like(q)], axis=0)
-        seg_q = seg_ref[plan_ref[tile, 2]].astype(F32)
+        others = other_segments(seg_ref[plan_ref[tile, 2]])
+        q_pad = jnp.concatenate([q, jnp.zeros_like(q), others], axis=0)
 
         def block(key_tile, carry):
             top, total, acc = carry
             here = span(key_tile, KEY_TILE)
-            scores = masked(matmul(kv_ref[here, :], q_pad), segk, here, seg_q)
+            scores = matmul(kv_ref[here, :], q_pad)
             new_top = jnp.maximum(top, jnp.max(scores, axis=0, keepdims=True))
             probs = jnp.exp(scores - new_top)
             shrink = jnp.exp(top - new_top)
@@ -680,18 +698,23 @@
         out_shape=(shaped(q_t.shape), shaped(q_t.shape, BF16), shaped((1, q_t.shape[1]))),
         in_specs=[smem_spec()] + [vmem_spec()] * 3,
         out_specs=(vmem_spec(),) * 3,
-        scratch_shapes=[pltpu.VMEM(kv.shape[::-1], BF16), pltpu.VMEM(kv.shape, F32)],
+        scratch_shapes=[pltpu.VMEM((LANES, kv.shape[0]), BF16)],
         compiler_params=pltpu.CompilerParams(vmem_limit_bytes=VMEM_MOST),
         name="attend",
     )(plan, q_t, kv, seg)
 
 
 def attend_back_body(
-    rows, plan_ref, q_ref, do_ref, o_ref, lse_ref, kv_ref, seg_ref, dq_ref, dkv_ref, turned, segk, dkv_acc
+    rows, plan_ref, q_ref, do_ref, o_ref, lse_ref, seg_ref, kv_in, seg_in, dq_ref, dkv_ref, kv_ref, segk, turned, dkv_acc, sems
 ):
+    loads = [
+        move(kv_in.at[:, pl.ds(0, LANES)], kv_ref, sems.at[0]),
+        move(seg_in, segk, sems.at[1]),
+    ]
+    dkv_acc[...] = jnp.zeros_like(dkv_acc)
+    loads[0].wait()
     turn_keys(kv_ref, turned)
-    key_segments(seg_ref, segk)
-    dkv_acc[...] = jnp.zeros_like(dkv_acc)
+    loads[1].wait()
     scale = HEAD_DIM**-0.5
 
     @pl.loop(0, q_ref.shape[1] // rows)
@@ -710,7 +733,9 @@
         def block(key_tile, dq):
             here = span(key_tile, KEY_TILE)
             pair = matmul(kv_ref[here, :], both)
-            probs = jnp.exp(masked(pair[:, :rows], segk, here, seg_q) - lse)
+            seg_k = jnp.concatenate([segk[here, :]] * (rows // LANES), axis=1)
+            scores = jnp.where(seg_k == seg_q, pair[:, :rows], MASK_FILL)
+            probs = jnp.exp(scores - lse)
             score_grad = (probs * (pair[:, rows:] - delta)).astype(BF16)
             joined = jnp.concatenate([score_grad, probs.astype(BF16)], axis=1)
             dkv_acc[here, :] += back_mul(joined, both)
@@ -723,27 +748,29 @@
     dkv_ref[...] = dkv_acc[...].astype(BF16)
 
 
-def attend_back(plan, q_t, do_t, o_t, lse, kv, seg, rows):
+def attend_back(plan, q_t, do_t, o_t, lse, seg, kv, seg_cols, rows):
     return pl.pallas_call(
         functools.partial(attend_back_body, rows),
-        out_shape=(shaped(q_t.shape, BF16), shaped(kv.shape, BF16)),
-        in_specs=[smem_spec()] + [vmem_spec()] * 6,
+        out_shape=(shaped(q_t.shape, BF16), shaped((kv.shape[0], LANES), BF16)),
+        in_specs=[smem_spec()] + [vmem_spec()] * 5 + [any_spec()] * 2,
         out_specs=(vmem_spec(),) * 2,
         scratch_shapes=[
-            pltpu.VMEM(kv.shape[::-1], BF16),
-            pltpu.VMEM(kv.shape, F32),
-            pltpu.VMEM(kv.shape, F32),
+            pltpu.VMEM((kv.shape[0], LANES), BF16),
+            pltpu.VMEM((kv.shape[0], LANES), F32),
+            pltpu.VMEM((LANES, kv.shape[0]), BF16),
+            pltpu.VMEM((kv.shape[0], LANES), F32),
+            pltpu.SemaphoreType.DMA((2,)),
         ],
         compiler_params=pltpu.CompilerParams(vmem_limit_bytes=VMEM_MOST),
         name="attend_back",
-    )(plan, q_t, do_t, o_t, lse, kv, seg)
+    )(plan, q_t, do_t, o_t, lse, seg, kv, seg_cols)
 
 
 def middle_body(
     count,
     heads,
     o_in,
-    out_grad,
+    out_grad_in,
     small_in,
     x2_in,
     early_in,
@@ -752,6 +779,8 @@
     dx3_out,
     grads_out,
     do_out,
+    out_grad,
+    small_raw,
     weights,
     x2,
     small,
@@ -773,18 +802,26 @@
     parts = count // heads
     head, part = own // parts, lax.rem(own, parts)
     rows = out_grad.shape[0]
-    loads = [move(early_in, weights, load_sem.at[0]), move(x2_in, x2, load_sem.at[1])]
+    slot = o_t.at[span(head, HEAD_DIM), :]
+    loads = [
+        move(o_in.at[:, span(head, rows)], slot, load_sem.at[2]),
+        move(small_in, small_raw, load_sem.at[3]),
+        move(x2_in, x2, load_sem.at[1]),
+        move(early_in, weights, load_sem.at[0]),
+        move(out_grad_in, out_grad, load_sem.at[4]),
+    ]
     near = [lax.rem(head + gap, heads) for gap in range(1, heads)]
     peers = [(other * parts + part, core) for other in near]
     greet(peers)
     copies = [
-        push(o_in.at[:, span(other, rows)], o_t.at[span(head, HEAD_DIM), :], (o_send, o_recv), gap, peer)
+        push(o_in.at[:, span(other, rows)], slot, (o_send, o_recv), gap, peer)
         for gap, (other, peer) in enumerate(zip(near, peers))
     ]
-    copies.append(move(o_in.at[:, span(head, rows)], o_t.at[span(head, HEAD_DIM), :], load_sem.at[2]))
-    widened(small, small_in)
     small_grads[...] = jnp.zeros_like(small_grads)
-    for copy in copies + loads:
+    for copy in loads:
+        copy.wait()
+    widened(small, small_raw)
+    for copy in copies:
         copy.wait()
 
     state = (
@@ -841,16 +878,16 @@
     put_vector(small_grads, ATTNB, col_sum(dy3))
     put_vector(small_grads, EXPANDB, col_sum(dpre[...]))
     put_vector(small_grads, SHRINKB, col_sum(dz))
+    for block in range(FF // BLOCK):
+        side, column = block // 4, SHRINK + D * (block % 4)
+        grads[side * BLOCK : (side + 1) * BLOCK, column : column + D] = matmul(
+            turn(hidden[:, block * BLOCK : (block + 1) * BLOCK]), dz
+        ).astype(BF16)
     grads[:, ATTN : ATTN + D] = matmul(o_t[...], dy3).astype(BF16)
     low_t = turn(low)
     for step in range(FF // 512):
         grads[:, EXPAND + 512 * step : EXPAND + 512 * (step + 1)] = matmul(
             low_t, dpre[:, 512 * step : 512 * (step + 1)]
-        ).astype(BF16)
-    for block in range(FF // BLOCK):
-        side, column = block // 4, SHRINK + D * (block % 4)
-        grads[side * BLOCK : (side + 1) * BLOCK, column : column + D] = matmul(
-            turn(hidden[:, block * BLOCK : (block + 1) * BLOCK]), dz
         ).astype(BF16)
     copies.append(move(grads, grads_out, load_sem.at[2]))
     for copy in copies:
@@ -868,9 +905,11 @@
             shaped(early.shape, BF16),
             shaped((HEAD_DIM, heads * rows), BF16),
         ),
-        in_specs=[vmem_spec()] * 3 + [any_spec()] * 2,
+        in_specs=[any_spec()] * 5,
         out_specs=[vmem_spec()] * 2 + [any_spec()] * 3,
         scratch_shapes=[
+            pltpu.VMEM((rows, D), BF16),
+            pltpu.VMEM((2, SMALL_ROWS, SMALL_WIDTH), F32),
             pltpu.VMEM(early.shape, BF16),
             pltpu.VMEM((rows, D), F32),
             pltpu.VMEM((2, SMALL_ROWS, SMALL_WIDTH), F32),
@@ -882,7 +921,7 @@
             pltpu.VMEM((D, rows), BF16),
             pltpu.VMEM(early.shape, BF16),
             pltpu.VMEM((rows, D), F32),
-            pltpu.SemaphoreType.DMA((3,)),
+            pltpu.SemaphoreType.DMA((5,)),
         ]
         + sem_pair(heads - 1)
         + sem_pair(heads - 1),
@@ -902,14 +941,16 @@
     ]
     groups = []
     for size, order in zip([long, long, tiles - 2 * long], orders):
+        if size == 0:
+            continue
         groups.append((first, size * LANES, order))
         first += size * LANES
     return groups
 
 
 def grad_sets(bits):
-    bounds = [LATE, LATE + SHRINK, QKV, LEFT, CONV]
-    widths = [SHRINK, EARLY - SHRINK, LEFT - QKV, CONV - LEFT, LATE - CONV]
+    bounds = [LATE, LATE + SHRINK, QKV, POINT, LEFT, LEFT + FF // 2, CONV, CONV + FF // 2]
+    widths = [SHRINK, EARLY - SHRINK, POINT - QKV, LEFT - POINT] + [FF // 2] * 4
     return [column_groups(first, width, bits) for first, width in zip(bounds, widths)]
 
 
@@ -919,6 +960,7 @@
         self.core, self.sibling, self.bit_of, self.partner = links
         self.view, self.got, self.total, self.sems = sums, got, total, sems
         self.bits, self.phase, self.trail = len(self.order), 0, []
+        self.since = -1
         self.copy = None
 
     def whole(self):
@@ -980,6 +1022,9 @@
     def done(self):
         return self.phase > 2 * self.bits
 
+    def sent_all(self):
+        return self.phase >= 2 * self.bits
+
     def advance(self):
         if self.done():
             return
@@ -1002,8 +1047,12 @@
         self.phase += 1
 
 
-def last_body(count, heads, dq_in, dkv_in, small_in, small_grads_in, *refs):
+def last_body(count, heads, *refs):
     (
+        dq_in,
+        dkv_in,
+        small_in,
+        small_grads_in,
         early_grads,
         dx3_in,
         late_in,
@@ -1017,8 +1066,9 @@
         n4_in,
         inv_in,
         masks_in,
+        total_out,
+        grad_out,
         total,
-        grad_out,
         weights,
         dx3,
         n1,
@@ -1035,6 +1085,8 @@
         small_grads,
         dq_t,
         dkv_own,
+        dkv_mine,
+        small_raw,
         shared,
         summed,
         dqkv,
@@ -1053,6 +1105,7 @@
         result,
         load_sem,
         keep_sem,
+        store_sem,
         dq_send,
         dq_recv,
         dkv_send,
@@ -1080,8 +1133,17 @@
 
     sources = (dx3_in, late_in, n4_in, inv_in, depth_in, masks_in, n3_in, left_in, conv_in, n2_in, glu_in, n1_in)
     targets = (dx3, weights, n4, inv, depth, masks, n3, left_pre, conv_pre, n2, glu_pre, n1)
+    slot = dq_t.at[span(head, HEAD_DIM), :]
+    own_rows = pl.ds(bound(core * BLOCK, BLOCK), BLOCK)
+    keeps = [
+        move(dkv_in.at[:, part], dkv_mine, keep_sem.at[2]),
+        move(early_grads.at[own_rows, :], early_own, keep_sem.at[1]),
+        move(dq_in.at[:, span(head, rows)], slot, keep_sem.at[0]),
+        move(small_in, small_raw, keep_sem.at[3]),
+        move(small_grads_in, small_grads, keep_sem.at[4]),
+    ]
+    greet([sibling] + peers)
     loads = [move(a, b, load_sem.at[at]) for at, (a, b) in enumerate(zip(sources, targets))]
-    greet([sibling] + peers)
 
     bit_of = [lax.rem(own // 2**bit, 2) for bit in range(bits)]
     partner = [(own + 2**bit - 2 * 2**bit * bit_of[bit], core) for bit in range(bits)]
@@ -1105,7 +1167,6 @@
             at += 1
         sets.append(members)
     other_rows = pl.ds(bound((1 - core) * BLOCK, BLOCK), BLOCK)
-    own_rows = pl.ds(bound(core * BLOCK, BLOCK), BLOCK)
 
     def start(members, source, shift):
         for piece in members:
@@ -1115,9 +1176,7 @@
         for piece in members:
             piece.advance()
 
-    keep = move(early_grads.at[own_rows, :], early_own, keep_sem.at[1])
     start(sets[0] + sets[1], early_grads, LATE)
-    slot = dq_t.at[span(head, HEAD_DIM), :]
     heads_on = [lax.rem(head + gap, heads) for gap in range(heads)]
     sharing = []
     for gap, other in enumerate(heads_on[1:] + heads_on[:1]):
@@ -1125,7 +1184,7 @@
             twin = lax.rem(part + at + 1, parts)
             sharing.append(
                 push(
-                    dkv_in.at[span(other * parts + twin, rows), :],
+                    dkv_in.at[other, twin],
                     shared.at[at, other],
                     (pass_send, pass_recv),
                     at * heads + gap,
@@ -1137,16 +1196,14 @@
         collect.append(
             push(dq_in.at[:, span(other, rows)], slot, (dq_send, dq_recv), gap, (other * parts + part, core))
         )
-    collect.append(move(dq_in.at[:, span(head, rows)], slot, keep_sem.at[0]))
-    widened(small, small_in)
-    small_grads[...] = small_grads_in[...]
-    keep.wait()
-    advance(sets[0])
-    advance(sets[1])
+    for copy in keeps:
+        copy.wait()
+    widened(small, small_raw)
+    advance(sets[0] + sets[1])
     for gap, other in enumerate(heads_on[1:] + heads_on[:1]):
         for copy in sharing[gap * (parts - 1) : (gap + 1) * (parts - 1)]:
             copy.wait()
-        total_kv = dkv_in[span(other * parts + part, rows), :].astype(F32)
+        total_kv = dkv_mine[other].astype(F32)
         for at in range(parts - 1):
             total_kv = total_kv + shared[at, other].astype(F32)
         if gap < heads - 1:
@@ -1162,12 +1219,15 @@
             )
         else:
             dkv_own[:, span(head, LANES)] = total_kv.astype(BF16)
+        if gap == heads // 2:
+            advance(sets[0][1:])
+    advance(sets[1][1:])
     for copy in loads:
         copy.wait()
-    advance(sets[0][:2])
+    advance(sets[0][:1])
     for copy in collect:
         copy.wait()
-    advance(sets[1][:2])
+    advance(sets[1][:1])
 
     dqkv[:, :D] = turn(dq_t[...])
     lane = lax.broadcasted_iota(jnp.int32, (rows, LANES), 1) < HEAD_DIM
@@ -1210,14 +1270,15 @@
         grads[:, QKV + D * step : QKV + D * (step + 1)] = matmul(
             low_t, dqkv[:, D * step : D * (step + 1)]
         ).astype(BF16)
+    start(sets[2], grads, 0)
     for block in range(FF // BLOCK):
         side, column = block // 4, POINT + HALF * (block % 4)
         grads[side * BLOCK : (side + 1) * BLOCK, column : column + HALF] = matmul(
             turn(depth[:, block * BLOCK : (block + 1) * BLOCK]), sep_own[...]
         ).astype(BF16)
+    start(sets[3], grads, 0)
+    advance(sets[1])
     put_vector(small_grads, POINTB, col_sum(sep_own[...]))
-    start(sets[2], grads, 0)
-    advance(sets[1])
 
     for copy in edge_copies:
         copy.wait()
@@ -1231,9 +1292,9 @@
             .astype(BF16)
             .astype(F32)
         )
+
     advance(sets[2])
     advance(sets[0])
-
     row_sums[...] = jnp.zeros_like(row_sums)
     half = FF // 2 // LANES
 
@@ -1257,18 +1318,17 @@
         row_sums[0] = row_sums[0] + scaled
         row_sums[1] = row_sums[1] + scaled * normed
 
-    pl.loop(0, half)(tap_block)
-    advance(sets[1])
-    advance(sets[2])
-    pl.loop(half, 2 * half)(tap_block)
-    advance(sets[0])
+    for quarter, turns in enumerate(
+        (sets[1] + sets[3], sets[0] + sets[2], sets[1] + sets[3], sets[0] + sets[2])
+    ):
+        pl.loop(quarter * half // 2, (quarter + 1) * half // 2)(tap_block)
+        advance(turns)
     inner = jnp.sum(row_sums[0], axis=1, keepdims=True) * (1.0 / FF)
     cross = jnp.sum(row_sums[1], axis=1, keepdims=True) * (1.0 / FF)
     row_sums[0] = jnp.broadcast_to(inner, (ext, LANES))
     row_sums[1] = jnp.broadcast_to(cross, (ext, LANES))
 
-    @pl.loop(0, FF // LANES)
-    def _(step):
+    def left_block(step):
         cols = span(step, LANES)
         side, lanes = step // half, span(lax.rem(step, half), LANES)
         scaled = g3_grad[mid, cols] * small[side, LN3G : LN3G + 1, lanes]
@@ -1277,7 +1337,10 @@
         dleft[:, cols] = low
         small_grads[side, LEFTB : LEFTB + 1, lanes] = col_sum(low)
 
+    pl.loop(0, half)(left_block)
     advance(sets[1])
+    pl.loop(half, 2 * half)(left_block)
+    advance(sets[3] + sets[0])
     for step in range(HALF // LANES):
         cols = slice(step * LANES, (step + 1) * LANES)
         scaled = g3_grad[:, cols] * small[0, LN3G : LN3G + 1, cols]
@@ -1294,30 +1357,30 @@
         grads[:, LEFT + 512 * step : LEFT + 512 * (step + 1)] = matmul(
             low_t, dleft[:, 512 * step : 512 * (step + 1)]
         ).astype(BF16)
-    start(sets[3], grads, 0)
+        if step % 2:
+            start(sets[4 + step // 2], grads, 0)
     advance(sets[2])
-    advance(sets[0])
+    advance(sets[1])
     for tap in range(3):
         grads[:, CONV + HALF * tap : CONV + HALF * (tap + 1)] = matmul(
             low_t, conv_taps[:, HALF * tap : HALF * (tap + 1)]
         ).astype(BF16)
-    advance(sets[3])
-    advance(sets[1])
+    advance(sets[4] + sets[5])
     grad = through(dleft[...], LEFT, FF) + through(conv_taps[...], CONV, 3 * HALF)
     dx1 = dx3[...] + norm_step(grad, n2[...], inv[1, mid, :1], LN2G)
     gate = jax.nn.sigmoid(glu_pre[:, D:])
     value_grad = dx1 * gate
     dglu = jnp.concatenate([value_grad, value_grad * glu_pre[:, :D] * (1.0 - gate)], axis=1).astype(BF16)
     put_vector(small_grads, GLUB, col_sum(dglu))
+    advance(sets[3])
     advance(sets[0])
-    advance(sets[2])
     low_t = turn(n1[...] * vector(small, LN1G, D) + vector(small, LN1B, D))
     for step in range(2):
         grads[:, GLU + D * step : GLU + D * (step + 1)] = matmul(
             low_t, dglu[:, D * step : D * (step + 1)]
         ).astype(BF16)
-    advance(sets[1])
-    advance(sets[3])
+    start(sets[6], grads, 0)
+    advance(sets[1] + sets[2])
     grad = through(dglu, GLU, 2 * D)
     result[...] = dx1 + norm_step(grad, n1[...], inv[0, mid, :1], LN1G)
     keep = move(result, grad_out, keep_sem.at[0])
@@ -1331,10 +1394,23 @@
         grads[first : (side + 1) * BLOCK, SMALL : SMALL + BLOCK] = jnp.zeros(
             ((side + 1) * BLOCK - first, BLOCK), BF16
         )
-    start(sets[4], grads, 0)
-    while not all(piece.done() for members in sets for piece in members):
-        for members in sets:
-            advance(members)
+    start(sets[7], grads, 0)
+    advance(sets[4] + sets[5])
+    pieces = [piece for number in (0, 3, 1, 2, 6, 7, 4, 5) for piece in sets[number]]
+    stores, rounds = [], 0
+    while not all(piece.done() for piece in pieces):
+        last = all(piece.sent_all() for piece in pieces)
+        for piece in pieces:
+            if not piece.sent_all():
+                piece.advance()
+                piece.since = rounds
+            elif not piece.done() and (last or piece.since < rounds - 1):
+                piece.advance()
+                cols = pl.ds(piece.first, piece.width)
+                stores.append(move(total.at[:, cols], total_out.at[:, cols], store_sem.at[piece.at]))
+        rounds += 1
+    for copy in stores:
+        copy.wait()
     keep.wait()
 
 
@@ -1344,8 +1420,8 @@
     parts = count // heads
     bits = count.bit_length() - 1
     pieces = sum(len(groups) for groups in grad_sets(bits))
-    early = tensors[0].shape
     scratch = [
+        pltpu.VMEM((BLOCK, WIDTH), BF16),
         pltpu.VMEM(tensors[2].shape, BF16),
         pltpu.VMEM((rows, D), F32),
         pltpu.VMEM((rows, D), F32),
@@ -1362,6 +1438,8 @@
         pltpu.VMEM((2, SMALL_ROWS, SMALL_WIDTH), F32),
         pltpu.VMEM((D, rows), BF16),
         pltpu.VMEM((rows, 2 * D), BF16),
+        pltpu.VMEM((heads, rows, LANES), BF16),
+        pltpu.VMEM((2, SMALL_ROWS, SMALL_WIDTH), F32),
         pltpu.VMEM((parts - 1, heads, rows, LANES), BF16),
         pltpu.VMEM((heads, rows, LANES), BF16),
         pltpu.VMEM((rows, 3 * D), BF16),
@@ -1379,7 +1457,8 @@
         pltpu.VMEM((BLOCK + ROW_BLOCK * max(0, bits - 4), WIDTH), BF16),
         pltpu.VMEM((rows, D), F32),
         pltpu.SemaphoreType.DMA((12,)),
-        pltpu.SemaphoreType.DMA((3,)),
+        pltpu.SemaphoreType.DMA((5,)),
+        pltpu.SemaphoreType.DMA((pieces,)),
     ]
     scratch += sem_pair(heads - 1) + sem_pair(heads - 1) + sem_pair((parts - 1) * heads)
     scratch += sem_pair(2) + sem_pair(pieces)
@@ -1387,17 +1466,17 @@
     return pl.pallas_call(
         functools.partial(last_body, count, heads),
         out_shape=(shaped((BLOCK, WIDTH), BF16), shaped((rows, D))),
-        in_specs=[vmem_spec()] * 4 + [any_spec()] * len(tensors),
-        out_specs=[vmem_spec(), any_spec()],
+        in_specs=[any_spec()] * (4 + len(tensors)),
+        out_specs=[any_spec(), any_spec()],
         scratch_shapes=scratch,
         compiler_params=comm_params(3),
         name="last_layers",
-    )(dq, dkv, small, small_grads, *tensors)
+    )(dq, dkv.reshape(heads, parts, rows, LANES), small, small_grads, *tensors)
 
 
 def unpack_body(output_in, grad_in, packed_in, *refs):
     size = len(MATRICES) + len(VECTORS) + 2
-    outs, (packed, *stages, load_sem, out_sem) = refs[:size], refs[size:]
+    outs, (packed, output, grad, *stages, load_sem, out_sem) = refs[:size], refs[size:]
     output_ref, grad_ref, *outs = outs
     order = [len(MATRICES)] + list(range(len(MATRICES)))
     bounds = [(first, width * blocks) for first, width, blocks in MATRICES] + [(SMALL, BLOCK)]
@@ -1405,25 +1484,31 @@
     for at in order:
         cols = pl.ds(*bounds[at])
         loads[at] = move(packed_in.at[:, cols], packed.at[:, cols], load_sem.at[at])
-    stores = [
-        move(output_in, output_ref, out_sem.at[len(MATRICES)]),
-        move(grad_in, grad_ref, out_sem.at[len(MATRICES) + 1]),
+    passed = [
+        move(output_in, output, load_sem.at[len(MATRICES) + 1]),
+        move(grad_in, grad, load_sem.at[len(MATRICES) + 2]),
     ]
+    stores = []
     for at, (first, width, blocks) in enumerate(MATRICES):
         loads[at].wait()
         stage = stages[at]
-        for block in range(blocks):
-
-            @pl.loop(0, BLOCK // ROW_BLOCK)
-            def _(step):
-                value = packed[span(step, ROW_BLOCK), first + block * width : first + (block + 1) * width].astype(F32)
+        tall = 2 * ROW_BLOCK
+
+        @pl.loop(0, BLOCK // tall, unroll=2)
+        def _(step):
+            for block in range(blocks):
+                value = packed[span(step, tall), first + block * width : first + (block + 1) * width].astype(F32)
                 if blocks == 3:
-                    stage[block, span(step, ROW_BLOCK), :] = value
+                    stage[block, span(step, tall), :] = value
                 else:
-                    stage[pl.ds(bound(block * BLOCK + step * ROW_BLOCK, ROW_BLOCK), ROW_BLOCK), :] = value
+                    stage[pl.ds(bound(block * BLOCK + step * tall, tall), tall), :] = value
 
         stores.append(move(stage, outs[at], out_sem.at[at]))
 
+    for copy in passed:
+        copy.wait()
+    stores.append(move(output, output_ref, out_sem.at[len(MATRICES)]))
+    stores.append(move(grad, grad_ref, out_sem.at[len(MATRICES) + 1]))
     loads[len(MATRICES)].wait()
     small = jnp.concatenate(
         [
@@ -1447,11 +1532,15 @@
         unpack_body,
         out_shape=(shaped(output.shape, output.dtype), shaped(grad.shape))
         + tuple(shaped(shape) for shape in shapes + vectors),
-        in_specs=[vmem_spec()] * 2 + [any_spec()],
+        in_specs=[any_spec()] * 3,
         out_specs=[any_spec()] * (2 + len(shapes)) + [vmem_spec()] * len(vectors),
-        scratch_shapes=[pltpu.VMEM(packed.shape, packed.dtype)]
+        scratch_shapes=[
+            pltpu.VMEM(packed.shape, packed.dtype),
+            pltpu.VMEM(output.shape, output.dtype),
+            pltpu.VMEM(grad.shape, F32),
+        ]
         + [pltpu.VMEM(shape, F32) for shape in shapes]
-        + [pltpu.SemaphoreType.DMA((len(shapes) + 1,)), pltpu.SemaphoreType.DMA((len(shapes) + 2,))],
+        + [pltpu.SemaphoreType.DMA((len(shapes) + 3,)), pltpu.SemaphoreType.DMA((len(shapes) + 2,))],
         compiler_params=pltpu.CompilerParams(vmem_limit_bytes=VMEM_MOST),
         name="unpack",
     )(output, grad, packed)
@@ -1474,13 +1563,15 @@
     weights = (glu_w, left_w, conv_w, point_w, qkv_w, attn_w, expand_w, shrink_w)
     (
         late, early, small, seg, plan, q_head, kv_head, n1, glu_pre, n2, left_pre, conv_pre, n3,
-        depth, n4, x2, inv, masks,
+        depth, n4, x2, inv, masks, seg_cols,
     ) = first_kernel(tokens[0], segment_ids, vectors, weights, count, heads)
     o_head, o_low, log_sum = attend(plan, q_head, kv_head, seg, rows)
     output, small_grads, dx3, early_grads, do_head = middle_kernel(
         o_low, out_grad[0], small, x2, early, count, heads
     )
-    dq_head, dkv_head = attend_back(plan, q_head, do_head, o_head, log_sum, kv_head, seg, rows)
+    dq_head, dkv_head = attend_back(
+        plan, q_head, do_head, o_head, log_sum, seg, kv_head, seg_cols, rows
+    )
     tensors = (
         early_grads, dx3, late, n1, glu_pre, n2, left_pre, conv_pre, n3, depth, n4, inv, masks,
     )

time: 245 us -> 232 us (0.947)
  Pallas kernels: 244 us -> 229 us
    pallas_call x1, Pallas kernels: 18.6 us -> 13.3 us  [attend(): pl.pallas_call(functools.partial(attend_body, rows), out_shape=(shaped(q_...]
    pallas_call x1, Pallas kernels: 19.8 us -> 15.2 us  [attend_back(): pl.pallas_call(functools.partial(attend_back_body, rows), out_shape=(shap...]
    pallas_call x1, Pallas kernels: 129 us -> 126 us  [last_kernel(): pl.pallas_call(functools.partial(last_body, count, heads), out_shape=(sha...]
where the time goes in v5:
time: 232 us; the launch traced here: 230 us
  Pallas kernels  229 us (99%)
    pallas_call x1, Pallas kernels, last_kernel(): pl.pallas_call(functools.partial(last_body, count, heads), out_shape=(sha...  126 us
    pallas_call x1, Pallas kernels, first_kernel(): pl.pallas_call(functools.partial(first_body, count, heads), out_shape=out...  43.3 us
    pallas_call x1, Pallas kernels, middle_kernel(): pl.pallas_call(functools.partial(middle_body, count, heads), out_shape=(s...  25.1 us
    pallas_call x1, Pallas kernels, attend_back(): pl.pallas_call(functools.partial(attend_back_body, rows), out_shape=(shap...  15.2 us
    pallas_call x1, Pallas kernels, attend(): pl.pallas_call(functools.partial(attend_body, rows), out_shape=(shaped(q_...  13.3 us
    pallas_call x1, Pallas kernels, unpack(): pl.pallas_call(unpack_body, out_shape=(shaped(output.shape, output.dtype)...  6.85 us

profile of v5, /device:TPU:0, one launch (start us, length us, event | category | flops | bytes accessed | tf_op | source)
XLA Modules:
  0.0 230.2 jit_solution(3377143526326274662)
XLA Ops:
  0.7 43.3 %first_layers.1 = (bf16[512,6400]{1,0:T(8,128)(2,1)}, bf16[512,4608]{1,0:T(8,128)(2,1)}, f32[2,32,1024]{2,1,0:T(8,128)}, s32[16,1,256]{2,1,0:T(1,128)}, s32[8,12...) custom-call(bf16[256,512]{1,0:T(8,128)(2,1)} %bitcast.40, ...), custom_call_target="tpu_custom_call" | custom-call | tf_op jit(solution)/shard_map/first_layers/pallas_call | solution.py:630
  43.9 13.3 %attend.1 = (f32[64,2048]{1,0:T(8,128)}, bf16[64,2048]{1,0:T(8,128)(2,1)}, f32[1,2048]{1,0:T(1,128)}) custom-call(s32[8,128]{1,0:T(8,128)} %get-tuple-element.87.plan_ref, bf16[64,2048]{1,0:T(8,128)(2,1)} %get-tuple-element.88.q_ref, bf16[4096,256]{1,0:T(8,128)(2,1)} %get-tuple-element.89.kv_ref.kv_in, s32[16,1,256]{2,1,0:T(1,128)} %get-tuple-element.90.seg_ref), custom_call_target="tpu_custom_call" | custom-call | tf_op jit(solution)/shard_map/attend/pallas_call | solution.py:696
  57.2 25.1 %middle_layers.1 = (bf16[256,512]{1,0:T(8,128)(2,1)}, f32[2,32,1024]{2,1,0:T(8,128)}, f32[256,512]{1,0:T(8,128)}, bf16[512,4608]{1,0:T(8,128)(2,1)}, bf16[64,2048]{1,0:T(8,128)(2,1)}) custom-call(bf16[64,2048]{1,0:T(8,128)(2,1)} %get-tuple-element.91.o_in, bf16[256,512]{1,0:T(8,128)(2,1)} %bitcast.41, f32[2,32,1024]{2,1,0:T(8,128)} %get-tuple-element.92.small_in.refs_2_, ...), custom_call_target="tpu_custom_call" | custom-call | tf_op jit(solution)/shard_map/middle_layers/pallas_call | solution.py:899
  82.3 15.2 %attend_back.1 = (bf16[64,2048]{1,0:T(8,128)(2,1)}, bf16[4096,128]{1,0:T(8,128)(2,1)}) custom-call(s32[8,128]{1,0:T(8,128)} %get-tuple-element.87.plan_ref, bf16[64,2048]{1,0:T(8,128)(2,1)} %get-tuple-element.88.q_ref, bf16[64,2048]{1,0:T(8,128)(2,1)} %get-tuple-element.96.do_ref, f32[64,2048]{1,0:T(8,128)} %get-tuple-element.97.o_ref, ...), custom_call_target="tpu_custom_call" | custom-call | tf_op jit(solution)/shard_map/attend_back/pallas_call | solution.py:752
  97.6 125.6 %last_layers.1 = (bf16[256,11264]{1,0:T(8,128)(2,1)}, f32[256,512]{1,0:T(8,128)}) custom-call(bf16[64,2048]{1,0:T(8,128)(2,1)} %get-tuple-element.100.refs_0_, bf16[8,2,256,128]{3,2,1,0:T(8,128)(2,1)} %bitcast.39, f32[2,32,1024]{2,1,0:T(8,128)} %get-tuple-element.92.small_in.refs_2_, f32[2,32,1024]{2,1,0:T(8,128)} %get-tuple-element.102.refs_3_, ...), custom_call_target="tpu_custom_call" | custom-call | tf_op jit(solution)/shard_map/last_layers/pallas_call | solution.py:1466
  223.2 6.8 %unpack.1 = (bf16[256,512]{1,0:T(8,128)(2,1)}, f32[256,512]{1,0:T(8,128)}, f32[256,1024]{1,0:T(8,128)}, f32[256,2048]{1,0:T(8,128)}, f32[3,256,256]{2,1,0:T(8,12...) custom-call(bf16[256,512]{1,0:T(8,128)(2,1)} %get-tuple-element.95.o, ...), custom_call_target="tpu_custom_call" | custom-call | tf_op jit(solution)/shard_map/unpack/pallas_call | solution.py:1531

commit v6 on v5

--- a/solution.py
+++ b/solution.py
@@ -19,7 +19,7 @@
 EDGE = 16
 KEY_TILE = 1024
 BLOCK = 256
-VMEM_MOST = 60 * 1024 * 1024
+VMEM_MOST = 62 * 1024 * 1024
 
 D = 512
 FF = 2048
@@ -91,11 +91,19 @@
     )
 
 
-def greet(peers):
+def announce(peers):
     barrier = pltpu.get_barrier_semaphore()
     for peer in peers:
         pl.semaphore_signal(barrier, inc=1, device_id=peer, device_id_type=MESH_ID)
-    pl.semaphore_wait(barrier, len(peers))
+
+
+def all_here(peers):
+    pl.semaphore_wait(pltpu.get_barrier_semaphore(), len(peers))
+
+
+def greet(peers):
+    announce(peers)
+    all_here(peers)
 
 
 def push(src, dst, sems, at, peer):
@@ -704,68 +712,6 @@
     )(plan, q_t, kv, seg)
 
 
-def attend_back_body(
-    rows, plan_ref, q_ref, do_ref, o_ref, lse_ref, seg_ref, kv_in, seg_in, dq_ref, dkv_ref, kv_ref, segk, turned, dkv_acc, sems
-):
-    loads = [
-        move(kv_in.at[:, pl.ds(0, LANES)], kv_ref, sems.at[0]),
-        move(seg_in, segk, sems.at[1]),
-    ]
-    dkv_acc[...] = jnp.zeros_like(dkv_acc)
-    loads[0].wait()
-    turn_keys(kv_ref, turned)
-    loads[1].wait()
-    scale = HEAD_DIM**-0.5
-
-    @pl.loop(0, q_ref.shape[1] // rows)
-    def _(tile):
-        at = span(tile, rows)
-        q = q_ref[:, at] * jnp.bfloat16(scale)
-        do = do_ref[:, at]
-        none = jnp.zeros_like(q)
-        both = jnp.concatenate(
-            [jnp.concatenate([q, none], axis=1), jnp.concatenate([none, do], axis=1)], axis=0
-        )
-        delta = jnp.sum(o_ref[:, at] * do.astype(F32), axis=0, keepdims=True)
-        lse = lse_ref[:, at]
-        seg_q = seg_ref[plan_ref[tile, 2]].astype(F32)
-
-        def block(key_tile, dq):
-            here = span(key_tile, KEY_TILE)
-            pair = matmul(kv_ref[here, :], both)
-            seg_k = jnp.concatenate([segk[here, :]] * (rows // LANES), axis=1)
-            scores = jnp.where(seg_k == seg_q, pair[:, :rows], MASK_FILL)
-            probs = jnp.exp(scores - lse)
-            score_grad = (probs * (pair[:, rows:] - delta)).astype(BF16)
-            joined = jnp.concatenate([score_grad, probs.astype(BF16)], axis=1)
-            dkv_acc[here, :] += back_mul(joined, both)
-            return dq + matmul(turned[:HEAD_DIM, here], score_grad)
-
-        first, end = key_tiles(plan_ref, tile)
-        dq = lax.fori_loop(first, end, block, jnp.zeros((HEAD_DIM, rows), F32))
-        dq_ref[:, at] = (dq * scale).astype(BF16)
-
-    dkv_ref[...] = dkv_acc[...].astype(BF16)
-
-
-def attend_back(plan, q_t, do_t, o_t, lse, seg, kv, seg_cols, rows):
-    return pl.pallas_call(
-        functools.partial(attend_back_body, rows),
-        out_shape=(shaped(q_t.shape, BF16), shaped((kv.shape[0], LANES), BF16)),
-        in_specs=[smem_spec()] + [vmem_spec()] * 5 + [any_spec()] * 2,
-        out_specs=(vmem_spec(),) * 2,
-        scratch_shapes=[
-            pltpu.VMEM((kv.shape[0], LANES), BF16),
-            pltpu.VMEM((kv.shape[0], LANES), F32),
-            pltpu.VMEM((LANES, kv.shape[0]), BF16),
-            pltpu.VMEM((kv.shape[0], LANES), F32),
-            pltpu.SemaphoreType.DMA((2,)),
-        ],
-        compiler_params=pltpu.CompilerParams(vmem_limit_bytes=VMEM_MOST),
-        name="attend_back",
-    )(plan, q_t, do_t, o_t, lse, seg, kv, seg_cols)
-
-
 def middle_body(
     count,
     heads,
@@ -1049,10 +995,15 @@
 
 def last_body(count, heads, *refs):
     (
-        dq_in,
-        dkv_in,
+        q_in,
+        do_in,
+        o_in,
+        lse_in,
+        kv_in,
+        seg_in,
         small_in,
         small_grads_in,
+        seg_ref,
         early_grads,
         dx3_in,
         late_in,
@@ -1085,7 +1036,19 @@
         small_grads,
         dq_t,
         dkv_own,
-        dkv_mine,
+        q_all,
+        do_all,
+        o_all,
+        lse,
+        both,
+        delta,
+        kv_slots,
+        seg_slots,
+        turned,
+        dkv_acc,
+        dq_acc,
+        dq_low,
+        dkv_all,
         small_raw,
         shared,
         summed,
@@ -1102,10 +1065,10 @@
         grads,
         early_own,
         got,
-        result,
         load_sem,
         keep_sem,
         store_sem,
+        tile_sem,
         dq_send,
         dq_recv,
         dkv_send,
@@ -1133,17 +1096,44 @@
 
     sources = (dx3_in, late_in, n4_in, inv_in, depth_in, masks_in, n3_in, left_in, conv_in, n2_in, glu_in, n1_in)
     targets = (dx3, weights, n4, inv, depth, masks, n3, left_pre, conv_pre, n2, glu_pre, n1)
-    slot = dq_t.at[span(head, HEAD_DIM), :]
+    announce([sibling] + peers)
     own_rows = pl.ds(bound(core * BLOCK, BLOCK), BLOCK)
-    keeps = [
-        move(dkv_in.at[:, part], dkv_mine, keep_sem.at[2]),
-        move(early_grads.at[own_rows, :], early_own, keep_sem.at[1]),
-        move(dq_in.at[:, span(head, rows)], slot, keep_sem.at[0]),
-        move(small_in, small_raw, keep_sem.at[3]),
-        move(small_grads_in, small_grads, keep_sem.at[4]),
+    attention_loads = [
+        move(q_in, q_all, keep_sem.at[2]),
+        move(do_in, do_all, keep_sem.at[5]),
+        move(o_in, o_all, keep_sem.at[6]),
+        move(lse_in, lse, keep_sem.at[7]),
     ]
-    greet([sibling] + peers)
-    loads = [move(a, b, load_sem.at[at]) for at, (a, b) in enumerate(zip(sources, targets))]
+
+    near_heads = max(1, KEY_TILE // (parts * rows))
+    tiles_each = max(1, parts * rows // KEY_TILE)
+    group_count = heads // near_heads
+    key_count = count * rows
+    longest = key_count // 2
+
+    def group_first(group):
+        return lax.rem(head // near_heads + group, group_count) * near_heads
+
+    def group_head(group, at):
+        mixed = lax.rem(head, near_heads)
+        bit = sum(
+            (lax.rem(mixed // 2**k, 2) + (at >> k & 1) - 2 * lax.rem(mixed // 2**k, 2) * (at >> k & 1)) * 2**k
+            for k in range(near_heads.bit_length() - 1)
+        )
+        return group_first(group) + bit
+
+    def tile_first(number):
+        group, tile = number // tiles_each, number % tiles_each
+        return group_first(group) * parts * rows + tile * KEY_TILE
+
+    def fetch(number):
+        here = pl.ds(bound(tile_first(number), KEY_TILE), KEY_TILE)
+        return [
+            move(kv_in.at[here, pl.ds(0, LANES)], kv_slots.at[number % 2], tile_sem.at[number % 2]),
+            move(seg_in.at[here, :], seg_slots.at[number % 2], tile_sem.at[2 + number % 2]),
+        ]
+
+    fetched = fetch(0)
 
     bit_of = [lax.rem(own // 2**bit, 2) for bit in range(bits)]
     partner = [(own + 2**bit - 2 * 2**bit * bit_of[bit], core) for bit in range(bits)]
@@ -1174,60 +1164,153 @@
 
     def advance(members):
         for piece in members:
-            piece.advance()
-
-    start(sets[0] + sets[1], early_grads, LATE)
-    heads_on = [lax.rem(head + gap, heads) for gap in range(heads)]
-    sharing = []
-    for gap, other in enumerate(heads_on[1:] + heads_on[:1]):
-        for at in range(parts - 1):
-            twin = lax.rem(part + at + 1, parts)
-            sharing.append(
-                push(
-                    dkv_in.at[other, twin],
-                    shared.at[at, other],
-                    (pass_send, pass_recv),
-                    at * heads + gap,
-                    (head * parts + twin, core),
+            if not piece.sent_all():
+                piece.advance()
+
+    scale = HEAD_DIM**-0.5
+    for copy in attention_loads:
+        copy.wait()
+    dq_acc[...] = jnp.zeros_like(dq_acc)
+
+    @pl.loop(0, heads)
+    def _(tile):
+        at = span(tile, rows)
+        q = q_all[:, at] * jnp.bfloat16(scale)
+        do = do_all[:, at]
+        none = jnp.zeros_like(q)
+        both[tile] = jnp.concatenate(
+            [jnp.concatenate([q, none], axis=1), jnp.concatenate([none, do], axis=1)], axis=0
+        )
+        delta[:, at] = jnp.sum(o_all[:, at] * do.astype(F32), axis=0, keepdims=True)
+
+    def attention_tile(number):
+        first, slot = tile_first(number), number % 2
+
+        def one(tile):
+            source = tile * parts + part
+            apart = jnp.maximum(
+                first - (source * rows + rows - 1), source * rows - (first + KEY_TILE - 1)
+            )
+
+            @pl.when(apart < longest)
+            def _():
+                at = span(tile, rows)
+                operand = both[tile]
+                pair = matmul(kv_slots[slot], operand)
+                seg_k = jnp.concatenate([seg_slots[slot]] * (rows // LANES), axis=1)
+                seg_q = seg_ref[source].astype(F32)
+                scores = jnp.where(seg_k == seg_q, pair[:, :rows], MASK_FILL)
+                probs = jnp.exp(scores - lse[:, at])
+                score_grad = (probs * (pair[:, rows:] - delta[:, at])).astype(BF16)
+                joined = jnp.concatenate([score_grad, probs.astype(BF16)], axis=1)
+                dkv_acc[...] += back_mul(joined, operand)
+                dq_acc[:, at] += matmul(turned[...], score_grad)
+
+        return one
+
+    collect, sharing, arrived = [], [], []
+
+    def share_group(group):
+        for at in range(near_heads):
+            other = group_head(group, at)
+            for gap in range(parts - 1):
+                twin = lax.rem(part + gap + 1, parts)
+                sharing.append(
+                    push(
+                        dkv_all.at[span(other * parts + twin, rows), :],
+                        shared.at[gap, group * near_heads + at],
+                        (pass_send, pass_recv),
+                        gap * heads + group * near_heads + at,
+                        (head * parts + twin, core),
+                    )
                 )
-            )
-    collect = []
-    for gap, other in enumerate(heads_on[1:]):
-        collect.append(
-            push(dq_in.at[:, span(other, rows)], slot, (dq_send, dq_recv), gap, (other * parts + part, core))
-        )
-    for copy in keeps:
-        copy.wait()
-    widened(small, small_raw)
-    advance(sets[0] + sets[1])
-    for gap, other in enumerate(heads_on[1:] + heads_on[:1]):
-        for copy in sharing[gap * (parts - 1) : (gap + 1) * (parts - 1)]:
-            copy.wait()
-        total_kv = dkv_mine[other].astype(F32)
-        for at in range(parts - 1):
-            total_kv = total_kv + shared[at, other].astype(F32)
-        if gap < heads - 1:
-            summed[other] = total_kv.astype(BF16)
+
+    def send_group(group):
+        for at in range(near_heads):
+            other, index = group_head(group, at), group * near_heads + at
+            for copy in sharing[index * (parts - 1) : (index + 1) * (parts - 1)]:
+                copy.wait()
+            total_kv = dkv_all[span(other * parts + part, rows), :].astype(F32)
+            for gap in range(parts - 1):
+                total_kv = total_kv + shared[gap, index].astype(F32)
+            if index:
+                summed[index] = total_kv.astype(BF16)
+                collect.append(
+                    push(
+                        summed.at[index],
+                        dkv_own.at[:, span(head, LANES)],
+                        (dkv_send, dkv_recv),
+                        index - 1,
+                        (other * parts + part, core),
+                    )
+                )
+            else:
+                dkv_own[:, span(head, LANES)] = total_kv.astype(BF16)
+
+    slot = dq_t.at[span(head, HEAD_DIM), :]
+
+    def send_dq(gap, other):
+        here = span(other, rows)
+        dq_low[:, here] = (dq_acc[:, here] * scale).astype(BF16)
+        if gap < heads:
             collect.append(
-                push(
-                    summed.at[other],
-                    dkv_own.at[:, span(head, LANES)],
-                    (dkv_send, dkv_recv),
-                    gap,
-                    (other * parts + part, core),
-                )
+                push(dq_low.at[:, here], slot, (dq_send, dq_recv), gap - 1, (other * parts + part, core))
             )
         else:
-            dkv_own[:, span(head, LANES)] = total_kv.astype(BF16)
-        if gap == heads // 2:
-            advance(sets[0][1:])
-    advance(sets[1][1:])
+            collect.append(move(dq_low.at[:, here], slot, keep_sem.at[0]))
+
+    points, keeps, loads = [], [], []
+
+    def pump():
+        at = len(points)
+        points.append(at)
+        if at == 0:
+            all_here([sibling] + peers)
+            start(sets[0] + sets[1], early_grads, LATE)
+            keeps.append(move(early_grads.at[own_rows, :], early_own, keep_sem.at[1]))
+            keeps.append(move(small_in, small_raw, keep_sem.at[3]))
+            keeps.append(move(small_grads_in, small_grads, keep_sem.at[4]))
+        elif at == 1:
+            for copy in keeps:
+                copy.wait()
+            widened(small, small_raw)
+            advance(sets[0])
+            loads.extend(move(a, b, load_sem.at[k]) for k, (a, b) in enumerate(zip(sources, targets)))
+        elif at in (5, 9, 12, 15):
+            advance(sets[0])
+        elif at in (2, 7, 11, 14):
+            advance(sets[1])
+
+    tiles = group_count * tiles_each
+    for number in range(tiles):
+        for copy in fetched:
+            copy.wait()
+        if number + 1 < tiles:
+            fetched = fetch(number + 1)
+        turned[...] = turn(kv_slots[number % 2, :, :HEAD_DIM])
+        dkv_acc[...] = jnp.zeros_like(dkv_acc)
+        group = number // tiles_each
+        one = attention_tile(number)
+        for turn_no in range(4):
+            reach = (turn_no * heads // 4 + 1, (turn_no + 1) * heads // 4 + 1)
+            pl.loop(*reach)(lambda gap: one(lax.rem(head + gap, heads)))
+            if number == tiles - 1:
+                for gap in range(*reach):
+                    send_dq(gap, lax.rem(head + gap, heads))
+            if turn_no == 2 and group and number % tiles_each == 0:
+                send_group(group - 1)
+            if turn_no < 3:
+                pump()
+        here = pl.ds(bound(tile_first(number), KEY_TILE), KEY_TILE)
+        dkv_all[here, :] = dkv_acc[...].astype(BF16)
+        if number % tiles_each == tiles_each - 1:
+            share_group(group)
+        pump()
     for copy in loads:
         copy.wait()
-    advance(sets[0][:1])
+    send_group(group_count - 1)
     for copy in collect:
         copy.wait()
-    advance(sets[1][:1])
 
     dqkv[:, :D] = turn(dq_t[...])
     lane = lax.broadcasted_iota(jnp.int32, (rows, LANES), 1) < HEAD_DIM
@@ -1264,20 +1347,19 @@
         push(sep_own.at[pl.ds(rows - EDGE, EDGE), :], sep_edges.at[0], (edge_send, edge_recv), 0, right),
         push(sep_own.at[pl.ds(0, EDGE), :], sep_edges.at[1], (edge_send, edge_recv), 1, left),
     ]
-    advance(sets[0])
     low_t = turn(n4[...] * vector(small, LN4G, D) + vector(small, LN4B, D))
     for step in range(3):
         grads[:, QKV + D * step : QKV + D * (step + 1)] = matmul(
             low_t, dqkv[:, D * step : D * (step + 1)]
         ).astype(BF16)
     start(sets[2], grads, 0)
+    advance(sets[0])
     for block in range(FF // BLOCK):
         side, column = block // 4, POINT + HALF * (block % 4)
         grads[side * BLOCK : (side + 1) * BLOCK, column : column + HALF] = matmul(
             turn(depth[:, block * BLOCK : (block + 1) * BLOCK]), sep_own[...]
         ).astype(BF16)
     start(sets[3], grads, 0)
-    advance(sets[1])
     put_vector(small_grads, POINTB, col_sum(sep_own[...]))
 
     for copy in edge_copies:
@@ -1294,7 +1376,6 @@
         )
 
     advance(sets[2])
-    advance(sets[0])
     row_sums[...] = jnp.zeros_like(row_sums)
     half = FF // 2 // LANES
 
@@ -1318,9 +1399,7 @@
         row_sums[0] = row_sums[0] + scaled
         row_sums[1] = row_sums[1] + scaled * normed
 
-    for quarter, turns in enumerate(
-        (sets[1] + sets[3], sets[0] + sets[2], sets[1] + sets[3], sets[0] + sets[2])
-    ):
+    for quarter, turns in enumerate((sets[1], sets[3], sets[2], sets[1])):
         pl.loop(quarter * half // 2, (quarter + 1) * half // 2)(tap_block)
         advance(turns)
     inner = jnp.sum(row_sums[0], axis=1, keepdims=True) * (1.0 / FF)
@@ -1338,9 +1417,9 @@
         small_grads[side, LEFTB : LEFTB + 1, lanes] = col_sum(low)
 
     pl.loop(0, half)(left_block)
-    advance(sets[1])
+    advance(sets[3])
     pl.loop(half, 2 * half)(left_block)
-    advance(sets[3] + sets[0])
+    advance(sets[0])
     for step in range(HALF // LANES):
         cols = slice(step * LANES, (step + 1) * LANES)
         scaled = g3_grad[:, cols] * small[0, LN3G : LN3G + 1, cols]
@@ -1360,30 +1439,30 @@
         if step % 2:
             start(sets[4 + step // 2], grads, 0)
     advance(sets[2])
-    advance(sets[1])
     for tap in range(3):
         grads[:, CONV + HALF * tap : CONV + HALF * (tap + 1)] = matmul(
             low_t, conv_taps[:, HALF * tap : HALF * (tap + 1)]
         ).astype(BF16)
-    advance(sets[4] + sets[5])
+    advance(sets[4])
+    advance(sets[5])
     grad = through(dleft[...], LEFT, FF) + through(conv_taps[...], CONV, 3 * HALF)
     dx1 = dx3[...] + norm_step(grad, n2[...], inv[1, mid, :1], LN2G)
     gate = jax.nn.sigmoid(glu_pre[:, D:])
     value_grad = dx1 * gate
     dglu = jnp.concatenate([value_grad, value_grad * glu_pre[:, :D] * (1.0 - gate)], axis=1).astype(BF16)
     put_vector(small_grads, GLUB, col_sum(dglu))
+    advance(sets[1])
     advance(sets[3])
-    advance(sets[0])
     low_t = turn(n1[...] * vector(small, LN1G, D) + vector(small, LN1B, D))
     for step in range(2):
         grads[:, GLU + D * step : GLU + D * (step + 1)] = matmul(
             low_t, dglu[:, D * step : D * (step + 1)]
         ).astype(BF16)
     start(sets[6], grads, 0)
-    advance(sets[1] + sets[2])
+    advance(sets[2])
     grad = through(dglu, GLU, 2 * D)
-    result[...] = dx1 + norm_step(grad, n1[...], inv[0, mid, :1], LN1G)
-    keep = move(result, grad_out, keep_sem.at[0])
+    dx3[...] = dx1 + norm_step(grad, n1[...], inv[0, mid, :1], LN1G)
+    keep = move(dx3, grad_out, keep_sem.at[0])
     for side in range(2):
         for block in range(SMALL_WIDTH // BLOCK):
             first = side * BLOCK + block * SMALL_ROWS
@@ -1414,8 +1493,8 @@
     keep.wait()
 
 
-def last_kernel(dq, dkv, small, small_grads, tensors, count, heads):
-    rows = dkv.shape[0] // count
+def last_kernel(attention, small, small_grads, seg, tensors, count, heads):
+    rows = seg.shape[2]
     ext = rows + 2 * EDGE
     parts = count // heads
     bits = count.bit_length() - 1
@@ -1438,7 +1517,19 @@
         pltpu.VMEM((2, SMALL_ROWS, SMALL_WIDTH), F32),
         pltpu.VMEM((D, rows), BF16),
         pltpu.VMEM((rows, 2 * D), BF16),
-        pltpu.VMEM((heads, rows, LANES), BF16),
+        pltpu.VMEM((HEAD_DIM, heads * rows), BF16),
+        pltpu.VMEM((HEAD_DIM, heads * rows), BF16),
+        pltpu.VMEM((HEAD_DIM, heads * rows), F32),
+        pltpu.VMEM((1, heads * rows), F32),
+        pltpu.VMEM((heads, LANES, 2 * rows), BF16),
+        pltpu.VMEM((1, heads * rows), F32),
+        pltpu.VMEM((2, KEY_TILE, LANES), BF16),
+        pltpu.VMEM((2, KEY_TILE, LANES), F32),
+        pltpu.VMEM((HEAD_DIM, KEY_TILE), BF16),
+        pltpu.VMEM((KEY_TILE, LANES), F32),
+        pltpu.VMEM((HEAD_DIM, heads * rows), F32),
+        pltpu.VMEM((HEAD_DIM, heads * rows), BF16),
+        pltpu.VMEM((count * rows, LANES), BF16),
         pltpu.VMEM((2, SMALL_ROWS, SMALL_WIDTH), F32),
         pltpu.VMEM((parts - 1, heads, rows, LANES), BF16),
         pltpu.VMEM((heads, rows, LANES), BF16),
@@ -1455,10 +1546,10 @@
         pltpu.VMEM((2 * BLOCK, LATE), BF16),
         pltpu.VMEM((BLOCK, EARLY), BF16),
         pltpu.VMEM((BLOCK + ROW_BLOCK * max(0, bits - 4), WIDTH), BF16),
-        pltpu.VMEM((rows, D), F32),
         pltpu.SemaphoreType.DMA((12,)),
-        pltpu.SemaphoreType.DMA((5,)),
+        pltpu.SemaphoreType.DMA((8,)),
         pltpu.SemaphoreType.DMA((pieces,)),
+        pltpu.SemaphoreType.DMA((4,)),
     ]
     scratch += sem_pair(heads - 1) + sem_pair(heads - 1) + sem_pair((parts - 1) * heads)
     scratch += sem_pair(2) + sem_pair(pieces)
@@ -1466,12 +1557,12 @@
     return pl.pallas_call(
         functools.partial(last_body, count, heads),
         out_shape=(shaped((BLOCK, WIDTH), BF16), shaped((rows, D))),
-        in_specs=[any_spec()] * (4 + len(tensors)),
+        in_specs=[any_spec()] * (len(attention) + 2) + [vmem_spec()] + [any_spec()] * len(tensors),
         out_specs=[any_spec(), any_spec()],
         scratch_shapes=scratch,
         compiler_params=comm_params(3),
         name="last_layers",
-    )(dq, dkv.reshape(heads, parts, rows, LANES), small, small_grads, *tensors)
+    )(*attention, small, small_grads, seg, *tensors)
 
 
 def unpack_body(output_in, grad_in, packed_in, *refs):
@@ -1569,13 +1660,11 @@
     output, small_grads, dx3, early_grads, do_head = middle_kernel(
         o_low, out_grad[0], small, x2, early, count, heads
     )
-    dq_head, dkv_head = attend_back(
-        plan, q_head, do_head, o_head, log_sum, seg, kv_head, seg_cols, rows
-    )
     tensors = (
         early_grads, dx3, late, n1, glu_pre, n2, left_pre, conv_pre, n3, depth, n4, inv, masks,
     )
-    total, input_grad = last_kernel(dq_head, dkv_head, small, small_grads, tensors, count, heads)
+    attention = (q_head, do_head, o_head, log_sum, kv_head, seg_cols)
+    total, input_grad = last_kernel(attention, small, small_grads, seg, tensors, count, heads)
     output, input_grad, *pieces = unpack(output, input_grad, total)
     matrices, lines = pieces[: len(MATRICES)], pieces[len(MATRICES) :]
     lines = [line if line.shape[0] > 1 else line.reshape(-1) for line in lines]

time: 232 us -> 226 us (0.974)
  Pallas kernels: 229 us -> 224 us
    pallas_call x1 -> x0, Pallas kernels: 15.2 us -> none  [attend_back(): pl.pallas_call(functools.partial(attend_back_body, rows), out_shape=(shap...]
    pallas_call x1, Pallas kernels: 126 us -> 135 us  [last_kernel(): pl.pallas_call(functools.partial(last_body, count, heads), out_shape=(sha...]
    pallas_call x1, Pallas kernels: 13.3 us -> 16.8 us  [attend(): pl.pallas_call(functools.partial(attend_body, rows), out_shape=(shaped(q_...]
    pallas_call x1, Pallas kernels: 25.1 us -> 22.5 us  [middle_kernel(): pl.pallas_call(functools.partial(middle_body, count, heads), out_shape=(s...]
where the time goes in v6:
time: 226 us; the launch traced here: 225 us
  Pallas kernels  224 us (99%)
    pallas_call x1, Pallas kernels, last_kernel(): pl.pallas_call(functools.partial(last_body, count, heads), out_shape=(sha...  135 us
    pallas_call x1, Pallas kernels, first_kernel(): pl.pallas_call(functools.partial(first_body, count, heads), out_shape=out...  43.3 us
    pallas_call x1, Pallas kernels, middle_kernel(): pl.pallas_call(functools.partial(middle_body, count, heads), out_shape=(s...  22.5 us
    pallas_call x1, Pallas kernels, attend(): pl.pallas_call(functools.partial(attend_body, rows), out_shape=(shaped(q_...  16.8 us
    pallas_call x1, Pallas kernels, unpack(): pl.pallas_call(unpack_body, out_shape=(shaped(output.shape, output.dtype)...  6.85 us

profile of v6, /device:TPU:0, one launch (start us, length us, event | category | flops | bytes accessed | tf_op | source)
XLA Modules:
  0.0 225.1 jit_solution(12307917845423043777)
XLA Ops:
  0.7 43.3 %first_layers.1 = (bf16[512,6400]{1,0:T(8,128)(2,1)}, bf16[512,4608]{1,0:T(8,128)(2,1)}, f32[2,32,1024]{2,1,0:T(8,128)}, s32[16,1,256]{2,1,0:T(1,128)}, s32[8,12...) custom-call(bf16[256,512]{1,0:T(8,128)(2,1)} %bitcast.38, ...), custom_call_target="tpu_custom_call" | custom-call | tf_op jit(solution)/shard_map/first_layers/pallas_call | solution.py:638
  44.0 16.8 %attend.1 = (f32[64,2048]{1,0:T(8,128)}, bf16[64,2048]{1,0:T(8,128)(2,1)}, f32[1,2048]{1,0:T(1,128)}) custom-call(s32[8,128]{1,0:T(8,128)} %get-tuple-element.85.plan_ref, bf16[64,2048]{1,0:T(8,128)(2,1)} %get-tuple-element.86.q_ref.refs_0_, bf16[4096,256]{1,0:T(8,128)(2,1)} %get-tuple-element.87.kv_ref.refs_4_, s32[16,1,256]{2,1,0:T(1,128)} %get-tuple-element.88.seg_ref.refs_8_), custom_call_target="tpu_custom_call" | custom-call | tf_op jit(solution)/shard_map/attend/pallas_call | solution.py:704
  60.8 22.5 %middle_layers.1 = (bf16[256,512]{1,0:T(8,128)(2,1)}, f32[2,32,1024]{2,1,0:T(8,128)}, f32[256,512]{1,0:T(8,128)}, bf16[512,4608]{1,0:T(8,128)(2,1)}, bf16[64,2048]{1,0:T(8,128)(2,1)}) custom-call(bf16[64,2048]{1,0:T(8,128)(2,1)} %get-tuple-element.89.o_in, bf16[256,512]{1,0:T(8,128)(2,1)} %bitcast.39, f32[2,32,1024]{2,1,0:T(8,128)} %get-tuple-element.90.small_in.refs_6_, ...), custom_call_target="tpu_custom_call" | custom-call | tf_op jit(solution)/shard_map/middle_layers/pallas_call | solution.py:845
  83.3 134.8 %last_layers.1 = (bf16[256,11264]{1,0:T(8,128)(2,1)}, f32[256,512]{1,0:T(8,128)}) custom-call(bf16[64,2048]{1,0:T(8,128)(2,1)} %get-tuple-element.86.q_ref.refs_0_, bf16[64,2048]{1,0:T(8,128)(2,1)} %get-tuple-element.94.refs_1_, f32[64,2048]{1,0:T(8,128)} %get-tuple-element.95.refs_2_, f32[1,2048]{1,0:T(1,128)} %get-tuple-element.96.refs_3_, ...), custom_call_target="tpu_custom_call" | custom-call | tf_op jit(solution)/shard_map/last_layers/pallas_call | solution.py:1557
  218.1 6.8 %unpack.1 = (bf16[256,512]{1,0:T(8,128)(2,1)}, f32[256,512]{1,0:T(8,128)}, f32[256,1024]{1,0:T(8,128)}, f32[256,2048]{1,0:T(8,128)}, f32[3,256,256]{2,1,0:T(8,12...) custom-call(bf16[256,512]{1,0:T(8,128)(2,1)} %get-tuple-element.93.o, ...), custom_call_target="tpu_custom_call" | custom-call | tf_op jit(solution)/shard_map/unpack/pallas_call | solution.py:1622

commit v7 on v6

--- a/solution.py
+++ b/solution.py
@@ -112,6 +112,19 @@
         dst_ref=dst,
         send_sem=sems[0].at[at],
         recv_sem=sems[1].at[at],
+        device_id=peer,
+        device_id_type=MESH_ID,
+    )
+    copy.start()
+    return copy
+
+
+def push_by(src, dst, send_sem, recv_sem, peer):
+    copy = pltpu.make_async_remote_copy(
+        src_ref=src,
+        dst_ref=dst,
+        send_sem=send_sem,
+        recv_sem=recv_sem,
         device_id=peer,
         device_id_type=MESH_ID,
     )
@@ -917,7 +930,9 @@
         return self.total.at[pl.ds(bound(row, ROW_BLOCK), tall), pl.ds(bound(col, LANES), wide)]
 
     def start(self, other_half):
-        self.copy = push(other_half, self.out(self.whole()), self.sems[0], self.at, self.sibling)
+        self.copy = push_by(
+            other_half, self.out(self.whole()), self.sems[0].at[self.at], self.sems[1].at[self.at], self.sibling
+        )
 
     def add(self, where, source, spot, last):
         row, tall, col, wide = where
@@ -946,22 +961,22 @@
             half = wide // 2
             kept = (row, tall, col + half * mine, half)
             sent = (row, tall, col + half * (1 - mine), half)
-        self.copy = push(
+        self.copy = push_by(
             self.view(sent),
             self.got.at[pl.ds(self.spot, sent[1]), pl.ds(self.first, sent[3])],
-            self.sems[1],
-            self.at * self.bits + step,
+            self.sems[0].at[self.at],
+            self.sems[2].at[self.at * self.bits + step],
             self.partner[bit],
         )
         self.where = kept
 
     def double(self, step):
         place_out = self.out(self.trail[step])
-        self.copy = push(
+        self.copy = push_by(
             place_out,
             place_out,
-            self.sems[2],
-            self.at * self.bits + step,
+            self.sems[0].at[self.at],
+            self.sems[3].at[self.at * self.bits + step],
             self.partner[self.order[step]],
         )
 
@@ -1077,11 +1092,9 @@
         pass_recv,
         edge_send,
         edge_recv,
-        ws_send,
+        piece_send,
         ws_recv,
-        rs_send,
         rs_recv,
-        ag_send,
         ag_recv,
     ) = refs
     own, core = place()
@@ -1138,7 +1151,7 @@
     bit_of = [lax.rem(own // 2**bit, 2) for bit in range(bits)]
     partner = [(own + 2**bit - 2 * 2**bit * bit_of[bit], core) for bit in range(bits)]
     links = (core, sibling, bit_of, partner)
-    sems = ((ws_send, ws_recv), (rs_send, rs_recv), (ag_send, ag_recv))
+    sems = (piece_send, ws_recv, rs_recv, ag_recv)
 
     def early_view(where):
         row, tall, col, wide = where
@@ -1276,9 +1289,9 @@
             widened(small, small_raw)
             advance(sets[0])
             loads.extend(move(a, b, load_sem.at[k]) for k, (a, b) in enumerate(zip(sources, targets)))
-        elif at in (5, 9, 12, 15):
+        elif at in (4, 7, 9, 11, 13, 15):
             advance(sets[0])
-        elif at in (2, 7, 11, 14):
+        elif at in (2, 6, 8, 10, 12, 14):
             advance(sets[1])
 
     tiles = group_count * tiles_each
@@ -1475,7 +1488,7 @@
         )
     start(sets[7], grads, 0)
     advance(sets[4] + sets[5])
-    pieces = [piece for number in (0, 3, 1, 2, 6, 7, 4, 5) for piece in sets[number]]
+    pieces = [piece for number in (6, 7, 4, 5, 2, 3, 0, 1) for piece in sets[number]]
     stores, rounds = [], 0
     while not all(piece.done() for piece in pieces):
         last = all(piece.sent_all() for piece in pieces)
@@ -1553,7 +1566,7 @@
     ]
     scratch += sem_pair(heads - 1) + sem_pair(heads - 1) + sem_pair((parts - 1) * heads)
     scratch += sem_pair(2) + sem_pair(pieces)
-    scratch += sem_pair(pieces * bits) + sem_pair(pieces * bits)
+    scratch += [pltpu.SemaphoreType.DMA((pieces * bits,))] * 2
     return pl.pallas_call(
         functools.partial(last_body, count, heads),
         out_shape=(shaped((BLOCK, WIDTH), BF16), shaped((rows, D))),

time: 226 us -> 220 us (0.973)
  Pallas kernels: 224 us -> 218 us
    pallas_call x1, Pallas kernels: 16.8 us -> 12.5 us  [attend(): pl.pallas_call(functools.partial(attend_body, rows), out_shape=(shaped(q_...]
where the time goes in v7:
time: 220 us; the launch traced here: 219 us
  Pallas kernels  218 us (99%)
    pallas_call x1, Pallas kernels, last_kernel(): pl.pallas_call(functools.partial(last_body, count, heads), out_shape=(sha...  133 us
    pallas_call x1, Pallas kernels, first_kernel(): pl.pallas_call(functools.partial(first_body, count, heads), out_shape=out...  43.3 us
    pallas_call x1, Pallas kernels, middle_kernel(): pl.pallas_call(functools.partial(middle_body, count, heads), out_shape=(s...  22.5 us
    pallas_call x1, Pallas kernels, attend(): pl.pallas_call(functools.partial(attend_body, rows), out_shape=(shaped(q_...  12.5 us
    pallas_call x1, Pallas kernels, unpack(): pl.pallas_call(unpack_body, out_shape=(shaped(output.shape, output.dtype)...  6.85 us

profile of v7, /device:TPU:0, one launch (start us, length us, event | category | flops | bytes accessed | tf_op | source)
XLA Modules:
  0.0 218.6 jit_solution(2159951552383822196)
XLA Ops:
  0.7 43.3 %first_layers.1 = (bf16[512,6400]{1,0:T(8,128)(2,1)}, bf16[512,4608]{1,0:T(8,128)(2,1)}, f32[2,32,1024]{2,1,0:T(8,128)}, s32[16,1,256]{2,1,0:T(1,128)}, s32[8,12...) custom-call(bf16[256,512]{1,0:T(8,128)(2,1)} %bitcast.38, ...), custom_call_target="tpu_custom_call" | custom-call | tf_op jit(solution)/shard_map/first_layers/pallas_call | solution.py:651
  44.0 12.5 %attend.1 = (f32[64,2048]{1,0:T(8,128)}, bf16[64,2048]{1,0:T(8,128)(2,1)}, f32[1,2048]{1,0:T(1,128)}) custom-call(s32[8,128]{1,0:T(8,128)} %get-tuple-element.85.plan_ref, bf16[64,2048]{1,0:T(8,128)(2,1)} %get-tuple-element.86.q_ref.refs_0_, bf16[4096,256]{1,0:T(8,128)(2,1)} %get-tuple-element.87.kv_ref.refs_4_, s32[16,1,256]{2,1,0:T(1,128)} %get-tuple-element.88.seg_ref.refs_8_), custom_call_target="tpu_custom_call" | custom-call | tf_op jit(solution)/shard_map/attend/pallas_call | solution.py:717
  56.5 22.5 %middle_layers.1 = (bf16[256,512]{1,0:T(8,128)(2,1)}, f32[2,32,1024]{2,1,0:T(8,128)}, f32[256,512]{1,0:T(8,128)}, bf16[512,4608]{1,0:T(8,128)(2,1)}, bf16[64,2048]{1,0:T(8,128)(2,1)}) custom-call(bf16[64,2048]{1,0:T(8,128)(2,1)} %get-tuple-element.89.o_in, bf16[256,512]{1,0:T(8,128)(2,1)} %bitcast.39, f32[2,32,1024]{2,1,0:T(8,128)} %get-tuple-element.90.small_in.refs_6_, ...), custom_call_target="tpu_custom_call" | custom-call | tf_op jit(solution)/shard_map/middle_layers/pallas_call | solution.py:858
  79.0 132.6 %last_layers.1 = (bf16[256,11264]{1,0:T(8,128)(2,1)}, f32[256,512]{1,0:T(8,128)}) custom-call(bf16[64,2048]{1,0:T(8,128)(2,1)} %get-tuple-element.86.q_ref.refs_0_, bf16[64,2048]{1,0:T(8,128)(2,1)} %get-tuple-element.94.refs_1_, f32[64,2048]{1,0:T(8,128)} %get-tuple-element.95.refs_2_, f32[1,2048]{1,0:T(1,128)} %get-tuple-element.96.refs_3_, ...), custom_call_target="tpu_custom_call" | custom-call | tf_op jit(solution)/shard_map/last_layers/pallas_call | solution.py:1570
  211.6 6.8 %unpack.1 = (bf16[256,512]{1,0:T(8,128)(2,1)}, f32[256,512]{1,0:T(8,128)}, f32[256,1024]{1,0:T(8,128)}, f32[256,2048]{1,0:T(8,128)}, f32[3,256,256]{2,1,0:T(8,12...) custom-call(bf16[256,512]{1,0:T(8,128)(2,1)} %get-tuple-element.93.o, ...), custom_call_target="tpu_custom_call" | custom-call | tf_op jit(solution)/shard_map/unpack/pallas_call | solution.py:1635

commit v8 on v7

--- a/solution.py
+++ b/solution.py
@@ -1582,7 +1582,8 @@
     size = len(MATRICES) + len(VECTORS) + 2
     outs, (packed, output, grad, *stages, load_sem, out_sem) = refs[:size], refs[size:]
     output_ref, grad_ref, *outs = outs
-    order = [len(MATRICES)] + list(range(len(MATRICES)))
+    turns = (0, 1, 6, 7, 4, 2, 3, 5)
+    order = list(turns) + [len(MATRICES)]
     bounds = [(first, width * blocks) for first, width, blocks in MATRICES] + [(SMALL, BLOCK)]
     loads = {}
     for at in order:
@@ -1593,7 +1594,8 @@
         move(grad_in, grad, load_sem.at[len(MATRICES) + 2]),
     ]
     stores = []
-    for at, (first, width, blocks) in enumerate(MATRICES):
+    for at in turns:
+        first, width, blocks = MATRICES[at]
         loads[at].wait()
         stage = stages[at]
         tall = 2 * ROW_BLOCK

time: 220 us -> 225 us (1.023)
  Pallas kernels: 218 us -> 223 us
    pallas_call x1, Pallas kernels: 12.5 us -> 15.4 us  [attend(): pl.pallas_call(functools.partial(attend_body, rows), out_shape=(shaped(q_...]
    pallas_call x1, Pallas kernels: 22.5 us -> 24.9 us  [middle_kernel(): pl.pallas_call(functools.partial(middle_body, count, heads), out_shape=(s...]
where the time goes in v8:
time: 225 us; the launch traced here: 224 us
  Pallas kernels  223 us (99%)
    pallas_call x1, Pallas kernels, last_kernel(): pl.pallas_call(functools.partial(last_body, count, heads), out_shape=(sha...  133 us
    pallas_call x1, Pallas kernels, first_kernel(): pl.pallas_call(functools.partial(first_body, count, heads), out_shape=out...  43.3 us
    pallas_call x1, Pallas kernels, middle_kernel(): pl.pallas_call(functools.partial(middle_body, count, heads), out_shape=(s...  24.9 us
    pallas_call x1, Pallas kernels, attend(): pl.pallas_call(functools.partial(attend_body, rows), out_shape=(shaped(q_...  15.4 us
    pallas_call x1, Pallas kernels, unpack(): pl.pallas_call(unpack_body, out_shape=(shaped(output.shape, output.dtype)...  6.85 us

profile of v8, /device:TPU:0, one launch (start us, length us, event | category | flops | bytes accessed | tf_op | source)
XLA Modules:
  0.0 224.2 jit_solution(7175586731309466662)
XLA Ops:
  0.7 43.3 %first_layers.1 = (bf16[512,6400]{1,0:T(8,128)(2,1)}, bf16[512,4608]{1,0:T(8,128)(2,1)}, f32[2,32,1024]{2,1,0:T(8,128)}, s32[16,1,256]{2,1,0:T(1,128)}, s32[8,12...) custom-call(bf16[256,512]{1,0:T(8,128)(2,1)} %bitcast.38, ...), custom_call_target="tpu_custom_call" | custom-call | tf_op jit(solution)/shard_map/first_layers/pallas_call | solution.py:651
  44.0 15.4 %attend.1 = (f32[64,2048]{1,0:T(8,128)}, bf16[64,2048]{1,0:T(8,128)(2,1)}, f32[1,2048]{1,0:T(1,128)}) custom-call(s32[8,128]{1,0:T(8,128)} %get-tuple-element.85.plan_ref, bf16[64,2048]{1,0:T(8,128)(2,1)} %get-tuple-element.86.q_ref.refs_0_, bf16[4096,256]{1,0:T(8,128)(2,1)} %get-tuple-element.87.kv_ref.refs_4_, s32[16,1,256]{2,1,0:T(1,128)} %get-tuple-element.88.seg_ref.refs_8_), custom_call_target="tpu_custom_call" | custom-call | tf_op jit(solution)/shard_map/attend/pallas_call | solution.py:717
  59.3 24.9 %middle_layers.1 = (bf16[256,512]{1,0:T(8,128)(2,1)}, f32[2,32,1024]{2,1,0:T(8,128)}, f32[256,512]{1,0:T(8,128)}, bf16[512,4608]{1,0:T(8,128)(2,1)}, bf16[64,2048]{1,0:T(8,128)(2,1)}) custom-call(bf16[64,2048]{1,0:T(8,128)(2,1)} %get-tuple-element.89.o_in, bf16[256,512]{1,0:T(8,128)(2,1)} %bitcast.39, f32[2,32,1024]{2,1,0:T(8,128)} %get-tuple-element.90.small_in.refs_6_, ...), custom_call_target="tpu_custom_call" | custom-call | tf_op jit(solution)/shard_map/middle_layers/pallas_call | solution.py:858
  84.2 132.9 %last_layers.1 = (bf16[256,11264]{1,0:T(8,128)(2,1)}, f32[256,512]{1,0:T(8,128)}) custom-call(bf16[64,2048]{1,0:T(8,128)(2,1)} %get-tuple-element.86.q_ref.refs_0_, bf16[64,2048]{1,0:T(8,128)(2,1)} %get-tuple-element.94.refs_1_, f32[64,2048]{1,0:T(8,128)} %get-tuple-element.95.refs_2_, f32[1,2048]{1,0:T(1,128)} %get-tuple-element.96.refs_3_, ...), custom_call_target="tpu_custom_call" | custom-call | tf_op jit(solution)/shard_map/last_layers/pallas_call | solution.py:1570
  217.1 6.8 %unpack.1 = (bf16[256,512]{1,0:T(8,128)(2,1)}, f32[256,512]{1,0:T(8,128)}, f32[256,1024]{1,0:T(8,128)}, f32[256,2048]{1,0:T(8,128)}, f32[3,256,256]{2,1,0:T(8,12...) custom-call(bf16[256,512]{1,0:T(8,128)(2,1)} %get-tuple-element.93.o, ...), custom_call_target="tpu_custom_call" | custom-call | tf_op jit(solution)/shard_map/unpack/pallas_call | solution.py:1637
